TPU v7x, 256 devices: a whole 4x4x8 slice. The times are simulated.
256 devices in a mesh: ctx: 128 (over y, z, x), head: 2 (over core).
Axes of the slice: x: 4, y: 4, z: 8, core: 2. Of those that a mesh axis runs over, the one named last changes fastest.
Arguments:
- queries: bfloat16 [32768, 1024], P('ctx', 'head'), may hold values from -2.5 to 2.5
- keys: bfloat16 [32768, 1024], P('ctx', 'head'), may hold values from -2.5 to 2.5
- values: bfloat16 [32768, 1024], P('ctx', 'head'), may hold values from -6 to 6
- log_decay: float32 [8, 32768], P('head', 'ctx'), may hold values from -0.75 to 0, as said below
- out_weight: bfloat16 [1024, 2048], P('head'), may hold values from -0.1875 to 0.1875
- out_grad: bfloat16 [32768, 2048], P('ctx', 'head'), may hold values from -6 to 6
Outputs:
- mixed: bfloat16 [32768, 2048], P('ctx', 'head')
- grad_queries: bfloat16 [32768, 1024], P('ctx', 'head')
- grad_keys: bfloat16 [32768, 1024], P('ctx', 'head')
- grad_values: bfloat16 [32768, 1024], P('ctx', 'head')
Inputs may be any that keep to these rules, and one draw needn't show every extreme that they name: log_decay is negative everywhere.
All inputs are finite; a program needn't handle non-finite values.
Results may differ from a plain program's by a relative error of at most 0.018.
Values may be sent and summed in bfloat16 or wider, within the bound.
No kernel may reach another device: no remote copies, remote signals or barrier semaphores. Data moves between devices by JAX's collectives and lax.ppermute only.
A program may use at most 128 MiB of HBM per device.

v0:
```python
import jax
import jax.numpy as jnp
from jax import lax
from jax.sharding import PartitionSpec as P

SPAN = 256


epsilon = 1e-05


def prefix(shard, axis, join, neutral, backward):
    count = lax.axis_size(axis)
    place = lax.axis_index(axis)
    ahead = count - 1 - place if backward else place
    gathered = jax.tree.map(
        lambda a, kind: lax.all_gather(a.astype(kind), axis),
        shard,
        jax.tree.map(lambda a: jnp.bfloat16 if a.dtype == jnp.float32 else a.dtype, shard),
    )
    state = jax.tree.map(lambda a, e: jnp.zeros_like(a) + jnp.asarray(e, a.dtype), shard, neutral)

    def one(lap, state):
        source = count - 1 - lap if backward else lap
        return join(
            state,
            jax.tree.map(
                lambda a, own: lax.dynamic_index_in_dim(a, source, 0, False).astype(own.dtype),
                gathered,
                shard,
            ),
        )

    return lax.fori_loop(0, ahead, one, state)


def combine(earlier, later):
    return (earlier[0] + later[0], jnp.exp(later[0])[:, None, None] * earlier[1] + later[1])


def carry_prefix(local_part, reverse):
    identity = (jnp.zeros_like(local_part[0]), jnp.zeros_like(local_part[1]))
    if reverse:
        return prefix(local_part, "ctx", combine, identity, True)
    return prefix(local_part, "ctx", combine, identity, False)


def local(queries, keys, values, log_decay, out_weight, out_grad):
    tok_rows, key_cols = queries.shape
    head_count = log_decay.shape[0]
    key_dim = key_cols // head_count
    val_dim = values.shape[1] // head_count
    blocks = tok_rows // SPAN
    query_blocks = queries.reshape(blocks, SPAN, head_count, key_dim)
    key_blocks = keys.reshape(blocks, SPAN, head_count, key_dim)
    value_blocks = values.reshape(blocks, SPAN, head_count, val_dim)
    cumulative = jnp.cumsum(log_decay.reshape(head_count, blocks, SPAN), axis=2)
    block_end = cumulative[:, :, -1]
    span_decay = block_end.T
    token_positions = jnp.arange(SPAN)
    causal = token_positions[:, None] >= token_positions[None, :]
    decay_mask = jnp.where(
        causal, jnp.exp(jnp.minimum(cumulative[..., :, None] - cumulative[..., None, :], 0.0)), 0.0
    )
    scores = jnp.einsum(
        "nihd,njhd->hnij", query_blocks, key_blocks, preferred_element_type=jnp.float32
    )
    attn_probs = (scores * decay_mask).astype(jnp.bfloat16)
    inside_term = jnp.einsum(
        "hnij,njhe->nihe", attn_probs, value_blocks, preferred_element_type=jnp.float32
    )
    weight_key = jnp.transpose(jnp.exp(block_end[:, :, None] - cumulative), (1, 2, 0))
    growth = jnp.exp(jnp.transpose(cumulative, (1, 2, 0)))
    key_weighted = (key_blocks * weight_key[..., None]).astype(jnp.bfloat16)
    block_delta = jnp.einsum(
        "nihd,nihe->nhde", key_weighted, value_blocks, preferred_element_type=jnp.float32
    )
    local_state = jnp.zeros((head_count, key_dim, val_dim), jnp.float32)
    block_no = 0
    local_state = jnp.exp(span_decay[block_no])[:, None, None] * local_state + block_delta[block_no]
    device_decay = span_decay[block_no]
    start_decay, start_state = carry_prefix((device_decay, local_state), False)
    current = start_state
    block_no = 0
    states = [current]
    state_bf = jnp.stack(states).astype(jnp.bfloat16)
    carried_term = growth[..., None] * jnp.einsum(
        "nihd,nhde->nihe", query_blocks, state_bf, preferred_element_type=jnp.float32
    )
    attended = (inside_term + carried_term).reshape(tok_rows, head_count, val_dim)
    inv_rms = lax.rsqrt(jnp.mean(attended * attended, axis=2) + epsilon)
    normed = (
        (attended * inv_rms[..., None]).astype(jnp.bfloat16).reshape(tok_rows, head_count * val_dim)
    )
    partial_value = jnp.dot(normed, out_weight, preferred_element_type=jnp.float32)
    mixed = lax.psum_scatter(
        partial_value.astype(jnp.bfloat16), "head", scatter_dimension=1, tiled=True
    )
    grad_norm = lax.dot_general(
        lax.all_gather(out_grad, "head", axis=1, tiled=True),
        out_weight,
        (((1,), (1,)), ((), ())),
        preferred_element_type=jnp.float32,
    )
    grad_norm = grad_norm.reshape(tok_rows, head_count, val_dim)
    grad_att = (
        inv_rms[..., None] * grad_norm
        - attended * (inv_rms**3 * jnp.mean(grad_norm * attended, axis=2))[..., None]
    )
    grad_bf = grad_att.astype(jnp.bfloat16).reshape(blocks, SPAN, head_count, val_dim)
    d_probs = jnp.einsum(
        "nihe,njhe->hnij", grad_bf, value_blocks, preferred_element_type=jnp.float32
    )
    d_scores = (d_probs * decay_mask).astype(jnp.bfloat16)
    grad_query = jnp.einsum(
        "hnij,njhd->nihd", d_scores, key_blocks, preferred_element_type=jnp.float32
    )
    grad_query = grad_query + growth[..., None] * jnp.einsum(
        "nihe,nhde->nihd", grad_bf, state_bf, preferred_element_type=jnp.float32
    )
    grad_key = jnp.einsum(
        "hnij,nihd->njhd", d_scores, query_blocks, preferred_element_type=jnp.float32
    )
    grad_value = jnp.einsum(
        "hnij,nihe->njhe", attn_probs, grad_bf, preferred_element_type=jnp.float32
    )
    query_weighted = (query_blocks * growth[..., None]).astype(jnp.bfloat16)
    back_delta = jnp.einsum(
        "nihd,nihe->nhde", query_weighted, grad_bf, preferred_element_type=jnp.float32
    )
    local_grad = jnp.zeros((head_count, key_dim, val_dim), jnp.float32)
    for block_no in reversed(range(blocks)):
        local_grad = (
            jnp.exp(span_decay[block_no])[:, None, None] * local_grad + back_delta[block_no]
        )
    end_decay, end_grad = carry_prefix((device_decay, local_grad), True)
    leaving = [None] * blocks
    current = end_grad
    for block_no in reversed(range(blocks)):
        leaving[block_no] = current
        current = jnp.exp(span_decay[block_no])[:, None, None] * current + back_delta[block_no]
    leaving_bf = jnp.stack(leaving).astype(jnp.bfloat16)
    grad_key = grad_key + weight_key[..., None] * jnp.einsum(
        "nihe,nhde->nihd", value_blocks, leaving_bf, preferred_element_type=jnp.float32
    )
    grad_value = grad_value + weight_key[..., None] * jnp.einsum(
        "nihd,nhde->nihe", key_blocks, leaving_bf, preferred_element_type=jnp.float32
    )
    grad_queries = grad_query.astype(jnp.bfloat16).reshape(tok_rows, key_cols)
    grad_keys = grad_key.astype(jnp.bfloat16).reshape(tok_rows, key_cols)
    grad_values = grad_value.astype(jnp.bfloat16).reshape(tok_rows, head_count * val_dim)
    return (mixed, grad_queries, grad_keys, grad_values)


def solution(mesh):
    placed = (
        P("ctx", "head"),
        P("ctx", "head"),
        P("ctx", "head"),
        P("head", "ctx"),
        P("head", None),
        P("ctx", "head"),
    )
    return jax.shard_map(
        local,
        mesh=mesh,
        in_specs=placed,
        out_specs=(P("ctx", "head"), P("ctx", "head"), P("ctx", "head"), P("ctx", "head")),
        check_vma=False,
    )
```

profile of v0, /device:TPU:2, one launch (start us, length us, event | category | flops | bytes accessed | tf_op | source)
XLA Modules:
  0.0 798.1 jit_solution(7391648483359610288)
XLA Ops:
  8.7 1.2 reduce-window.6
  10.5 1.1 copy.137
  12.8 1.3 dynamic-slice
  14.9 347.8 %all-reduce = bf16[512]{0:T(512)(128)(2,1)S(1)} all-reduce(bf16[512]{0:T(512)(128)(2,1)S(1)} %dynamic-update-slice), channel_id=2, replica_groups=mesh['ctx'=128,'head'=2] {'ctx'}, use_global_device_ids=true, to_apply=%add | all-reduce | flops 512 | bytes 2048
  363.5 1.1 convolution_bitcast_fusion.7
  364.7 2.8 fusion.38
  367.4 1.1 while.26
  368.5 1.6 fusion.17
  371.3 1.4 fusion.1
  374.5 1.7 convolution_convert_fusion
  376.2 1.0 convolution_bitcast_fusion.2
  378.1 2.1 convolution_bitcast_fusion
  380.2 271.6 %all-gather.11.cloned.1.call-done = bf16[512,128,128]{2,1,0:T(8,128)(2,1)} async-done(((bf16[4,128,128]{2,1,0:T(8,128)(2,1)}), bf16[512,128,128]{2,1,0:T(8,128)(2,1)}) %all-gather.11.cloned.1.call-update) | async-done | bytes 16777232 | tf_op jit(solution)/shard_map/all_gather | solution.py:17
  651.9 133.9 %while.27 = (s32[]{:T(128)}, f32[4,128,128]{2,1,0:T(8,128)S(1)}, s32[]{:T(128)}, bf16[128,4]{1,0:T(8,128)(2,1)S(1)}, bf16[128,4,128,128]{3,2,1,0:T(8,128)(2,1)},...) while((s32[]{:T(128)}, f32[4,128,128]{2,1,0:T(8,128)S(1)}, s32[]{:T(128)}, bf16[128,4]{1,0:T(8,128)(2,1)S(1)}, ...), condition=%wide.region_8.9_spmd, body=%wide.region_7.8_spmd.sunk | while | flops 196618 | bytes 655555 | solution.py:34
  651.9 1.1 convert_add_fusion.5
  653.0 1.0 convert_add_fusion.5
  655.2 1.0 convert_add_fusion.5
  662.6 1.0 convert_add_fusion.5
  663.7 1.0 convert_add_fusion.5
  664.7 1.0 convert_add_fusion.5
  665.8 1.0 convert_add_fusion.5
  785.8 1.9 fusion.10
  787.7 1.8 copy.99
  789.5 1.2 fusion.11
  (320 shorter events, 132.7 us)
Async XLA Ops:
  7.2 357.5 %copy-start = (bf16[512,2048]{1,0:T(8,128)(2,1)S(1)}, bf16[512,2048]{1,0:T(8,128)(2,1)}, u32[]{:S(2)}) copy-start(bf16[512,2048]{1,0:T(8,128)(2,1)} %param.14) | copy-start | bytes 6291460
  7.2 355.9 %copy-start.8 = (bf16[256,512]{1,0:T(8,128)(2,1)S(1)}, bf16[256,512]{1,0:T(8,128)(2,1)}, u32[]{:S(2)}) copy-start(bf16[256,512]{1,0:T(8,128)(2,1)} %param.11) | copy-start | bytes 786436
  7.2 4.4 copy-start.7
  7.2 355.7 %copy-start.12 = (bf16[256,512]{1,0:T(8,128)(2,1)S(1)}, bf16[256,512]{1,0:T(8,128)(2,1)}, u32[]{:S(2)}) copy-start(bf16[256,512]{1,0:T(8,128)(2,1)} %param.10) | copy-start | bytes 786436
  7.2 357.4 %all-gather.7.cloned.1.call-start = ((), (), s32[]{:S(2)}) async-start(), calls=%async_computation.2 | async-start | bytes 1572864 | tf_op jit(solution)/shard_map/all_gather | solution.py:100
  7.9 359.5 %all-gather.9.cloned.1.call-start = ((), (), s32[]{:S(2)}) async-start(), calls=%async_computation.3 | async-start | bytes 16908288 | tf_op jit(solution)/shard_map/all_gather | solution.py:17
  10.4 2.3 copy-start.13
  11.6 351.1 %copy-start.9 = (bf16[256,512]{0,1:T(8,128)(2,1)}, bf16[256,512]{0,1:T(8,128)(2,1)S(1)}, u32[]{:S(2)}) copy-start(bf16[256,512]{0,1:T(8,128)(2,1)S(1)} %copy.137) | copy-start | bytes 786436
  12.5 639.3 %all-gather.11.cloned.1.call-start = ((), (), s32[]{:S(2)}) async-start(), calls=%async_computation.4 | async-start | bytes 16908288 | tf_op jit(solution)/shard_map/all_gather | solution.py:17
  363.5 3.9 copy-start.1
  368.5 1.6 copy-start.6
  368.5 1.7 copy-start.14
  371.2 420.4 %reduce-scatter.2.cloned.1.call-start = ((), (), s32[]{:S(2)}) async-start(), calls=%async_computation.1 | async-start | bytes 1572864 | tf_op jit(solution)/shard_map/reduce_scatter | solution.py:96
  371.2 1.5 copy-start.10
  372.7 0.8 copy-start.5
  374.5 1.7 copy-start.2
  374.5 2.8 copy-start.11
  380.2 405.6 %copy-start.3 = (f32[1,256,4,128]{1,3,2,0:T(8,128)S(1)}, f32[1,256,4,128]{1,3,2,0:T(8,128)}, u32[]{:S(2)}) copy-start(f32[1,256,4,128]{1,3,2,0:T(8,128)} %convolution_bitcast_fusion.2) | copy-start | bytes 1572868
  651.9 137.7 %copy-start.4 = (f32[1,256,4,128]{1,3,2,0:T(8,128)S(1)}, f32[1,256,4,128]{1,3,2,0:T(8,128)}, u32[]{:S(2)}) copy-start(f32[1,256,4,128]{1,3,2,0:T(8,128)} %convolution_bitcast_fusion) | copy-start | bytes 1572868
Sparse Core Ops, SparseCore 0:
  9.8 17.3 all-gather.6
  31.4 151.6 all-gather.8
  371.3 280.5 all-gather.10
  654.8 11.2 reduce-scatter.1
where the time goes:
time: 803 us; the launch traced here: 798 us
  blocking collectives  348 us (43%)
  waiting for transfers between devices  272 us (34%)
  other arithmetic  133 us (17%)
  matrix products  18.3 us (2%)
  between operations  14.8 us (2%)
  local copies, waits for them, and re-layouts  8.26 us (1%)
    unnamed x1, blocking collectives  348 us
    all_gather x2, waiting for transfers between devices, prefix(): lax.all_gather(a.astype(kind), axis)  272 us
    add x127, other arithmetic, combine(): jnp.exp(later[0])[:, None, None] * earlier[1] + later[1]  130 us
  transfers between devices with their start and end apart: 4, of which 1 were waited for; matrix products, arithmetic and copies ran while one was open for 19% of the time, Pallas kernels for 0%

commit v1 on v0

v1 whole, which is shorter than its diff:
```python
import functools

import jax
import jax.numpy as jnp
from jax import lax
from jax.experimental import pallas as pl
from jax.experimental.pallas import tpu as pltpu
from jax.sharding import PartitionSpec as P

EPS = 1e-05
F32 = jnp.float32
BF = jnp.bfloat16
W = 128


def dot(a, b, da=1, db=0, precision=None):
    return lax.dot_general(
        a, b, (((da,), (db,)), ((), ())), preferred_element_type=F32, precision=precision
    )


def call(body, outs, *args, flops=0, smem=0):
    spec = [pl.BlockSpec(memory_space=pltpu.SMEM)] * smem
    spec += [pl.BlockSpec(memory_space=pltpu.VMEM)] * (len(args) - smem)
    moved = sum(a.size * a.dtype.itemsize for a in (*args, *outs))
    return pl.pallas_call(
        body,
        out_shape=outs,
        in_specs=spec,
        out_specs=[pl.BlockSpec(memory_space=pltpu.VMEM)] * len(outs),
        cost_estimate=pl.CostEstimate(flops=flops, bytes_accessed=moved, transcendentals=0),
        name=body.__name__ if hasattr(body, "__name__") else body.func.__name__,
    )(*args)


def shape(*dims, dtype=BF):
    return jax.ShapeDtypeStruct(dims, dtype)


def head_cols(h):
    return slice(h * W, (h + 1) * W)


def spread(ref, h, matrix, per):
    for r in range(matrix.shape[0] // per):
        ref[h * per : (h + 1) * per, r * W : (r + 1) * W] = matrix[r * per : (r + 1) * per].astype(ref.dtype)


def collect(ref, h, per):
    return jnp.concatenate(
        [ref[h * per : (h + 1) * per, r * W : (r + 1) * W] for r in range(W // per)], axis=0
    )


def block_delta(k_ref, v_ref, ld_ref, pay_ref, col_ref, row_ref):
    heads, span = ld_ref.shape
    per = pay_ref.shape[0] // heads
    ld = ld_ref[...]
    a = lax.broadcasted_iota(jnp.int32, (span, span), 0)
    b = lax.broadcasted_iota(jnp.int32, (span, span), 1)
    row = dot(ld, (a <= b).astype(F32), precision=lax.Precision.HIGHEST)
    col = dot((b <= a).astype(F32), ld, 1, 1, precision=lax.Precision.HIGHEST)
    row_ref[...] = row
    last = col[span - 1 : span, :]
    col_ref[0] = jnp.exp(col)
    weight = jnp.exp(last - col)
    col_ref[1] = weight
    col_ref[2] = col
    lane = lax.broadcasted_iota(jnp.int32, (per, W), 1)
    for h in range(heads):
        kw = (k_ref[:, head_cols(h)].astype(F32) * weight[:, h : h + 1]).astype(BF)
        spread(pay_ref, h, dot(kw, v_ref[:, head_cols(h)], 0, 0), per)
        end = jnp.broadcast_to(last[:, h : h + 1], (per, W))
        hi = end.astype(BF).astype(F32)
        mid = (end - hi).astype(BF).astype(F32)
        low = end - hi - mid
        tail = jnp.where(lane == 0, hi, jnp.where(lane == 1, mid, jnp.where(lane == 2, low, 0.0)))
        pay_ref[h * per : (h + 1) * per, W * W // per :] = tail.astype(BF)


def inside(q_ref, k_ref, v_ref, col_ref, row_ref, probs_ref, mask_ref, in_ref):
    heads, span = row_ref.shape
    a = lax.broadcasted_iota(jnp.int32, (span, span), 0)
    b = lax.broadcasted_iota(jnp.int32, (span, span), 1)
    for h in range(heads):
        gap = col_ref[2][:, h : h + 1] - row_ref[h : h + 1, :]
        mask = jnp.where(b <= a, jnp.exp(jnp.minimum(gap, 0.0)), 0.0)
        mask_ref[h] = mask
        probs = (dot(q_ref[:, head_cols(h)], k_ref[:, head_cols(h)], 1, 1) * mask).astype(BF)
        probs_ref[h] = probs
        in_ref[:, head_cols(h)] = dot(probs, v_ref[:, head_cols(h)])


def grad_of_norm(core_ref, own_ref, other_ref, w_ref, out_ref):
    width = own_ref.shape[1]
    mine = pl.multiple_of(core_ref[0] * width, width)
    theirs = pl.multiple_of((1 - core_ref[0]) * width, width)
    out_ref[...] = dot(own_ref[...], w_ref[:, pl.ds(mine, width)], 1, 1) + dot(
        other_ref[...], w_ref[:, pl.ds(theirs, width)], 1, 1
    )


def forward_scan(x_ref, y_ref, mh_ref, ml_ref):
    count, width = y_ref.shape
    i = lax.broadcasted_iota(jnp.int32, (count, count), 0)
    j = lax.broadcasted_iota(jnp.int32, (count, count), 1)
    before = (j < i).astype(BF)
    gap = jnp.zeros((count, count), F32)
    for piece in range(3):
        end = x_ref[:, width + piece : width + piece + 1].astype(F32)
        gap = gap + dot(before, jnp.where(j < i, end, 0.0).astype(BF))
    reach = jnp.where(j < i, jnp.exp(jnp.minimum(gap, 0.0)), 0.0)
    high = reach.astype(BF)
    low = (reach - high.astype(F32)).astype(BF)
    mh_ref[...] = high
    ml_ref[...] = low
    x = x_ref[:, :width]
    y_ref[...] = (dot(high, x) + dot(low, x)).astype(BF)


def backward_scan(x_ref, mh_ref, ml_ref, y_ref):
    x = x_ref[...]
    y_ref[...] = (dot(mh_ref[...], x, 0, 0) + dot(ml_ref[...], x, 0, 0)).astype(BF)


def norm_and_grad(q_ref, s_ref, col_ref, in_ref, gn_ref, normed_ref, g_ref, pay_ref):
    heads = in_ref.shape[1] // W
    per = s_ref.shape[0] // heads
    for h in range(heads):
        cols = head_cols(h)
        growth = col_ref[0][:, h : h + 1]
        q = q_ref[:, cols]
        att = in_ref[:, cols] + growth * dot(q, collect(s_ref, h, per))
        inv = lax.rsqrt(jnp.mean(att * att, axis=1, keepdims=True) + EPS)
        normed_ref[:, cols] = (att * inv).astype(BF)
        gn = gn_ref[:, cols]
        g = inv * gn - att * (inv * inv * inv * jnp.mean(gn * att, axis=1, keepdims=True))
        g = g.astype(BF)
        g_ref[:, cols] = g
        spread(pay_ref, h, dot((q.astype(F32) * growth).astype(BF), g, 0, 0), per)


def mix(core_ref, normed_ref, w_ref, own_ref, other_ref):
    width = own_ref.shape[1]
    mine = pl.multiple_of(core_ref[0] * width, width)
    theirs = pl.multiple_of((1 - core_ref[0]) * width, width)
    other_ref[...] = dot(normed_ref[...], w_ref[:, pl.ds(theirs, width)]).astype(BF)
    own_ref[...] = dot(normed_ref[...], w_ref[:, pl.ds(mine, width)])


def score_grads(q_ref, k_ref, v_ref, g_ref, s_ref, col_ref, probs_ref, mask_ref, gq_ref, gk_ref, gv_ref):
    heads = probs_ref.shape[0]
    per = s_ref.shape[0] // heads
    for h in range(heads):
        cols = head_cols(h)
        g = g_ref[:, cols]
        d = (dot(g, v_ref[:, cols], 1, 1) * mask_ref[h]).astype(BF)
        carried = dot(g, collect(s_ref, h, per), 1, 1)
        gq_ref[:, cols] = (dot(d, k_ref[:, cols]) + col_ref[0][:, h : h + 1] * carried).astype(BF)
        gk_ref[:, cols] = dot(d, q_ref[:, cols], 0, 0)
        gv_ref[:, cols] = dot(probs_ref[h], g, 0, 0)


def finish(k_ref, v_ref, e_ref, col_ref, gkp_ref, gvp_ref, gk_ref, gv_ref):
    heads = gk_ref.shape[1] // W
    per = e_ref.shape[0] // heads
    for h in range(heads):
        cols = head_cols(h)
        weight = col_ref[1][:, h : h + 1]
        e = collect(e_ref, h, per)
        gk_ref[:, cols] = (gkp_ref[:, cols] + weight * dot(v_ref[:, cols], e, 1, 1)).astype(BF)
        gv_ref[:, cols] = (gvp_ref[:, cols] + weight * dot(k_ref[:, cols], e)).astype(BF)


def local(queries, keys, values, log_decay, out_weight, out_grad):
    rows, width = queries.shape
    heads, span = log_decay.shape
    count = lax.axis_size("ctx")
    slots = heads * W * W // count
    model = out_weight.shape[1]
    core = lax.axis_index("head").astype(jnp.int32).reshape(1)
    swap = [(0, 1), (1, 0)]

    other_grad = lax.ppermute(out_grad, "head", swap)
    pay, col, row = call(
        block_delta,
        [shape(count, slots + W), shape(3, rows, heads, dtype=F32), shape(heads, span, dtype=F32)],
        keys, values, log_decay, flops=rows * width * W * 2,
    )
    got = lax.all_to_all(pay, "ctx", 0, 0, tiled=True)
    probs, mask, within = call(
        inside,
        [shape(heads, span, span), shape(heads, span, span, dtype=F32), shape(rows, width, dtype=F32)],
        queries, keys, values, col, row, flops=rows * width * span * 4,
    )
    (grad_norm,) = call(
        grad_of_norm, [shape(rows, width, dtype=F32)], core, out_grad, other_grad, out_weight,
        flops=2 * rows * width * model, smem=1,
    )
    sent, high, low = call(
        forward_scan, [shape(count, slots), shape(count, count), shape(count, count)], got,
        flops=4 * count * count * slots,
    )
    state = lax.all_to_all(sent, "ctx", 0, 0, tiled=True)
    normed, grad_att, pay = call(
        norm_and_grad,
        [shape(rows, width), shape(rows, width), shape(count, slots)],
        queries, state, col, within, grad_norm, flops=rows * width * W * 4,
    )
    got = lax.all_to_all(pay, "ctx", 0, 0, tiled=True)
    own, other = call(
        mix, [shape(rows, model // 2, dtype=F32), shape(rows, model // 2)], core, normed, out_weight,
        flops=2 * rows * width * model, smem=1,
    )
    theirs = lax.ppermute(other, "head", swap)
    grad_q, gk_part, gv_part = call(
        score_grads,
        [shape(rows, width), shape(rows, width, dtype=F32), shape(rows, width, dtype=F32)],
        queries, keys, values, grad_att, state, col, probs, mask, flops=rows * width * span * 9,
    )
    (sent,) = call(backward_scan, [shape(count, slots)], got, high, low, flops=4 * count * count * slots)
    leaving = lax.all_to_all(sent, "ctx", 0, 0, tiled=True)
    mixed = (own + theirs.astype(F32)).astype(BF)
    grad_k, grad_v = call(
        finish, [shape(rows, width), shape(rows, width)], keys, values, leaving, col, gk_part, gv_part,
        flops=rows * width * W * 4,
    )
    return mixed, grad_q, grad_k, grad_v


def solution(mesh):
    split = P("ctx", "head")
    return jax.shard_map(
        local,
        mesh=mesh,
        in_specs=(split, split, split, P("head", "ctx"), P("head", None), split),
        out_specs=(split,) * 4,
        check_vma=False,
    )
```

time: 803 us -> 114 us (0.14)
  blocking collectives: 348 us -> 0 us
  waiting for transfers between devices: 272 us -> 31.9 us
  other arithmetic: 133 us -> 7.23 us
  starting transfers between devices: 0.16 us -> 39 us
  Pallas kernels: 0 us -> 26.4 us
  matrix products: 18.3 us -> 0 us
  between operations: 14.8 us -> 0.72 us
    unnamed x1 -> x0, blocking collectives: 348 us -> none
    all_gather x3 -> x0, waiting for transfers between devices: 272 us -> none  [the longest x2 272 us: prefix(): lax.all_gather(a.astype(kind), axis)]
    add x127 -> x0, other arithmetic: 130 us -> none  [combine(): jnp.exp(later[0])[:, None, None] * earlier[1] + later[1]]
    all_to_all x0 -> x4, starting transfers between devices: none -> 38.9 us  [the longest x2 25.1 us: local(): got = lax.all_to_all(pay, 'ctx', 0, 0, tiled=True)]
    all_to_all x0 -> x4, waiting for transfers between devices: none -> 31.9 us  [the longest x2 20.4 us: local(): got = lax.all_to_all(pay, 'ctx', 0, 0, tiled=True)]
    pallas_call x0 -> x9, Pallas kernels: none -> 26.4 us  [call(): pl.pallas_call(body, out_shape=outs, in_specs=spec, out_specs=[pl.BlockSp...]
    dot_general x14 -> x0, matrix products: 18.3 us -> none  [the longest x1 2.76 us: local(): lax.dot_general(lax.all_gather(out_grad, 'head', axis=1, tiled=True), out...]
  transfers between devices with their start and end apart: 4 -> 6, of which waited for: 1 -> 4; matrix products, arithmetic and copies ran while one was open for 19% -> 6% of each run, Pallas kernels for 0% -> 18%
where the time goes in v1:
time: 114 us; the launch traced here: 113 us
  starting transfers between devices  39 us (34%)
  waiting for transfers between devices  31.9 us (28%)
  Pallas kernels  26.4 us (23%)
  local copies, waits for them, and re-layouts  7.57 us (7%)
  other arithmetic  7.23 us (6%)
    pallas_call x9, Pallas kernels, call(): pl.pallas_call(body, out_shape=outs, in_specs=spec, out_specs=[pl.BlockSp...  26.4 us
    all_to_all x2, starting transfers between devices, local(): got = lax.all_to_all(pay, 'ctx', 0, 0, tiled=True)  25.1 us
    all_to_all x2, waiting for transfers between devices, local(): got = lax.all_to_all(pay, 'ctx', 0, 0, tiled=True)  20.4 us
    all_to_all x1, waiting for transfers between devices, local(): leaving = lax.all_to_all(sent, 'ctx', 0, 0, tiled=True)  7.34 us
    unnamed x16, local copies, waits for them, and re-layouts  7.02 us
    all_to_all x1, starting transfers between devices, local(): state = lax.all_to_all(sent, 'ctx', 0, 0, tiled=True)  6.95 us
    all_to_all x1, starting transfers between devices, local(): leaving = lax.all_to_all(sent, 'ctx', 0, 0, tiled=True)  6.9 us
    all_to_all x1, waiting for transfers between devices, local(): state = lax.all_to_all(sent, 'ctx', 0, 0, tiled=True)  4.19 us
  transfers between devices with their start and end apart: 6, of which 4 were waited for; matrix products, arithmetic and copies ran while one was open for 6% of the time, Pallas kernels for 18%

profile of v1, /device:TPU:2, one launch (start us, length us, event | category | flops | bytes accessed | tf_op | source)
XLA Modules:
  0.0 112.9 jit_solution(118819337812755442)
XLA Ops:
  0.6 2.7 %block_delta.1 = (bf16[128,640]{1,0:T(8,128)(2,1)}, f32[3,256,4]{2,1,0:T(8,128)}, f32[4,256]{1,0:T(4,128)}) custom-call(bf16[256,512]{1,0:T(8,128)(2,1)} %k_ref.7, bf16[256,512]{1,0:T(8,128)(2,1)} %v_ref.7, f32[4,256]{1,0:T(4,128)} %ld_ref.1), custom_call_target="tpu_custom_call" | custom-call | flops 33554432 | bytes 708608 | tf_op jit(solution)/shard_map/block_delta/pallas_call | solution.py:26
  3.9 1.6 %reduce = bf16[128,640]{1,0:T(8,128)(2,1)S(1)} reduce(bf16[128,1,640]{2,0,1:T(8,128)(2,1)} %bitcast.23, bf16[]{:T(256)} %broadcast), dimensions={1}, to_apply=%copy.14.reduce_sub_computation | reduce | bytes 327682 | tf_op jit(solution)/shard_map/all_to_all | solution.py:190
  5.5 0.9 reshape.20
  6.3 15.4 %all-to-all-start = ((bf16[128,2,320]{2,1,0:T(2,128)(2,1)}), bf16[128,2,320]{2,1,0:T(2,128)(2,1)S(1)}, u32[]{:S(2)}, u32[]{:S(2)}) async-start(bf16[128,2,320]{2,1,0:T(2,128)(2,1)} %reshape.20), calls=%async_computation | async-start | bytes 393216 | tf_op jit(solution)/shard_map/all_to_all | solution.py:190
  21.9 12.4 %all-to-all-done = bf16[128,2,320]{2,1,0:T(2,128)(2,1)S(1)} async-done(((bf16[128,2,320]{2,1,0:T(2,128)(2,1)}), bf16[128,2,320]{2,1,0:T(2,128)(2,1)S(1)}, u32[]{:S(2)}, u32[]{:S(2)}) %all-to-all-start) | async-done | bytes 163872 | tf_op jit(solution)/shard_map/all_to_all | solution.py:190
  35.2 2.1 %forward_scan.1 = (bf16[128,512]{1,0:T(8,128)(2,1)}, bf16[128,128]{1,0:T(8,128)(2,1)}, bf16[128,128]{1,0:T(8,128)(2,1)}) custom-call(bf16[128,640]{1,0:T(8,128)(2,1)} %bitcast.19), custom_call_target="tpu_custom_call" | custom-call | flops 33554432 | bytes 360448 | tf_op jit(solution)/shard_map/forward_scan/pallas_call | solution.py:26
  37.3 1.6 %reduce.1 = bf16[128,512]{1,0:T(8,128)(2,1)S(1)} reduce(bf16[128,1,512]{2,0,1:T(8,128)(2,1)} %bitcast.25, bf16[]{:T(256)} %broadcast), dimensions={1}, to_apply=%copy.15.reduce_sub_computation | reduce | bytes 262146 | tf_op jit(solution)/shard_map/all_to_all | solution.py:204
  39.5 7.0 %all-to-all-start.1 = ((bf16[128,2,256]{2,1,0:T(2,128)(2,1)}), bf16[128,2,256]{2,1,0:T(2,128)(2,1)S(1)}, u32[]{:S(2)}, u32[]{:S(2)}) async-start(bf16[128,2,256]{2,1,0:T(2,128)(2,1)} %reshape.22), calls=%async_computation.1 | async-start | bytes 262144 | tf_op jit(solution)/shard_map/all_to_all | solution.py:204
  46.5 3.1 %inside.1 = (bf16[4,256,256]{2,1,0:T(8,128)(2,1)}, f32[4,256,256]{2,1,0:T(8,128)}, f32[256,512]{1,0:T(8,128)}) custom-call(bf16[256,512]{1,0:T(8,128)(2,1)} %q_ref.5, bf16[256,512]{1,0:T(8,128)(2,1)} %k_ref.7, bf16[256,512]{1,0:T(8,128)(2,1)} %v_ref.7, f32[3,256,4]{2,1,0:T(8,128)} %get-tuple-element.25.col_ref, f32[4,256]{1,0:T(4,128)} %get-tuple-element.26.row_ref), custom_call_target="tpu_custom_call" | custom-call | flops 134217728 | bytes 2899968 | tf_op jit(solution)/shard_map/inside/pallas_call | solution.py:26
  49.6 0.8 copy-done.1
  50.4 3.5 %grad_of_norm.1.gn_ref = f32[256,512]{1,0:T(8,128)} custom-call(s32[1]{0:T(128)} %bitcast.core_ref, bf16[256,1024]{1,0:T(8,128)(2,1)} %own_ref.1, bf16[256,1024]{1,0:T(8,128)(2,1)} %copy-done.1, bf16[512,2048]{1,0:T(8,128)(2,1)} %w_ref.3), custom_call_target="tpu_custom_call" | custom-call | flops 536870912 | bytes 3670020 | tf_op jit(solution)/shard_map/grad_of_norm/pallas_call | solution.py:26
  53.9 4.2 %all-to-all-done.1 = bf16[128,2,256]{2,1,0:T(2,128)(2,1)S(1)} async-done(((bf16[128,2,256]{2,1,0:T(2,128)(2,1)}), bf16[128,2,256]{2,1,0:T(2,128)(2,1)S(1)}, u32[]{:S(2)}, u32[]{:S(2)}) %all-to-all-start.1) | async-done | bytes 131104 | tf_op jit(solution)/shard_map/all_to_all | solution.py:204
  58.8 3.0 %norm_and_grad.1 = (bf16[256,512]{1,0:T(8,128)(2,1)}, bf16[256,512]{1,0:T(8,128)(2,1)}, bf16[128,512]{1,0:T(8,128)(2,1)}) custom-call(bf16[256,512]{1,0:T(8,128)(2,1)} %q_ref.5, bf16[128,512]{1,0:T(8,128)(2,1)} %bitcast.17, f32[3,256,4]{2,1,0:T(8,128)} %get-tuple-element.25.col_ref, f32[256,512]{1,0:T(8,128)} %get-tuple-element.27.in_ref, ...), custom_call_target="tpu_custom_call" | custom-call | flops 67108864 | bytes 2109440 | tf_op jit(solution)/shard_map/norm_and_grad/pallas_call | solution.py:26
  61.8 1.6 %reduce.2 = bf16[128,512]{1,0:T(8,128)(2,1)S(1)} reduce(bf16[128,1,512]{2,0,1:T(8,128)(2,1)} %bitcast.24, bf16[]{:T(256)} %broadcast), dimensions={1}, to_apply=%copy.16.reduce_sub_computation | reduce | bytes 262146 | tf_op jit(solution)/shard_map/all_to_all | solution.py:210
  64.1 9.7 %all-to-all-start.2 = ((bf16[128,2,256]{2,1,0:T(2,128)(2,1)}), bf16[128,2,256]{2,1,0:T(2,128)(2,1)S(1)}, u32[]{:S(2)}, u32[]{:S(2)}) async-start(bf16[128,2,256]{2,1,0:T(2,128)(2,1)} %reshape.24), calls=%async_computation.2 | async-start | bytes 262144 | tf_op jit(solution)/shard_map/all_to_all | solution.py:210
  73.8 3.4 %mix.1 = (f32[256,1024]{1,0:T(8,128)}, bf16[256,1024]{1,0:T(8,128)(2,1)}) custom-call(s32[1]{0:T(128)} %bitcast.core_ref, bf16[256,512]{1,0:T(8,128)(2,1)} %get-tuple-element.28.normed_ref, bf16[512,2048]{1,0:T(8,128)(2,1)} %w_ref.3), custom_call_target="tpu_custom_call" | custom-call | flops 536870912 | bytes 3932164 | tf_op jit(solution)/shard_map/mix/pallas_call | solution.py:26
  77.2 8.0 %all-to-all-done.2 = bf16[128,2,256]{2,1,0:T(2,128)(2,1)S(1)} async-done(((bf16[128,2,256]{2,1,0:T(2,128)(2,1)}), bf16[128,2,256]{2,1,0:T(2,128)(2,1)S(1)}, u32[]{:S(2)}, u32[]{:S(2)}) %all-to-all-start.2) | async-done | bytes 131104 | tf_op jit(solution)/shard_map/all_to_all | solution.py:210
  86.0 1.8 %backward_scan.1 = bf16[128,512]{1,0:T(8,128)(2,1)} custom-call(bf16[128,512]{1,0:T(8,128)(2,1)} %bitcast.21, bf16[128,128]{1,0:T(8,128)(2,1)} %get-tuple-element.36.mh_ref, bf16[128,128]{1,0:T(8,128)(2,1)} %get-tuple-element.37.ml_ref), custom_call_target="tpu_custom_call" | custom-call | flops 33554432 | bytes 327680 | tf_op jit(solution)/shard_map/backward_scan/pallas_call | solution.py:26
  87.9 1.6 %reduce.3 = bf16[128,512]{1,0:T(8,128)(2,1)S(1)} reduce(bf16[128,1,512]{2,0,1:T(8,128)(2,1)} %bitcast.22, bf16[]{:T(256)} %broadcast), dimensions={1}, to_apply=%copy.17.reduce_sub_computation | reduce | bytes 262146 | tf_op jit(solution)/shard_map/all_to_all | solution.py:222
  90.1 6.9 %all-to-all-start.3 = ((bf16[128,2,256]{2,1,0:T(2,128)(2,1)}), bf16[128,2,256]{2,1,0:T(2,128)(2,1)S(1)}, u32[]{:S(2)}, u32[]{:S(2)}) async-start(bf16[128,2,256]{2,1,0:T(2,128)(2,1)} %reshape.26), calls=%async_computation.3 | async-start | bytes 262144 | tf_op jit(solution)/shard_map/all_to_all | solution.py:222
  97.0 4.2 %score_grads.1 = (bf16[256,512]{1,0:T(8,128)(2,1)}, f32[256,512]{1,0:T(8,128)}, f32[256,512]{1,0:T(8,128)}) custom-call(bf16[256,512]{1,0:T(8,128)(2,1)} %q_ref.5, bf16[256,512]{1,0:T(8,128)(2,1)} %k_ref.7, bf16[256,512]{1,0:T(8,128)(2,1)} %v_ref.7, bf16[256,512]{1,0:T(8,128)(2,1)} %get-tuple-element.31.g_ref, bf16[128,512]{1,0:T(8,128)(2,1)} %bitcast.18, ...), custom_call_target="tpu_custom_call" | custom-call | flops 301989888 | bytes 4075520 | tf_op jit(solution)/shard_map/score_grads/pallas_call | solution.py:26
  101.3 7.3 %all-to-all-done.3 = bf16[128,2,256]{2,1,0:T(2,128)(2,1)S(1)} async-done(((bf16[128,2,256]{2,1,0:T(2,128)(2,1)}), bf16[128,2,256]{2,1,0:T(2,128)(2,1)S(1)}, u32[]{:S(2)}, u32[]{:S(2)}) %all-to-all-start.3) | async-done | bytes 131104 | tf_op jit(solution)/shard_map/all_to_all | solution.py:222
  109.4 2.6 %finish.1 = (bf16[256,512]{1,0:T(8,128)(2,1)}, bf16[256,512]{1,0:T(8,128)(2,1)}) custom-call(bf16[256,512]{1,0:T(8,128)(2,1)} %k_ref.7, bf16[256,512]{1,0:T(8,128)(2,1)} %v_ref.7, bf16[128,512]{1,0:T(8,128)(2,1)} %bitcast.20, f32[3,256,4]{2,1,0:T(8,128)} %get-tuple-element.25.col_ref, f32[256,512]{1,0:T(8,128)} %get-tuple-element.38.gkp_ref, ...), custom_call_target="tpu_custom_call" | custom-call | flops 67108864 | bytes 2240512 | tf_op jit(solution)/shard_map/finish/pallas_call | solution.py:26
  112.0 0.9 add_convert_fusion
  (19 shorter events, 6.0 us)
Async XLA Ops:
  6.3 27.9 %all-to-all-start = ((bf16[128,2,320]{2,1,0:T(2,128)(2,1)}), bf16[128,2,320]{2,1,0:T(2,128)(2,1)S(1)}, u32[]{:S(2)}, u32[]{:S(2)}) async-start(bf16[128,2,320]{2,1,0:T(2,128)(2,1)} %reshape.20), calls=%async_computation | async-start | bytes 393216 | tf_op jit(solution)/shard_map/all_to_all | solution.py:190
  21.8 27.8 %collective-permute-start = (bf16[256,1024]{1,0:T(8,128)(2,1)}, bf16[256,1024]{1,0:T(8,128)(2,1)S(1)}, u32[]{:S(2)}, u32[]{:S(2)}) collective-permute-start(bf16[256,1024]{1,0:T(8,128)(2,1)} %own_ref.1), channel_id=1, source_target_pairs={{0,1},{1,0},{2,3},{3,2},{4,5},{5,4},{6,7},{7,6},{8,9},{9,8},{10,11... | collective-permute-start | bytes 1572872 | tf_op jit(solution)/shard_map/ppermute | solution.py:184
  39.5 18.5 %all-to-all-start.1 = ((bf16[128,2,256]{2,1,0:T(2,128)(2,1)}), bf16[128,2,256]{2,1,0:T(2,128)(2,1)S(1)}, u32[]{:S(2)}, u32[]{:S(2)}) async-start(bf16[128,2,256]{2,1,0:T(2,128)(2,1)} %reshape.22), calls=%async_computation.1 | async-start | bytes 262144 | tf_op jit(solution)/shard_map/all_to_all | solution.py:204
  49.6 0.8 copy-start.1
  64.1 21.2 %all-to-all-start.2 = ((bf16[128,2,256]{2,1,0:T(2,128)(2,1)}), bf16[128,2,256]{2,1,0:T(2,128)(2,1)S(1)}, u32[]{:S(2)}, u32[]{:S(2)}) async-start(bf16[128,2,256]{2,1,0:T(2,128)(2,1)} %reshape.24), calls=%async_computation.2 | async-start | bytes 262144 | tf_op jit(solution)/shard_map/all_to_all | solution.py:210
  77.2 34.8 %collective-permute-start.1 = (bf16[256,1024]{1,0:T(8,128)(2,1)}, bf16[256,1024]{1,0:T(8,128)(2,1)S(1)}, u32[]{:S(2)}, u32[]{:S(2)}) collective-permute-start(bf16[256,1024]{1,0:T(8,128)(2,1)} %get-tuple-element.30), channel_id=1, source_target_pairs={{0,1},{1,0},{2,3},{3,2},{4,5},{5,4},{6,7},{7,6},{8,9},{9,8},{10,11... | collective-permute-start | bytes 1572872 | tf_op jit(solution)/shard_map/ppermute | solution.py:215
  90.1 18.5 %all-to-all-start.3 = ((bf16[128,2,256]{2,1,0:T(2,128)(2,1)}), bf16[128,2,256]{2,1,0:T(2,128)(2,1)S(1)}, u32[]{:S(2)}, u32[]{:S(2)}) async-start(bf16[128,2,256]{2,1,0:T(2,128)(2,1)} %reshape.26), calls=%async_computation.3 | async-start | bytes 262144 | tf_op jit(solution)/shard_map/all_to_all | solution.py:222
  101.3 10.7 %copy-start = (f32[256,1024]{1,0:T(8,128)S(1)}, f32[256,1024]{1,0:T(8,128)}, u32[]{:S(2)}) copy-start(f32[256,1024]{1,0:T(8,128)} %get-tuple-element.29) | copy-start | bytes 3145732

commit v2 on v1

v2 whole, which is shorter than its diff:
```python
import functools

import jax
import jax.numpy as jnp
from jax import lax
from jax.experimental import pallas as pl
from jax.experimental.pallas import tpu as pltpu
from jax.sharding import PartitionSpec as P

EPS = 1e-05
F32 = jnp.float32
BF = jnp.bfloat16
W = 128
OWN = 4


def dot(a, b, da=1, db=0, precision=None):
    return lax.dot_general(
        a, b, (((da,), (db,)), ((), ())), preferred_element_type=F32, precision=precision
    )


def call(body, outs, *args, flops=0, smem=0, scratch=()):
    spec = [pl.BlockSpec(memory_space=pltpu.SMEM)] * smem
    spec += [pl.BlockSpec(memory_space=pltpu.VMEM)] * (len(args) - smem)
    moved = sum(a.size * a.dtype.itemsize for a in (*args, *outs))
    return pl.pallas_call(
        body,
        out_shape=outs,
        in_specs=spec,
        out_specs=[pl.BlockSpec(memory_space=pltpu.VMEM)] * len(outs),
        scratch_shapes=[pltpu.VMEM(dims, F32) for dims in scratch],
        compiler_params=pltpu.CompilerParams(vmem_limit_bytes=12 << 20),
        cost_estimate=pl.CostEstimate(flops=flops, bytes_accessed=moved, transcendentals=0),
        name=body.__name__ if hasattr(body, "__name__") else body.func.__name__,
    )(*args)


def shape(*dims, dtype=BF):
    return jax.ShapeDtypeStruct(dims, dtype)


def head_cols(h):
    return slice(h * W, (h + 1) * W)


def block_delta(k_ref, v_ref, ld_ref, pay_ref, col_ref, row_ref, delta_ref, mixed_ref):
    heads, span = ld_ref.shape
    slots, six = delta_ref.shape[0] // OWN, OWN + 2
    per = slots // heads
    ld = ld_ref[...]
    a = lax.broadcasted_iota(jnp.int32, (span, span), 0)
    b = lax.broadcasted_iota(jnp.int32, (span, span), 1)
    col = dot((b <= a).astype(F32), ld, 1, 1, precision=lax.Precision.HIGHEST)
    last = col[span - 1 : span, :]
    weight = jnp.exp(last - col)
    lane = lax.broadcasted_iota(jnp.int32, (per, W), 1)
    for h in range(heads):
        kw = (k_ref[:, head_cols(h)].astype(F32) * weight[:, h : h + 1]).astype(BF)
        delta_ref[h * W : (h + 1) * W] = dot(kw, v_ref[:, head_cols(h)], 0, 0)
        end = jnp.broadcast_to(last[:, h : h + 1], (per, W))
        hi = end.astype(BF).astype(F32)
        mid = (end - hi).astype(BF).astype(F32)
        low = end - hi - mid
        tail = jnp.where(lane == 0, hi, jnp.where(lane == 1, mid, jnp.where(lane == 2, low, 0.0)))
        mixed_ref[pl.ds(h * per * six + OWN, per, stride=six)] = tail
        mixed_ref[pl.ds(h * per * six + OWN + 1, per, stride=six)] = tail
    for r in range(OWN):
        mixed_ref[pl.ds(r, slots, stride=six)] = delta_ref[pl.ds(r, slots, stride=OWN)]
    pay_ref[...] = mixed_ref[...].astype(BF)
    col_ref[0] = jnp.exp(col)
    col_ref[1] = weight
    col_ref[2] = col
    row_ref[...] = dot(ld, (a <= b).astype(F32), precision=lax.Precision.HIGHEST)


def inside(q_ref, k_ref, v_ref, col_ref, row_ref, probs_ref, mask_ref, in_ref):
    heads, span = row_ref.shape
    a = lax.broadcasted_iota(jnp.int32, (span, span), 0)
    b = lax.broadcasted_iota(jnp.int32, (span, span), 1)
    for h in range(heads):
        gap = col_ref[2][:, h : h + 1] - row_ref[h : h + 1, :]
        mask = jnp.where(b <= a, jnp.exp(jnp.minimum(gap, 0.0)), 0.0)
        mask_ref[h] = mask
        probs = (dot(q_ref[:, head_cols(h)], k_ref[:, head_cols(h)], 1, 1) * mask).astype(BF)
        probs_ref[h] = probs
        in_ref[:, head_cols(h)] = dot(probs, v_ref[:, head_cols(h)])


def grad_of_norm(core_ref, own_ref, other_ref, w_ref, out_ref):
    width = own_ref.shape[1]
    mine = pl.multiple_of(core_ref[0] * width, width)
    theirs = pl.multiple_of((1 - core_ref[0]) * width, width)
    out_ref[...] = dot(own_ref[...], w_ref[:, pl.ds(mine, width)], 1, 1) + dot(
        other_ref[...], w_ref[:, pl.ds(theirs, width)], 1, 1
    )


def forward_scan(x_ref, y_ref, mh_ref, ml_ref, x32_ref, y32_ref):
    count = mh_ref.shape[0]
    six = x_ref.shape[0] // count
    x32_ref[...] = x_ref[...].astype(F32)
    i = lax.broadcasted_iota(jnp.int32, (count, count), 0)
    j = lax.broadcasted_iota(jnp.int32, (count, count), 1)
    before = (j < i).astype(BF)
    gap = jnp.zeros((count, count), F32)
    ends = x32_ref[pl.ds(OWN, count, stride=six)]
    for piece in range(3):
        gap = gap + dot(before, jnp.where(j < i, ends[:, piece : piece + 1], 0.0).astype(BF))
    reach = jnp.where(j < i, jnp.exp(jnp.minimum(gap, 0.0)), 0.0)
    high = reach.astype(BF)
    low = (reach - high.astype(F32)).astype(BF)
    mh_ref[...] = high
    ml_ref[...] = low
    for r in range(OWN):
        x = x32_ref[pl.ds(r, count, stride=six)].astype(BF)
        y32_ref[pl.ds(r, count, stride=OWN)] = dot(high, x) + dot(low, x)
    y_ref[...] = y32_ref[...].astype(BF)


def backward_scan(x_ref, mh_ref, ml_ref, y_ref, x32_ref, y32_ref):
    count = mh_ref.shape[0]
    x32_ref[...] = x_ref[...].astype(F32)
    for r in range(OWN):
        x = x32_ref[pl.ds(r, count, stride=OWN)].astype(BF)
        y32_ref[pl.ds(r, count, stride=OWN)] = dot(mh_ref[...], x, 0, 0) + dot(ml_ref[...], x, 0, 0)
    y_ref[...] = y32_ref[...].astype(BF)


def norm_and_grad(q_ref, s_ref, col_ref, in_ref, gn_ref, normed_ref, g_ref, pay_ref):
    heads = in_ref.shape[1] // W
    for h in range(heads):
        cols = head_cols(h)
        growth = col_ref[0][:, h : h + 1]
        q = q_ref[:, cols]
        att = in_ref[:, cols] + growth * dot(q, s_ref[h * W : (h + 1) * W])
        inv = lax.rsqrt(jnp.mean(att * att, axis=1, keepdims=True) + EPS)
        normed_ref[:, cols] = (att * inv).astype(BF)
        gn = gn_ref[:, cols]
        g = inv * gn - att * (inv * inv * inv * jnp.mean(gn * att, axis=1, keepdims=True))
        g = g.astype(BF)
        g_ref[:, cols] = g
        pay_ref[h * W : (h + 1) * W] = dot((q.astype(F32) * growth).astype(BF), g, 0, 0).astype(BF)


def mix(core_ref, normed_ref, w_ref, own_ref, other_ref):
    width = own_ref.shape[1]
    mine = pl.multiple_of(core_ref[0] * width, width)
    theirs = pl.multiple_of((1 - core_ref[0]) * width, width)
    other_ref[...] = dot(normed_ref[...], w_ref[:, pl.ds(theirs, width)]).astype(BF)
    own_ref[...] = dot(normed_ref[...], w_ref[:, pl.ds(mine, width)])


def score_grads(q_ref, k_ref, v_ref, g_ref, s_ref, col_ref, probs_ref, mask_ref, gq_ref, gk_ref, gv_ref):
    heads = probs_ref.shape[0]
    for h in range(heads):
        cols = head_cols(h)
        g = g_ref[:, cols]
        d = (dot(g, v_ref[:, cols], 1, 1) * mask_ref[h]).astype(BF)
        carried = dot(g, s_ref[h * W : (h + 1) * W], 1, 1)
        gq_ref[:, cols] = (dot(d, k_ref[:, cols]) + col_ref[0][:, h : h + 1] * carried).astype(BF)
        gk_ref[:, cols] = dot(d, q_ref[:, cols], 0, 0)
        gv_ref[:, cols] = dot(probs_ref[h], g, 0, 0)


def finish(k_ref, v_ref, e_ref, col_ref, gkp_ref, gvp_ref, gk_ref, gv_ref):
    heads = gk_ref.shape[1] // W
    for h in range(heads):
        cols = head_cols(h)
        weight = col_ref[1][:, h : h + 1]
        e = e_ref[h * W : (h + 1) * W]
        gk_ref[:, cols] = (gkp_ref[:, cols] + weight * dot(v_ref[:, cols], e, 1, 1)).astype(BF)
        gv_ref[:, cols] = (gvp_ref[:, cols] + weight * dot(k_ref[:, cols], e)).astype(BF)


def local(queries, keys, values, log_decay, out_weight, out_grad):
    rows, width = queries.shape
    heads, span = log_decay.shape
    count = lax.axis_size("ctx")
    lines = heads * W
    assert lines == OWN * count
    model = out_weight.shape[1]
    core = lax.axis_index("head").astype(jnp.int32).reshape(1)
    swap = [(0, 1), (1, 0)]

    other_grad = lax.ppermute(out_grad, "head", swap)
    pay, col, row = call(
        block_delta,
        [shape(count * (OWN + 2), W), shape(3, rows, heads, dtype=F32), shape(heads, span, dtype=F32)],
        keys, values, log_decay, flops=rows * width * W * 2,
        scratch=[(lines, W), (count * (OWN + 2), W)],
    )
    got = lax.all_to_all(pay.reshape(-1, 2, W), "ctx", 0, 0, tiled=True).reshape(-1, W)
    probs, mask, within = call(
        inside,
        [shape(heads, span, span), shape(heads, span, span, dtype=F32), shape(rows, width, dtype=F32)],
        queries, keys, values, col, row, flops=rows * width * span * 4,
    )
    (grad_norm,) = call(
        grad_of_norm, [shape(rows, width, dtype=F32)], core, out_grad, other_grad, out_weight,
        flops=2 * rows * width * model, smem=1,
    )
    sent, high, low = call(
        forward_scan, [shape(lines, W), shape(count, count), shape(count, count)], got,
        flops=4 * count * lines * W, scratch=[(count * (OWN + 2), W), (lines, W)],
    )
    state = lax.all_to_all(sent, "ctx", 0, 0, tiled=True)
    normed, grad_att, pay = call(
        norm_and_grad,
        [shape(rows, width), shape(rows, width), shape(lines, W)],
        queries, state, col, within, grad_norm, flops=rows * width * W * 4,
    )
    got = lax.all_to_all(pay, "ctx", 0, 0, tiled=True)
    own, other = call(
        mix, [shape(rows, model // 2, dtype=F32), shape(rows, model // 2)], core, normed, out_weight,
        flops=2 * rows * width * model, smem=1,
    )
    theirs = lax.ppermute(other, "head", swap)
    grad_q, gk_part, gv_part = call(
        score_grads,
        [shape(rows, width), shape(rows, width, dtype=F32), shape(rows, width, dtype=F32)],
        queries, keys, values, grad_att, state, col, probs, mask, flops=rows * width * span * 9,
    )
    (sent,) = call(
        backward_scan, [shape(lines, W)], got, high, low, flops=4 * count * lines * W,
        scratch=[(lines, W), (lines, W)],
    )
    leaving = lax.all_to_all(sent, "ctx", 0, 0, tiled=True)
    mixed = (own + theirs.astype(F32)).astype(BF)
    mixed, gk_part = lax.optimization_barrier((mixed, gk_part))
    grad_k, grad_v = call(
        finish, [shape(rows, width), shape(rows, width)], keys, values, leaving, col, gk_part, gv_part,
        flops=rows * width * W * 4,
    )
    return mixed, grad_q, grad_k, grad_v


def solution(mesh):
    split = P("ctx", "head")
    return jax.shard_map(
        local,
        mesh=mesh,
        in_specs=(split, split, split, P("head", "ctx"), P("head", None), split),
        out_specs=(split,) * 4,
        check_vma=False,
    )
```

time: 114 us -> 108 us (0.947)
  Pallas kernels: 26.4 us -> 12.1 us
  local copies, waits for them, and re-layouts: 7.57 us -> 19.7 us
  other arithmetic: 7.23 us -> 1.98 us
  starting transfers between devices: 39 us -> 43.7 us
  waiting for transfers between devices: 31.9 us -> 28.5 us
    all_to_all x2 -> x1, waiting for transfers between devices: 20.4 us -> 4.86 us  [local(): got = lax.all_to_all(pay, 'ctx', 0, 0, tiled=True)]
    all_to_all x0 -> x1, starting transfers between devices: none -> 15.4 us  [local(): lax.all_to_all(pay.reshape(-1, 2, W), 'ctx', 0, 0, tiled=True)]
    pallas_call x9, Pallas kernels: 26.4 us -> 12.1 us  [call(): pl.pallas_call(body, out_shape=outs, in_specs=spec, out_specs=[pl.BlockSp...]
    all_to_all x2 -> x1, starting transfers between devices: 25.1 us -> 12.3 us  [local(): got = lax.all_to_all(pay, 'ctx', 0, 0, tiled=True)]
    unnamed x16 -> x62, local copies, waits for them, and re-layouts: 7.02 us -> 19.7 us
    all_to_all x0 -> x1, waiting for transfers between devices: none -> 12.4 us  [local(): lax.all_to_all(pay.reshape(-1, 2, W), 'ctx', 0, 0, tiled=True)]
    all_to_all x4 -> x0, other arithmetic: 6.28 us -> none  [the longest x2 3.15 us: local(): got = lax.all_to_all(pay, 'ctx', 0, 0, tiled=True)]
    all_to_all x1, waiting for transfers between devices: 4.19 us -> 1.76 us  [local(): state = lax.all_to_all(sent, 'ctx', 0, 0, tiled=True)]
  transfers between devices with their start and end apart: 6 -> 6, of which waited for: 4 -> 4; matrix products, arithmetic and copies ran while one was open for 6% -> 2% of each run, Pallas kernels for 18% -> 6%
where the time goes in v2:
time: 108 us; the launch traced here: 107 us
  starting transfers between devices  43.7 us (40%)
  waiting for transfers between devices  28.5 us (26%)
  local copies, waits for them, and re-layouts  19.7 us (18%)
  Pallas kernels  12.1 us (11%)
  other arithmetic  1.98 us (2%)
    unnamed x62, local copies, waits for them, and re-layouts  19.7 us
    all_to_all x1, starting transfers between devices, local(): lax.all_to_all(pay.reshape(-1, 2, W), 'ctx', 0, 0, tiled=True)  15.4 us
    all_to_all x1, waiting for transfers between devices, local(): lax.all_to_all(pay.reshape(-1, 2, W), 'ctx', 0, 0, tiled=True)  12.4 us
    all_to_all x1, starting transfers between devices, local(): got = lax.all_to_all(pay, 'ctx', 0, 0, tiled=True)  12.3 us
    pallas_call x9, Pallas kernels, call(): pl.pallas_call(body, out_shape=outs, in_specs=spec, out_specs=[pl.BlockSp...  12.1 us
    all_to_all x1, waiting for transfers between devices, local(): leaving = lax.all_to_all(sent, 'ctx', 0, 0, tiled=True)  9.48 us
    all_to_all x1, starting transfers between devices, local(): leaving = lax.all_to_all(sent, 'ctx', 0, 0, tiled=True)  8.94 us
    all_to_all x1, starting transfers between devices, local(): state = lax.all_to_all(sent, 'ctx', 0, 0, tiled=True)  6.95 us
  transfers between devices with their start and end apart: 6, of which 4 were waited for; matrix products, arithmetic and copies ran while one was open for 2% of the time, Pallas kernels for 6%

profile of v2, /device:TPU:2, one launch (start us, length us, event | category | flops | bytes accessed | tf_op | source)
XLA Modules:
  0.0 106.8 jit_solution(11074852295537828688)
XLA Ops:
  1.6 0.9 copy-done.4
  3.2 1.7 %block_delta.1 = (bf16[768,128]{1,0:T(8,128)(2,1)}, f32[3,256,4]{2,1,0:T(8,128)S(1)}, f32[4,256]{1,0:T(4,128)S(1)}) custom-call(bf16[256,512]{1,0:T(8,128)(2,1)S(1)} %copy-done.1, bf16[256,512]{1,0:T(8,128)(2,1)S(1)} %copy-done.4, f32[4,256]{1,0:T(4,128)S(1)} %copy-done.30), custom_call_target="tpu_custom_call" | custom-call | flops 33554432 | bytes 741376 | tf_op jit(solution)/shard_map/block_delta/pallas_call | solution.py:27
  4.9 15.4 %all-to-all-start = ((bf16[384,2,128]{2,1,0:T(2,128)(2,1)}), bf16[384,2,128]{2,1,0:T(2,128)(2,1)S(1)}, u32[]{:S(2)}, u32[]{:S(2)}) async-start(bf16[384,2,128]{2,1,0:T(2,128)(2,1)} %bitcast.1), calls=%async_computation | async-start | bytes 393216 | tf_op jit(solution)/shard_map/all_to_all | solution.py:193
  20.4 12.4 %all-to-all-done = bf16[384,2,128]{2,1,0:T(2,128)(2,1)S(1)} async-done(((bf16[384,2,128]{2,1,0:T(2,128)(2,1)}), bf16[384,2,128]{2,1,0:T(2,128)(2,1)S(1)}, u32[]{:S(2)}, u32[]{:S(2)}) %all-to-all-start) | async-done | bytes 196640 | tf_op jit(solution)/shard_map/all_to_all | solution.py:193
  32.8 1.2 %forward_scan.1 = (bf16[512,128]{1,0:T(8,128)(2,1)}, bf16[128,128]{1,0:T(8,128)(2,1)S(1)}, bf16[128,128]{1,0:T(8,128)(2,1)S(1)}) custom-call(bf16[768,128]{1,0:T(8,128)(2,1)S(1)} %bitcast.11), custom_call_target="tpu_custom_call" | custom-call | flops 33554432 | bytes 393216 | tf_op jit(solution)/shard_map/forward_scan/pallas_call | solution.py:27
  35.2 6.9 %all-to-all-start.1 = ((bf16[128,4,128]{2,1,0:T(4,128)(2,1)}), bf16[128,4,128]{2,1,0:T(4,128)(2,1)S(1)}, u32[]{:S(2)}, u32[]{:S(2)}) async-start(bf16[128,4,128]{2,1,0:T(4,128)(2,1)} %bitcast.3), calls=%async_computation.1 | async-start | bytes 262144 | tf_op jit(solution)/shard_map/all_to_all | solution.py:207
  45.7 1.0 copy-done.11
  48.3 1.1 %copy-done.17 = bf16[256,1024]{1,0:T(8,128)(2,1)S(1)} copy-done((bf16[256,1024]{1,0:T(8,128)(2,1)S(1)}, bf16[256,1024]{1,0:T(8,128)(2,1)}, u32[]{:S(2)}) %copy-start.17) | copy-done | bytes 524312
  49.3 1.8 %grad_of_norm.1.gn_ref = f32[256,512]{1,0:T(8,128)S(1)} custom-call(s32[1]{0:T(128)} %bitcast.core_ref, bf16[256,1024]{1,0:T(8,128)(2,1)S(1)} %copy-done.17, bf16[256,1024]{1,0:T(8,128)(2,1)} %collective-permute-done.other_ref, bf16[512,2048]{1,0:T(8,128)(2,1)S(1)} %copy-done), custom_call_target="tpu_custom_call" | custom-call | flops 536870912 | bytes 3670020 | tf_op jit(solution)/shard_map/grad_of_norm/pallas_call | solution.py:27
  51.9 1.8 %all-to-all-done.1 = bf16[128,4,128]{2,1,0:T(4,128)(2,1)S(1)} async-done(((bf16[128,4,128]{2,1,0:T(4,128)(2,1)}), bf16[128,4,128]{2,1,0:T(4,128)(2,1)S(1)}, u32[]{:S(2)}, u32[]{:S(2)}) %all-to-all-start.1) | async-done | bytes 131104 | tf_op jit(solution)/shard_map/all_to_all | solution.py:207
  53.7 1.0 copy-done.10
  54.8 1.0 copy-done.16
  55.8 1.6 %norm_and_grad.1 = (bf16[256,512]{1,0:T(8,128)(2,1)S(1)}, bf16[256,512]{1,0:T(8,128)(2,1)S(1)}, bf16[512,128]{1,0:T(8,128)(2,1)}) custom-call(bf16[256,512]{1,0:T(8,128)(2,1)S(1)} %copy-done.8, bf16[512,128]{1,0:T(8,128)(2,1)S(1)} %bitcast.9, f32[3,256,4]{2,1,0:T(8,128)S(1)} %get-tuple-element.27.col_ref, f32[256,512]{1,0:T(8,128)S(1)} %copy-done.16, ...), custom_call_target="tpu_custom_call" | custom-call | flops 67108864 | bytes 2109440 | tf_op jit(solution)/shard_map/norm_and_grad/pallas_call | solution.py:27
  58.1 1.2 %mix.1 = (f32[256,1024]{1,0:T(8,128)S(1)}, bf16[256,1024]{1,0:T(8,128)(2,1)}) custom-call(s32[1]{0:T(128)} %bitcast.core_ref, bf16[256,512]{1,0:T(8,128)(2,1)S(1)} %get-tuple-element.30.normed_ref, bf16[512,2048]{1,0:T(8,128)(2,1)S(1)} %copy-done), custom_call_target="tpu_custom_call" | custom-call | flops 536870912 | bytes 3932164 | tf_op jit(solution)/shard_map/mix/pallas_call | solution.py:27
  59.3 1.0 copy-done.13
  60.3 12.3 %all-to-all-start.2 = ((bf16[128,4,128]{2,1,0:T(4,128)(2,1)}), bf16[128,4,128]{2,1,0:T(4,128)(2,1)S(1)}, u32[]{:S(2)}, u32[]{:S(2)}) async-start(bf16[128,4,128]{2,1,0:T(4,128)(2,1)} %bitcast.5), calls=%async_computation.2 | async-start | bytes 262144 | tf_op jit(solution)/shard_map/all_to_all | solution.py:213
  72.6 1.2 %copy-done.12 = f32[4,256,256]{2,1,0:T(8,128)S(1)} copy-done((f32[4,256,256]{2,1,0:T(8,128)S(1)}, f32[4,256,256]{2,1,0:T(8,128)}, u32[]{:S(2)}) %copy-start.12) | copy-done | bytes 1048600
  73.8 1.0 copy-done.19
  75.8 2.0 %score_grads.1 = (bf16[256,512]{1,0:T(8,128)(2,1)}, f32[256,512]{1,0:T(8,128)S(1)}, f32[256,512]{1,0:T(8,128)S(1)}) custom-call(bf16[256,512]{1,0:T(8,128)(2,1)S(1)} %copy-done.8, bf16[256,512]{1,0:T(8,128)(2,1)S(1)} %copy-done.3, bf16[256,512]{1,0:T(8,128)(2,1)S(1)} %copy-done.6, bf16[256,512]{1,0:T(8,128)(2,1)S(1)} %copy-done.25, ...), custom_call_target="tpu_custom_call" | custom-call | flops 301989888 | bytes 4075520 | tf_op jit(solution)/shard_map/score_grads/pallas_call | solution.py:27
  79.5 4.9 %all-to-all-done.2 = bf16[128,4,128]{2,1,0:T(4,128)(2,1)S(1)} async-done(((bf16[128,4,128]{2,1,0:T(4,128)(2,1)}), bf16[128,4,128]{2,1,0:T(4,128)(2,1)S(1)}, u32[]{:S(2)}, u32[]{:S(2)}) %all-to-all-start.2) | async-done | bytes 131104 | tf_op jit(solution)/shard_map/all_to_all | solution.py:213
  85.3 8.9 %all-to-all-start.3 = ((bf16[128,4,128]{2,1,0:T(4,128)(2,1)}), bf16[128,4,128]{2,1,0:T(4,128)(2,1)S(1)}, u32[]{:S(2)}, u32[]{:S(2)}) async-start(bf16[128,4,128]{2,1,0:T(4,128)(2,1)} %bitcast.7), calls=%async_computation.3 | async-start | bytes 262144 | tf_op jit(solution)/shard_map/all_to_all | solution.py:228
  94.2 2.0 %add_convert_fusion = bf16[256,1024]{1,0:T(8,128)(2,1)} fusion(f32[256,1024]{1,0:T(8,128)S(1)} %copy-done.14, bf16[256,1024]{1,0:T(8,128)(2,1)} %collective-permute-done.1), kind=kLoop, calls=%fused_computation | loop fusion | flops 786432 | bytes 2097152 | tf_op jit(solution)/shard_map/convert_element_type | solution.py:229
  96.2 9.5 %all-to-all-done.3 = bf16[128,4,128]{2,1,0:T(4,128)(2,1)S(1)} async-done(((bf16[128,4,128]{2,1,0:T(4,128)(2,1)}), bf16[128,4,128]{2,1,0:T(4,128)(2,1)S(1)}, u32[]{:S(2)}, u32[]{:S(2)}) %all-to-all-start.3) | async-done | bytes 131104 | tf_op jit(solution)/shard_map/all_to_all | solution.py:228
  105.7 1.1 %finish.1 = (bf16[256,512]{1,0:T(8,128)(2,1)}, bf16[256,512]{1,0:T(8,128)(2,1)}) custom-call(bf16[256,512]{1,0:T(8,128)(2,1)S(1)} %copy-done.3, bf16[256,512]{1,0:T(8,128)(2,1)S(1)} %copy-done.6, bf16[512,128]{1,0:T(8,128)(2,1)S(1)} %bitcast.12, f32[3,256,4]{2,1,0:T(8,128)S(1)} %get-tuple-element.27.col_ref, f32[256,512]{1,0:T(8,128)S(1)} %copy-done.21, ...), custom_call_target="tpu_custom_call" | custom-call | flops 67108864 | bytes 2240512 | tf_op jit(solution)/shard_map/finish/pallas_call | solution.py:27
  (60 shorter events, 13.1 us)
Async XLA Ops:
  0.6 1.0 copy-start.1
  3.2 45.0 %copy-start = (bf16[512,2048]{1,0:T(8,128)(2,1)S(1)}, bf16[512,2048]{1,0:T(8,128)(2,1)}, u32[]{:S(2)}) copy-start(bf16[512,2048]{1,0:T(8,128)(2,1)} %w_ref.3) | copy-start | bytes 6291460
  4.9 27.9 %all-to-all-start = ((bf16[384,2,128]{2,1,0:T(2,128)(2,1)}), bf16[384,2,128]{2,1,0:T(2,128)(2,1)S(1)}, u32[]{:S(2)}, u32[]{:S(2)}) async-start(bf16[384,2,128]{2,1,0:T(2,128)(2,1)} %bitcast.1), calls=%async_computation | async-start | bytes 393216 | tf_op jit(solution)/shard_map/all_to_all | solution.py:193
  20.3 27.9 %collective-permute-start = (bf16[256,1024]{1,0:T(8,128)(2,1)}, bf16[256,1024]{1,0:T(8,128)(2,1)}, u32[]{:S(2)}, u32[]{:S(2)}) collective-permute-start(bf16[256,1024]{1,0:T(8,128)(2,1)} %own_ref.1), channel_id=1, source_target_pairs={{0,1},{1,0},{2,3},{3,2},{4,5},{5,4},{6,7},{7,6},{8,9},{9,8},{10,11... | collective-permute-start | bytes 1572872 | tf_op jit(solution)/shard_map/ppermute | solution.py:186
  35.2 18.5 %all-to-all-start.1 = ((bf16[128,4,128]{2,1,0:T(4,128)(2,1)}), bf16[128,4,128]{2,1,0:T(4,128)(2,1)S(1)}, u32[]{:S(2)}, u32[]{:S(2)}) async-start(bf16[128,4,128]{2,1,0:T(4,128)(2,1)} %bitcast.3), calls=%async_computation.1 | async-start | bytes 262144 | tf_op jit(solution)/shard_map/all_to_all | solution.py:207
  42.1 1.0 copy-start.2
  45.7 1.0 copy-start.11
  48.3 5.5 %copy-start.8 = (bf16[256,512]{1,0:T(8,128)(2,1)S(1)}, bf16[256,512]{1,0:T(8,128)(2,1)}, u32[]{:S(2)}) copy-start(bf16[256,512]{1,0:T(8,128)(2,1)} %q_ref.5) | copy-start | bytes 786436
  48.3 1.1 %copy-start.17 = (bf16[256,1024]{1,0:T(8,128)(2,1)S(1)}, bf16[256,1024]{1,0:T(8,128)(2,1)}, u32[]{:S(2)}) copy-start(bf16[256,1024]{1,0:T(8,128)(2,1)} %own_ref.1) | copy-start | bytes 1572868
  53.7 1.0 copy-start.10
  54.8 1.0 copy-start.16
  55.8 16.8 %copy-start.3 = (bf16[256,512]{1,0:T(8,128)(2,1)S(1)}, bf16[256,512]{1,0:T(8,128)(2,1)}, u32[]{:S(2)}) copy-start(bf16[256,512]{1,0:T(8,128)(2,1)} %k_ref.7) | copy-start | bytes 786436
  55.8 16.8 %copy-start.6 = (bf16[256,512]{1,0:T(8,128)(2,1)S(1)}, bf16[256,512]{1,0:T(8,128)(2,1)}, u32[]{:S(2)}) copy-start(bf16[256,512]{1,0:T(8,128)(2,1)} %v_ref.7) | copy-start | bytes 786436
  59.3 1.0 copy-start.13
  60.3 24.0 %copy-start.27 = (bf16[128,128]{1,0:T(8,128)(2,1)S(1)}, bf16[128,128]{1,0:T(8,128)(2,1)}, u32[]{:S(2)}) copy-start(bf16[128,128]{1,0:T(8,128)(2,1)} %copy-done.26) | copy-start | bytes 98308
  60.3 24.0 %copy-start.29 = (bf16[128,128]{1,0:T(8,128)(2,1)S(1)}, bf16[128,128]{1,0:T(8,128)(2,1)}, u32[]{:S(2)}) copy-start(bf16[128,128]{1,0:T(8,128)(2,1)} %copy-done.28) | copy-start | bytes 98308
  60.3 33.9 %collective-permute-start.1 = (bf16[256,1024]{1,0:T(8,128)(2,1)}, bf16[256,1024]{1,0:T(8,128)(2,1)}, u32[]{:S(2)}, u32[]{:S(2)}) collective-permute-start(bf16[256,1024]{1,0:T(8,128)(2,1)} %get-tuple-element.32), channel_id=1, source_target_pairs={{0,1},{1,0},{2,3},{3,2},{4,5},{5,4},{6,7},{7,6},{8,9},{9,8},{10,11... | collective-permute-start | bytes 1572872 | tf_op jit(solution)/shard_map/ppermute | solution.py:218
  60.3 24.0 %all-to-all-start.2 = ((bf16[128,4,128]{2,1,0:T(4,128)(2,1)}), bf16[128,4,128]{2,1,0:T(4,128)(2,1)S(1)}, u32[]{:S(2)}, u32[]{:S(2)}) async-start(bf16[128,4,128]{2,1,0:T(4,128)(2,1)} %bitcast.5), calls=%async_computation.2 | async-start | bytes 262144 | tf_op jit(solution)/shard_map/all_to_all | solution.py:213
  72.6 1.2 %copy-start.12 = (f32[4,256,256]{2,1,0:T(8,128)S(1)}, f32[4,256,256]{2,1,0:T(8,128)}, u32[]{:S(2)}) copy-start(f32[4,256,256]{2,1,0:T(8,128)} %copy-done.11) | copy-start | bytes 3145732
  73.8 1.0 copy-start.19
  75.8 18.4 %copy-start.14 = (f32[256,1024]{1,0:T(8,128)S(1)}, f32[256,1024]{1,0:T(8,128)}, u32[]{:S(2)}) copy-start(f32[256,1024]{1,0:T(8,128)} %copy-done.13) | copy-start | bytes 3145732
  84.3 21.4 %copy-start.21 = (f32[256,512]{1,0:T(8,128)S(1)}, f32[256,512]{1,0:T(8,128)}, u32[]{:S(2)}) copy-start(f32[256,512]{1,0:T(8,128)} %copy-done.20) | copy-start | bytes 1572868
  84.3 21.4 %copy-start.23 = (f32[256,512]{1,0:T(8,128)S(1)}, f32[256,512]{1,0:T(8,128)}, u32[]{:S(2)}) copy-start(f32[256,512]{1,0:T(8,128)} %copy-done.22) | copy-start | bytes 1572868
  85.3 20.4 %all-to-all-start.3 = ((bf16[128,4,128]{2,1,0:T(4,128)(2,1)}), bf16[128,4,128]{2,1,0:T(4,128)(2,1)S(1)}, u32[]{:S(2)}, u32[]{:S(2)}) async-start(bf16[128,4,128]{2,1,0:T(4,128)(2,1)} %bitcast.7), calls=%async_computation.3 | async-start | bytes 262144 | tf_op jit(solution)/shard_map/all_to_all | solution.py:228
  (13 other events, 10.4 us)

commit v3 on v2

v3 whole, which is shorter than its diff:
```python
import math

import jax
import jax.numpy as jnp
from jax import lax
from jax.experimental import pallas as pl
from jax.experimental.pallas import tpu as pltpu
from jax.sharding import PartitionSpec as P

EPS = 1e-05
F32 = jnp.float32
BF = jnp.bfloat16
W = 128
OWN = 4
EXACT = lax.Precision.HIGHEST


def dot(a, b, da=1, db=0, precision=None):
    return lax.dot_general(
        a, b, (((da,), (db,)), ((), ())), preferred_element_type=F32, precision=precision
    )


def call(body, outs, *args, flops=0, far=(), smem=0, scratch=()):
    def spec(i):
        if i < smem:
            return pl.BlockSpec(memory_space=pltpu.SMEM)
        return pl.BlockSpec(memory_space=pltpu.HBM if i in far else pltpu.VMEM)

    buffers = [pltpu.VMEM(dims, kind) for dims, kind in scratch]
    buffers += [pltpu.VMEM(args[i].shape, args[i].dtype) for i in far]
    if far:
        buffers += [pltpu.SemaphoreType.DMA((len(far),))]
    args = [pltpu.with_memory_space_constraint(a, pltpu.HBM) if i in far else a for i, a in enumerate(args)]
    moved = sum(math.prod(a.shape) * a.dtype.itemsize for a in (*args, *outs))
    return pl.pallas_call(
        body,
        out_shape=outs,
        in_specs=[spec(i) for i in range(len(args))],
        out_specs=[pl.BlockSpec(memory_space=pltpu.VMEM)] * len(outs),
        scratch_shapes=buffers,
        compiler_params=pltpu.CompilerParams(vmem_limit_bytes=12 << 20),
        cost_estimate=pl.CostEstimate(flops=flops, bytes_accessed=moved, transcendentals=0),
        name=body.__name__,
    )(*args)


def fetch(sources, places, sems):
    copies = [pltpu.make_async_copy(a, b, sems.at[i]) for i, (a, b) in enumerate(zip(sources, places))]
    for copy in copies:
        copy.start()
    return copies


def shape(*dims, dtype=BF):
    return jax.ShapeDtypeStruct(dims, dtype)


def near(*dims, dtype=BF):
    return pltpu.VMEM(dims, dtype)


def head_cols(h):
    return slice(h * W, (h + 1) * W)


def head_rows(h):
    return slice(h * W, (h + 1) * W)


def grid_of(n):
    return lax.broadcasted_iota(jnp.int32, (n, n), 0), lax.broadcasted_iota(jnp.int32, (n, n), 1)


def block_delta(k_far, v_far, ld_far, pay_ref, col_ref, delta_ref, mixed_ref, k_ref, v_ref, ld_ref, sems):
    heads, span = ld_ref.shape
    slots, six = delta_ref.shape[0] // OWN, OWN + 2
    per = slots // heads
    copies = fetch((k_far, v_far, ld_far), (k_ref, v_ref, ld_ref), sems)
    a, b = grid_of(span)
    lane = lax.broadcasted_iota(jnp.int32, (per, W), 1)
    copies[2].wait()
    col = dot((b <= a).astype(F32), ld_ref[...], 1, 1, precision=EXACT)
    last = col[span - 1 : span, :]
    weight = jnp.exp(last - col)
    copies[0].wait()
    copies[1].wait()
    for h in range(heads):
        kw = (k_ref[:, head_cols(h)].astype(F32) * weight[:, h : h + 1]).astype(BF)
        delta_ref[head_rows(h)] = dot(kw, v_ref[:, head_cols(h)], 0, 0)
        end = jnp.broadcast_to(last[:, h : h + 1], (per, W))
        hi = end.astype(BF).astype(F32)
        mid = (end - hi).astype(BF).astype(F32)
        low = end - hi - mid
        tail = jnp.where(lane == 0, hi, jnp.where(lane == 1, mid, jnp.where(lane == 2, low, 0.0)))
        mixed_ref[pl.ds(h * per * six + OWN, per, stride=six)] = tail
        mixed_ref[pl.ds(h * per * six + OWN + 1, per, stride=six)] = tail
    for r in range(OWN):
        mixed_ref[pl.ds(r, slots, stride=six)] = delta_ref[pl.ds(r, slots, stride=OWN)]
    pay_ref[...] = mixed_ref[...].astype(BF)
    col_ref[:, :heads] = jnp.exp(col)
    col_ref[:, heads : 2 * heads] = weight
    col_ref[:, 2 * heads : 3 * heads] = col


def masked_probs(h, heads, q, k, col_ref, row, a, b):
    gap = col_ref[:, 2 * heads + h : 2 * heads + h + 1] - row[h : h + 1, :]
    mask = jnp.where(b <= a, jnp.exp(jnp.minimum(gap, 0.0)), 0.0)
    return (dot(q, k, 1, 1) * mask).astype(BF), mask


def before_norm(core_ref, q_ref, col_ref, ld_ref, other_ref, k_far, v_far, own_far, w_far, in_ref, gn_ref, k_ref, v_ref, own_ref, w_ref, sems):
    heads, span = ld_ref.shape
    copies = fetch((k_far, v_far, own_far, w_far), (k_ref, v_ref, own_ref, w_ref), sems)
    a, b = grid_of(span)
    row = dot(ld_ref[...], (a <= b).astype(F32), precision=EXACT)
    copies[0].wait()
    copies[1].wait()
    for h in range(heads):
        cols = head_cols(h)
        probs, _ = masked_probs(h, heads, q_ref[:, cols], k_ref[:, cols], col_ref, row, a, b)
        in_ref[:, cols] = dot(probs, v_ref[:, cols])
    width = own_ref.shape[1]
    mine = pl.multiple_of(core_ref[0] * width, width)
    theirs = pl.multiple_of((1 - core_ref[0]) * width, width)
    for copy in copies[2:]:
        copy.wait()
    gn_ref[...] = dot(own_ref[...], w_ref[:, pl.ds(mine, width)], 1, 1) + dot(
        other_ref[...], w_ref[:, pl.ds(theirs, width)], 1, 1
    )


def forward_scan(x_ref, y_ref, reach_ref, x32_ref, y32_ref):
    count = reach_ref.shape[1]
    six = x_ref.shape[0] // count
    x32_ref[...] = x_ref[...].astype(F32)
    i, j = grid_of(count)
    before = (j < i).astype(BF)
    gap = jnp.zeros((count, count), F32)
    ends = x32_ref[pl.ds(OWN, count, stride=six)]
    for piece in range(3):
        gap = gap + dot(before, jnp.where(j < i, ends[:, piece : piece + 1], 0.0).astype(BF))
    reach = jnp.where(j < i, jnp.exp(jnp.minimum(gap, 0.0)), 0.0)
    high = reach.astype(BF)
    low = (reach - high.astype(F32)).astype(BF)
    reach_ref[:count] = high
    reach_ref[count:] = low
    for r in range(OWN):
        x = x32_ref[pl.ds(r, count, stride=six)].astype(BF)
        y32_ref[pl.ds(r, count, stride=OWN)] = dot(high, x) + dot(low, x)
    y_ref[...] = y32_ref[...].astype(BF)


def backward_scan(x_ref, reach_ref, y_ref, x32_ref, y32_ref):
    count = reach_ref.shape[1]
    x32_ref[...] = x_ref[...].astype(F32)
    high, low = reach_ref[:count], reach_ref[count:]
    for r in range(OWN):
        x = x32_ref[pl.ds(r, count, stride=OWN)].astype(BF)
        y32_ref[pl.ds(r, count, stride=OWN)] = dot(high, x, 0, 0) + dot(low, x, 0, 0)
    y_ref[...] = y32_ref[...].astype(BF)


def norm_and_grad(q_ref, s_ref, col_ref, in_ref, gn_ref, normed_ref, g_ref, pay_ref):
    heads = in_ref.shape[1] // W
    for h in range(heads):
        cols = head_cols(h)
        growth = col_ref[:, h : h + 1]
        q = q_ref[:, cols]
        att = in_ref[:, cols] + growth * dot(q, s_ref[head_rows(h)])
        inv = lax.rsqrt(jnp.mean(att * att, axis=1, keepdims=True) + EPS)
        normed_ref[:, cols] = (att * inv).astype(BF)
        gn = gn_ref[:, cols]
        g = inv * gn - att * (inv * inv * inv * jnp.mean(gn * att, axis=1, keepdims=True))
        g = g.astype(BF)
        g_ref[:, cols] = g
        pay_ref[head_rows(h)] = dot((q.astype(F32) * growth).astype(BF), g, 0, 0).astype(BF)


def mix(core_ref, normed_ref, other_ref, w_far, w_other_far, out_ref, w_ref, w_other_ref, sems):
    width = out_ref.shape[1]
    mine = pl.multiple_of(core_ref[0] * width, width)
    copies = fetch(
        (w_far.at[:, pl.ds(mine, width)], w_other_far.at[:, pl.ds(mine, width)]),
        (w_ref.at[:, pl.ds(0, width)], w_other_ref.at[:, pl.ds(0, width)]),
        sems,
    )
    copies[0].wait()
    copies[1].wait()
    out_ref[...] = (
        dot(normed_ref[...], w_ref[:, :width]) + dot(other_ref[...], w_other_ref[:, :width])
    ).astype(BF)


def after_norm(g_ref, s_ref, col_ref, ld_ref, q_far, k_far, v_far, gq_ref, gk_ref, gv_ref, q_ref, k_ref, v_ref, sems):
    heads, span = ld_ref.shape
    copies = fetch((q_far, k_far, v_far), (q_ref, k_ref, v_ref), sems)
    a, b = grid_of(span)
    row = dot(ld_ref[...], (a <= b).astype(F32), precision=EXACT)
    for copy in copies:
        copy.wait()
    for h in range(heads):
        cols = head_cols(h)
        q, k, g = q_ref[:, cols], k_ref[:, cols], g_ref[:, cols]
        probs, mask = masked_probs(h, heads, q, k, col_ref, row, a, b)
        d = (dot(g, v_ref[:, cols], 1, 1) * mask).astype(BF)
        carried = dot(g, s_ref[head_rows(h)], 1, 1)
        gq_ref[:, cols] = (dot(d, k) + col_ref[:, h : h + 1] * carried).astype(BF)
        gk_ref[:, cols] = dot(d, q, 0, 0)
        gv_ref[:, cols] = dot(probs, g, 0, 0)


def finish(k_ref, v_ref, e_ref, col_ref, gkp_ref, gvp_ref, gk_ref, gv_ref):
    heads = gk_ref.shape[1] // W
    for h in range(heads):
        cols = head_cols(h)
        weight = col_ref[:, heads + h : heads + h + 1]
        e = e_ref[head_rows(h)]
        gk_ref[:, cols] = (gkp_ref[:, cols] + weight * dot(v_ref[:, cols], e, 1, 1)).astype(BF)
        gv_ref[:, cols] = (gvp_ref[:, cols] + weight * dot(k_ref[:, cols], e)).astype(BF)


def local(queries, keys, values, log_decay, out_weight, out_grad):
    rows, width = queries.shape
    heads, span = log_decay.shape
    count = lax.axis_size("ctx")
    lines = heads * W
    assert lines == OWN * count and rows == span and span >= W
    model = out_weight.shape[1]
    core = lax.axis_index("head").astype(jnp.int32).reshape(1)
    swap = [(0, 1), (1, 0)]
    exchange = count * (OWN + 2)

    pay, col = call(
        block_delta, [near(exchange, W), near(rows, W, dtype=F32)], keys, values, log_decay,
        flops=rows * width * W * 2, far=(0, 1, 2), scratch=[((lines, W), F32), ((exchange, W), F32)],
    )
    got = lax.all_to_all(pay.reshape(-1, 2, W), "ctx", 0, 0, tiled=True).reshape(-1, W)
    other_grad = lax.ppermute(out_grad, "head", swap)
    other_weight = lax.ppermute(out_weight, "head", swap)
    within, grad_norm = call(
        before_norm, [near(rows, width, dtype=F32), near(rows, width, dtype=F32)],
        core, queries, col, log_decay, other_grad, keys, values, out_grad, out_weight,
        flops=rows * width * (span * 4 + model * 2), smem=1, far=(5, 6, 7, 8),
    )
    sent, reach = call(
        forward_scan, [near(lines, W), near(2 * count, count)], got,
        flops=4 * count * lines * W, scratch=[((exchange, W), F32), ((lines, W), F32)],
    )
    state = lax.all_to_all(sent, "ctx", 0, 0, tiled=True)
    normed, grad_att, pay = call(
        norm_and_grad, [shape(rows, width), near(rows, width), near(lines, W)],
        queries, state, col, within, grad_norm, flops=rows * width * W * 4,
    )
    got = lax.all_to_all(pay, "ctx", 0, 0, tiled=True)
    other_normed = lax.ppermute(normed, "head", swap)
    grad_q, gk_part, gv_part = call(
        after_norm,
        [shape(rows, width), near(rows, width, dtype=F32), near(rows, width, dtype=F32)],
        grad_att, state, col, log_decay, queries, keys, values, flops=rows * width * span * 9, far=(4, 5, 6),
    )
    (sent,) = call(
        backward_scan, [near(lines, W)], got, reach, flops=4 * count * lines * W,
        scratch=[((lines, W), F32), ((lines, W), F32)],
    )
    leaving = lax.all_to_all(sent, "ctx", 0, 0, tiled=True)
    (mixed,) = call(
        mix, [shape(rows, model // 2)], core, normed, other_normed, out_weight, other_weight,
        flops=2 * rows * width * model, smem=1, far=(3, 4),
    )
    mixed, gk_part = lax.optimization_barrier((mixed, gk_part))
    grad_k, grad_v = call(
        finish, [shape(rows, width), shape(rows, width)], keys, values, leaving, col, gk_part, gv_part,
        flops=rows * width * W * 4,
    )
    return mixed, grad_q, grad_k, grad_v


def solution(mesh):
    split = P("ctx", "head")
    return jax.shard_map(
        local,
        mesh=mesh,
        in_specs=(split, split, split, P("head", "ctx"), P("head", None), split),
        out_specs=(split,) * 4,
        check_vma=False,
    )
```

time: 108 us -> 92.5 us (0.86)
  local copies, waits for them, and re-layouts: 19.7 us -> 1.65 us
  waiting for transfers between devices: 28.5 us -> 36.8 us
  starting transfers between devices: 43.7 us -> 36.3 us
  Pallas kernels: 12.1 us -> 16.5 us
  other arithmetic: 1.98 us -> 0 us
    unnamed x62 -> x12, local copies, waits for them, and re-layouts: 19.7 us -> 1.65 us
    all_to_all x1, waiting for transfers between devices: 4.86 us -> 11.5 us  [local(): got = lax.all_to_all(pay, 'ctx', 0, 0, tiled=True)]
    all_to_all x1, starting transfers between devices: 12.3 us -> 6.77 us  [local(): got = lax.all_to_all(pay, 'ctx', 0, 0, tiled=True)]
    all_to_all x1, waiting for transfers between devices: 1.76 us -> 7.14 us  [local(): state = lax.all_to_all(sent, 'ctx', 0, 0, tiled=True)]
    all_to_all x1, waiting for transfers between devices: 9.48 us -> 5.03 us  [local(): leaving = lax.all_to_all(sent, 'ctx', 0, 0, tiled=True)]
    pallas_call x9 -> x8, Pallas kernels: 12.1 us -> 16.5 us  [call(): pl.pallas_call(body, out_shape=outs, in_specs=[spec(i) for i in range(len...]
    all_to_all x1, starting transfers between devices: 8.94 us -> 6.86 us  [local(): leaving = lax.all_to_all(sent, 'ctx', 0, 0, tiled=True)]
    convert_element_type x1 -> x0, other arithmetic: 1.98 us -> none  [local(): mixed = (own + theirs.astype(F32)).astype(BF)]
  transfers between devices with their start and end apart: 6 -> 7, of which waited for: 4 -> 4; matrix products, arithmetic and copies ran while one was open for 2% -> 0% of each run, Pallas kernels for 6% -> 17%
where the time goes in v3:
time: 92.5 us; the launch traced here: 92.1 us
  waiting for transfers between devices  36.8 us (40%)
  starting transfers between devices  36.3 us (39%)
  Pallas kernels  16.5 us (18%)
  local copies, waits for them, and re-layouts  1.65 us (2%)
    pallas_call x8, Pallas kernels, call(): pl.pallas_call(body, out_shape=outs, in_specs=[spec(i) for i in range(len...  16.5 us
    all_to_all x1, starting transfers between devices, local(): lax.all_to_all(pay.reshape(-1, 2, W), 'ctx', 0, 0, tiled=True)  15.4 us
    all_to_all x1, waiting for transfers between devices, local(): lax.all_to_all(pay.reshape(-1, 2, W), 'ctx', 0, 0, tiled=True)  13.1 us
    all_to_all x1, waiting for transfers between devices, local(): got = lax.all_to_all(pay, 'ctx', 0, 0, tiled=True)  11.5 us
    all_to_all x1, waiting for transfers between devices, local(): state = lax.all_to_all(sent, 'ctx', 0, 0, tiled=True)  7.14 us
    all_to_all x1, starting transfers between devices, local(): state = lax.all_to_all(sent, 'ctx', 0, 0, tiled=True)  6.98 us
    all_to_all x1, starting transfers between devices, local(): leaving = lax.all_to_all(sent, 'ctx', 0, 0, tiled=True)  6.86 us
    all_to_all x1, starting transfers between devices, local(): got = lax.all_to_all(pay, 'ctx', 0, 0, tiled=True)  6.77 us
  transfers between devices with their start and end apart: 7, of which 4 were waited for; matrix products, arithmetic and copies ran while one was open for 0% of the time, Pallas kernels for 17%

profile of v3, /device:TPU:2, one launch (start us, length us, event | category | flops | bytes accessed | tf_op | source)
XLA Modules:
  0.0 92.1 jit_solution(1939651096666972818)
XLA Ops:
  0.6 0.1 collective-permute-start.2
  0.7 2.6 %block_delta.1 = (bf16[768,128]{1,0:T(8,128)(2,1)}, f32[256,128]{1,0:T(8,128)S(1)}) custom-call(bf16[256,512]{1,0:T(8,128)(2,1)} %k_ref.1, bf16[256,512]{1,0:T(8,128)(2,1)} %v_ref.1, f32[4,256]{1,0:T(4,128)} %ld_ref.3), custom_call_target="tpu_custom_call" | custom-call | flops 33554432 | bytes 856064 | tf_op jit(solution)/shard_map/block_delta/pallas_call | solution.py:36
  3.4 15.4 %all-to-all-start = ((bf16[384,2,128]{2,1,0:T(2,128)(2,1)}), bf16[384,2,128]{2,1,0:T(2,128)(2,1)S(1)}, u32[]{:S(2)}, u32[]{:S(2)}) async-start(bf16[384,2,128]{2,1,0:T(2,128)(2,1)} %bitcast.1), calls=%async_computation | async-start | bytes 393216 | tf_op jit(solution)/shard_map/all_to_all | solution.py:238
  18.8 0.1 collective-permute-start
  18.9 13.1 %all-to-all-done = bf16[384,2,128]{2,1,0:T(2,128)(2,1)S(1)} async-done(((bf16[384,2,128]{2,1,0:T(2,128)(2,1)}), bf16[384,2,128]{2,1,0:T(2,128)(2,1)S(1)}, u32[]{:S(2)}, u32[]{:S(2)}) %all-to-all-start) | async-done | bytes 196640 | tf_op jit(solution)/shard_map/all_to_all | solution.py:238
  32.0 1.2 %forward_scan.1 = (bf16[512,128]{1,0:T(8,128)(2,1)}, bf16[256,128]{1,0:T(8,128)(2,1)S(1)}) custom-call(bf16[768,128]{1,0:T(8,128)(2,1)S(1)} %bitcast.11), custom_call_target="tpu_custom_call" | custom-call | flops 33554432 | bytes 393216 | tf_op jit(solution)/shard_map/forward_scan/pallas_call | solution.py:36
  33.2 7.0 %all-to-all-start.1 = ((bf16[128,4,128]{2,1,0:T(4,128)(2,1)}), bf16[128,4,128]{2,1,0:T(4,128)(2,1)S(1)}, u32[]{:S(2)}, u32[]{:S(2)}) async-start(bf16[128,4,128]{2,1,0:T(4,128)(2,1)} %bitcast.3), calls=%async_computation.1 | async-start | bytes 262144 | tf_op jit(solution)/shard_map/all_to_all | solution.py:250
  40.2 0.0 copy-start.2
  40.2 0.9 %copy-done.2 = bf16[256,512]{1,0:T(8,128)(2,1)S(1)} copy-done((bf16[256,512]{1,0:T(8,128)(2,1)S(1)}, bf16[256,512]{1,0:T(8,128)(2,1)}, u32[]{:S(2)}) %copy-start.2) | copy-done | bytes 262168
  41.2 0.7 copy-done.4
  41.8 2.7 %before_norm.1 = (f32[256,512]{1,0:T(8,128)S(1)}, f32[256,512]{1,0:T(8,128)S(1)}) custom-call(s32[1]{0:T(128)} %bitcast.core_ref, bf16[256,512]{1,0:T(8,128)(2,1)S(1)} %copy-done.2, f32[256,128]{1,0:T(8,128)S(1)} %get-tuple-element.22.col_ref, f32[4,256]{1,0:T(4,128)S(1)} %copy-done.4, bf16[256,1024]{1,0:T(8,128)(2,1)S(1)} %collective-permute-done.other_ref, ...), custom_call_target="tpu_custom_call" | custom-call | flops 671088640 | bytes 5115908 | tf_op jit(solution)/shard_map/before_norm/pallas_call | solution.py:36
  44.6 7.1 %all-to-all-done.1 = bf16[128,4,128]{2,1,0:T(4,128)(2,1)S(1)} async-done(((bf16[128,4,128]{2,1,0:T(4,128)(2,1)}), bf16[128,4,128]{2,1,0:T(4,128)(2,1)S(1)}, u32[]{:S(2)}, u32[]{:S(2)}) %all-to-all-start.1) | async-done | bytes 131104 | tf_op jit(solution)/shard_map/all_to_all | solution.py:250
  51.7 1.6 %norm_and_grad.1 = (bf16[256,512]{1,0:T(8,128)(2,1)S(1)}, bf16[256,512]{1,0:T(8,128)(2,1)S(1)}, bf16[512,128]{1,0:T(8,128)(2,1)}) custom-call(bf16[256,512]{1,0:T(8,128)(2,1)S(1)} %copy-done.3, bf16[512,128]{1,0:T(8,128)(2,1)S(1)} %bitcast.9, f32[256,128]{1,0:T(8,128)S(1)} %get-tuple-element.22.col_ref, f32[256,512]{1,0:T(8,128)S(1)} %get-tuple-element.23.in_ref, ...), custom_call_target="tpu_custom_call" | custom-call | flops 67108864 | bytes 2228224 | tf_op jit(solution)/shard_map/norm_and_grad/pallas_call | solution.py:36
  53.3 6.8 %all-to-all-start.2 = ((bf16[128,4,128]{2,1,0:T(4,128)(2,1)}), bf16[128,4,128]{2,1,0:T(4,128)(2,1)S(1)}, u32[]{:S(2)}, u32[]{:S(2)}) async-start(bf16[128,4,128]{2,1,0:T(4,128)(2,1)} %bitcast.5), calls=%async_computation.2 | async-start | bytes 262144 | tf_op jit(solution)/shard_map/all_to_all | solution.py:255
  60.1 0.1 collective-permute-start.1
  60.2 11.5 %all-to-all-done.2 = bf16[128,4,128]{2,1,0:T(4,128)(2,1)S(1)} async-done(((bf16[128,4,128]{2,1,0:T(4,128)(2,1)}), bf16[128,4,128]{2,1,0:T(4,128)(2,1)S(1)}, u32[]{:S(2)}, u32[]{:S(2)}) %all-to-all-start.2) | async-done | bytes 131104 | tf_op jit(solution)/shard_map/all_to_all | solution.py:255
  71.6 0.9 %backward_scan.1 = bf16[512,128]{1,0:T(8,128)(2,1)} custom-call(bf16[512,128]{1,0:T(8,128)(2,1)S(1)} %bitcast.13, bf16[256,128]{1,0:T(8,128)(2,1)S(1)} %get-tuple-element.31.reach_ref), custom_call_target="tpu_custom_call" | custom-call | flops 33554432 | bytes 327680 | tf_op jit(solution)/shard_map/backward_scan/pallas_call | solution.py:36
  72.6 6.9 %all-to-all-start.3 = ((bf16[128,4,128]{2,1,0:T(4,128)(2,1)}), bf16[128,4,128]{2,1,0:T(4,128)(2,1)S(1)}, u32[]{:S(2)}, u32[]{:S(2)}) async-start(bf16[128,4,128]{2,1,0:T(4,128)(2,1)} %bitcast.7), calls=%async_computation.3 | async-start | bytes 262144 | tf_op jit(solution)/shard_map/all_to_all | solution.py:266
  79.4 3.4 %after_norm.1 = (bf16[256,512]{1,0:T(8,128)(2,1)}, f32[256,512]{1,0:T(8,128)S(1)}, f32[256,512]{1,0:T(8,128)S(1)}) custom-call(bf16[256,512]{1,0:T(8,128)(2,1)S(1)} %get-tuple-element.26.g_ref, bf16[512,128]{1,0:T(8,128)(2,1)S(1)} %bitcast.10, f32[256,128]{1,0:T(8,128)S(1)} %get-tuple-element.22.col_ref, f32[4,256]{1,0:T(4,128)S(1)} %copy-done.5, ...), custom_call_target="tpu_custom_call" | custom-call | flops 301989888 | bytes 2625536 | tf_op jit(solution)/shard_map/after_norm/pallas_call | solution.py:36
  82.8 0.0 copy-start
  82.8 0.0 copy-start.1
  82.9 3.1 %mix.1 = bf16[256,1024]{1,0:T(8,128)(2,1)} custom-call(s32[1]{0:T(128)} %bitcast.core_ref, bf16[256,512]{1,0:T(8,128)(2,1)S(1)} %get-tuple-element.25.normed_ref, bf16[256,512]{1,0:T(8,128)(2,1)S(1)} %collective-permute-done.1.other_ref, bf16[512,2048]{1,0:T(8,128)(2,1)} %w_far.3, bf16[512,2048]{1,0:T(8,128)(2,1)} %collective-permute-done.2.w_other_far), custom_call_target="tpu_custom_call" | custom-call | flops 536870912 | bytes 5242884 | tf_op jit(solution)/shard_map/mix/pallas_call | solution.py:36
  86.0 5.0 %all-to-all-done.3 = bf16[128,4,128]{2,1,0:T(4,128)(2,1)S(1)} async-done(((bf16[128,4,128]{2,1,0:T(4,128)(2,1)}), bf16[128,4,128]{2,1,0:T(4,128)(2,1)S(1)}, u32[]{:S(2)}, u32[]{:S(2)}) %all-to-all-start.3) | async-done | bytes 131104 | tf_op jit(solution)/shard_map/all_to_all | solution.py:266
  91.0 1.1 %finish.1 = (bf16[256,512]{1,0:T(8,128)(2,1)}, bf16[256,512]{1,0:T(8,128)(2,1)}) custom-call(bf16[256,512]{1,0:T(8,128)(2,1)S(1)} %copy-done, bf16[256,512]{1,0:T(8,128)(2,1)S(1)} %copy-done.1, bf16[512,128]{1,0:T(8,128)(2,1)S(1)} %bitcast.12, f32[256,128]{1,0:T(8,128)S(1)} %get-tuple-element.22.col_ref, f32[256,512]{1,0:T(8,128)S(1)} %get-tuple-element.32.gkp_ref, ...), custom_call_target="tpu_custom_call" | custom-call | flops 67108864 | bytes 2359296 | tf_op jit(solution)/shard_map/finish/pallas_call | solution.py:36
  (10 shorter events, 0.0 us)
Async XLA Ops:
  0.6 82.2 %collective-permute-start.2 = (bf16[512,2048]{1,0:T(8,128)(2,1)}, bf16[512,2048]{1,0:T(8,128)(2,1)}, u32[]{:S(2)}, u32[]{:S(2)}) collective-permute-start(bf16[512,2048]{1,0:T(8,128)(2,1)} %w_far.3), channel_id=1, source_target_pairs={{0,1},{1,0},{2,3},{3,2},{4,5},{5,4},{6,7},{7,6},{8,9},{9,8},{10,11... | collective-permute-start | bytes 6291464 | tf_op jit(solution)/shard_map/ppermute | solution.py:240
  3.4 28.7 %all-to-all-start = ((bf16[384,2,128]{2,1,0:T(2,128)(2,1)}), bf16[384,2,128]{2,1,0:T(2,128)(2,1)S(1)}, u32[]{:S(2)}, u32[]{:S(2)}) async-start(bf16[384,2,128]{2,1,0:T(2,128)(2,1)} %bitcast.1), calls=%async_computation | async-start | bytes 393216 | tf_op jit(solution)/shard_map/all_to_all | solution.py:238
  18.8 21.4 %collective-permute-start = (bf16[256,1024]{1,0:T(8,128)(2,1)}, bf16[256,1024]{1,0:T(8,128)(2,1)S(1)}, u32[]{:S(2)}, u32[]{:S(2)}) collective-permute-start(bf16[256,1024]{1,0:T(8,128)(2,1)} %own_far.1), channel_id=1, source_target_pairs={{0,1},{1,0},{2,3},{3,2},{4,5},{5,4},{6,7},{7,6},{8,9},{9,8},{10,11... | collective-permute-start | bytes 1572872 | tf_op jit(solution)/shard_map/ppermute | solution.py:239
  33.2 18.5 %copy-start.3 = (bf16[256,512]{1,0:T(8,128)(2,1)S(1)}, bf16[256,512]{1,0:T(8,128)(2,1)}, u32[]{:S(2)}) copy-start(bf16[256,512]{1,0:T(8,128)(2,1)} %q_far.1) | copy-start | bytes 786436
  33.2 18.5 %all-to-all-start.1 = ((bf16[128,4,128]{2,1,0:T(4,128)(2,1)}), bf16[128,4,128]{2,1,0:T(4,128)(2,1)S(1)}, u32[]{:S(2)}, u32[]{:S(2)}) async-start(bf16[128,4,128]{2,1,0:T(4,128)(2,1)} %bitcast.3), calls=%async_computation.1 | async-start | bytes 262144 | tf_op jit(solution)/shard_map/all_to_all | solution.py:250
  40.2 1.0 %copy-start.2 = (bf16[256,512]{1,0:T(8,128)(2,1)S(1)}, bf16[256,512]{1,0:T(8,128)(2,1)}, u32[]{:S(2)}) copy-start(bf16[256,512]{1,0:T(8,128)(2,1)} %q_far.1) | copy-start | bytes 786436
  41.2 0.7 copy-start.4
  44.6 34.9 %copy-start.5 = (f32[4,256]{1,0:T(4,128)S(1)}, f32[4,256]{1,0:T(4,128)}, u32[]{:S(2)}) copy-start(f32[4,256]{1,0:T(4,128)} %ld_ref.3) | copy-start | bytes 12292
  53.3 18.3 %all-to-all-start.2 = ((bf16[128,4,128]{2,1,0:T(4,128)(2,1)}), bf16[128,4,128]{2,1,0:T(4,128)(2,1)S(1)}, u32[]{:S(2)}, u32[]{:S(2)}) async-start(bf16[128,4,128]{2,1,0:T(4,128)(2,1)} %bitcast.5), calls=%async_computation.2 | async-start | bytes 262144 | tf_op jit(solution)/shard_map/all_to_all | solution.py:255
  60.1 22.8 %collective-permute-start.1 = (bf16[256,512]{1,0:T(8,128)(2,1)S(1)}, bf16[256,512]{1,0:T(8,128)(2,1)S(1)}, u32[]{:S(2)}, u32[]{:S(2)}) collective-permute-start(bf16[256,512]{1,0:T(8,128)(2,1)S(1)} %get-tuple-element.25.normed_ref), channel_id=1, source_target_pairs={{0,1},{1,0},{2,3},{3,2},{4,5},{5,4},{6,7},{7,6},{8,9},{9,8},{10,11... | collective-permute-start | bytes 786440 | tf_op jit(solution)/shard_map/ppermute | solution.py:256
  72.6 18.4 %all-to-all-start.3 = ((bf16[128,4,128]{2,1,0:T(4,128)(2,1)}), bf16[128,4,128]{2,1,0:T(4,128)(2,1)S(1)}, u32[]{:S(2)}, u32[]{:S(2)}) async-start(bf16[128,4,128]{2,1,0:T(4,128)(2,1)} %bitcast.7), calls=%async_computation.3 | async-start | bytes 262144 | tf_op jit(solution)/shard_map/all_to_all | solution.py:266
  82.8 8.2 %copy-start = (bf16[256,512]{1,0:T(8,128)(2,1)S(1)}, bf16[256,512]{1,0:T(8,128)(2,1)}, u32[]{:S(2)}) copy-start(bf16[256,512]{1,0:T(8,128)(2,1)} %k_ref.1) | copy-start | bytes 786436
  82.8 8.2 %copy-start.1 = (bf16[256,512]{1,0:T(8,128)(2,1)S(1)}, bf16[256,512]{1,0:T(8,128)(2,1)}, u32[]{:S(2)}) copy-start(bf16[256,512]{1,0:T(8,128)(2,1)} %v_ref.1) | copy-start | bytes 786436

commit v4 on v3

--- a/solution.py
+++ b/solution.py
@@ -109,13 +109,14 @@
     return (dot(q, k, 1, 1) * mask).astype(BF), mask
 
 
-def before_norm(core_ref, q_ref, col_ref, ld_ref, other_ref, k_far, v_far, own_far, w_far, in_ref, gn_ref, k_ref, v_ref, own_ref, w_ref, sems):
+def before_norm(core_ref, col_ref, other_ref, ld_far, q_far, k_far, v_far, own_far, w_far, in_ref, gn_ref, ld_ref, q_ref, k_ref, v_ref, own_ref, w_ref, sems):
     heads, span = ld_ref.shape
-    copies = fetch((k_far, v_far, own_far, w_far), (k_ref, v_ref, own_ref, w_ref), sems)
+    copies = fetch((ld_far, q_far, k_far, v_far, own_far, w_far), (ld_ref, q_ref, k_ref, v_ref, own_ref, w_ref), sems)
     a, b = grid_of(span)
+    copies[0].wait()
     row = dot(ld_ref[...], (a <= b).astype(F32), precision=EXACT)
-    copies[0].wait()
-    copies[1].wait()
+    for copy in copies[1:4]:
+        copy.wait()
     for h in range(heads):
         cols = head_cols(h)
         probs, _ = masked_probs(h, heads, q_ref[:, cols], k_ref[:, cols], col_ref, row, a, b)
@@ -123,7 +124,7 @@
     width = own_ref.shape[1]
     mine = pl.multiple_of(core_ref[0] * width, width)
     theirs = pl.multiple_of((1 - core_ref[0]) * width, width)
-    for copy in copies[2:]:
+    for copy in copies[4:]:
         copy.wait()
     gn_ref[...] = dot(own_ref[...], w_ref[:, pl.ds(mine, width)], 1, 1) + dot(
         other_ref[...], w_ref[:, pl.ds(theirs, width)], 1, 1
@@ -192,12 +193,13 @@
     ).astype(BF)
 
 
-def after_norm(g_ref, s_ref, col_ref, ld_ref, q_far, k_far, v_far, gq_ref, gk_ref, gv_ref, q_ref, k_ref, v_ref, sems):
+def after_norm(g_ref, s_ref, col_ref, ld_far, q_far, k_far, v_far, gq_ref, gk_ref, gv_ref, ld_ref, q_ref, k_ref, v_ref, sems):
     heads, span = ld_ref.shape
-    copies = fetch((q_far, k_far, v_far), (q_ref, k_ref, v_ref), sems)
+    copies = fetch((ld_far, q_far, k_far, v_far), (ld_ref, q_ref, k_ref, v_ref), sems)
     a, b = grid_of(span)
+    copies[0].wait()
     row = dot(ld_ref[...], (a <= b).astype(F32), precision=EXACT)
-    for copy in copies:
+    for copy in copies[1:]:
         copy.wait()
     for h in range(heads):
         cols = head_cols(h)
@@ -235,35 +237,39 @@
         block_delta, [near(exchange, W), near(rows, W, dtype=F32)], keys, values, log_decay,
         flops=rows * width * W * 2, far=(0, 1, 2), scratch=[((lines, W), F32), ((exchange, W), F32)],
     )
+    other_grad = lax.ppermute(out_grad, "head", swap)
+    pay, other_grad = lax.optimization_barrier((pay, other_grad))
     got = lax.all_to_all(pay.reshape(-1, 2, W), "ctx", 0, 0, tiled=True).reshape(-1, W)
-    other_grad = lax.ppermute(out_grad, "head", swap)
-    other_weight = lax.ppermute(out_weight, "head", swap)
-    within, grad_norm = call(
-        before_norm, [near(rows, width, dtype=F32), near(rows, width, dtype=F32)],
-        core, queries, col, log_decay, other_grad, keys, values, out_grad, out_weight,
-        flops=rows * width * (span * 4 + model * 2), smem=1, far=(5, 6, 7, 8),
-    )
+    got, col = lax.optimization_barrier((got, col))
     sent, reach = call(
         forward_scan, [near(lines, W), near(2 * count, count)], got,
         flops=4 * count * lines * W, scratch=[((exchange, W), F32), ((lines, W), F32)],
     )
+    sent, weight_out = lax.optimization_barrier((sent, out_weight))
+    other_weight = lax.ppermute(weight_out, "head", swap)
     state = lax.all_to_all(sent, "ctx", 0, 0, tiled=True)
+    within, grad_norm = call(
+        before_norm, [near(rows, width, dtype=F32), near(rows, width, dtype=F32)],
+        core, col, other_grad, log_decay, queries, keys, values, out_grad, out_weight,
+        flops=rows * width * (span * 4 + model * 2), smem=1, far=(3, 4, 5, 6, 7, 8),
+    )
     normed, grad_att, pay = call(
-        norm_and_grad, [shape(rows, width), near(rows, width), near(lines, W)],
+        norm_and_grad, [near(rows, width), near(rows, width), near(lines, W)],
         queries, state, col, within, grad_norm, flops=rows * width * W * 4,
     )
     got = lax.all_to_all(pay, "ctx", 0, 0, tiled=True)
+    got, normed, grad_att = lax.optimization_barrier((got, normed, grad_att))
     other_normed = lax.ppermute(normed, "head", swap)
+    (sent,) = call(
+        backward_scan, [near(lines, W)], got, reach, flops=4 * count * lines * W,
+        scratch=[((lines, W), F32), ((lines, W), F32)],
+    )
+    leaving = lax.all_to_all(sent, "ctx", 0, 0, tiled=True)
     grad_q, gk_part, gv_part = call(
         after_norm,
         [shape(rows, width), near(rows, width, dtype=F32), near(rows, width, dtype=F32)],
-        grad_att, state, col, log_decay, queries, keys, values, flops=rows * width * span * 9, far=(4, 5, 6),
-    )
-    (sent,) = call(
-        backward_scan, [near(lines, W)], got, reach, flops=4 * count * lines * W,
-        scratch=[((lines, W), F32), ((lines, W), F32)],
-    )
-    leaving = lax.all_to_all(sent, "ctx", 0, 0, tiled=True)
+        grad_att, state, col, log_decay, queries, keys, values, flops=rows * width * span * 9, far=(3, 4, 5, 6),
+    )
     (mixed,) = call(
         mix, [shape(rows, model // 2)], core, normed, other_normed, out_weight, other_weight,
         flops=2 * rows * width * model, smem=1, far=(3, 4),

time: 92.5 us -> 93.1 us (level)
  blocking collectives: 0 us -> 46.3 us
  starting transfers between devices: 36.3 us -> 13.8 us
  waiting for transfers between devices: 36.8 us -> 15.5 us
  local copies, waits for them, and re-layouts: 1.65 us -> 0.02 us
  Pallas kernels: 16.5 us -> 15.4 us
    all_to_all x0 -> x2, blocking collectives: none -> 46.3 us  [the longest x1 28.3 us: local(): lax.all_to_all(pay.reshape(-1, 2, W), 'ctx', 0, 0, tiled=True)]
    all_to_all x2 -> x0, waiting for transfers between devices: 24.6 us -> none  [the longest x1 13.1 us: local(): lax.all_to_all(pay.reshape(-1, 2, W), 'ctx', 0, 0, tiled=True)]
    all_to_all x2 -> x0, starting transfers between devices: 22.2 us -> none  [the longest x1 15.4 us: local(): lax.all_to_all(pay.reshape(-1, 2, W), 'ctx', 0, 0, tiled=True)]
    all_to_all x1, waiting for transfers between devices: 7.14 us -> 9.49 us  [local(): state = lax.all_to_all(sent, 'ctx', 0, 0, tiled=True)]
    unnamed x12 -> x6, local copies, waits for them, and re-layouts: 1.65 us -> 0.02 us
    pallas_call x8, Pallas kernels: 16.5 us -> 15.4 us  [call(): pl.pallas_call(body, out_shape=outs, in_specs=[spec(i) for i in range(len...]
  transfers between devices with their start and end apart: 7 -> 5, of which waited for: 4 -> 3; matrix products, arithmetic and copies ran while one was open for 0% -> 0% of each run, Pallas kernels for 17% -> 14%
where the time goes in v4:
time: 93.1 us; the launch traced here: 91.8 us
  blocking collectives  46.3 us (50%)
  waiting for transfers between devices  15.5 us (17%)
  Pallas kernels  15.4 us (17%)
  starting transfers between devices  13.8 us (15%)
    all_to_all x1, blocking collectives, local(): lax.all_to_all(pay.reshape(-1, 2, W), 'ctx', 0, 0, tiled=True)  28.3 us
    all_to_all x1, blocking collectives, local(): got = lax.all_to_all(pay, 'ctx', 0, 0, tiled=True)  18 us
    pallas_call x8, Pallas kernels, call(): pl.pallas_call(body, out_shape=outs, in_specs=[spec(i) for i in range(len...  15.4 us
    all_to_all x1, waiting for transfers between devices, local(): state = lax.all_to_all(sent, 'ctx', 0, 0, tiled=True)  9.49 us
    all_to_all x1, starting transfers between devices, local(): leaving = lax.all_to_all(sent, 'ctx', 0, 0, tiled=True)  6.86 us
    all_to_all x1, starting transfers between devices, local(): state = lax.all_to_all(sent, 'ctx', 0, 0, tiled=True)  6.83 us
    all_to_all x1, waiting for transfers between devices, local(): leaving = lax.all_to_all(sent, 'ctx', 0, 0, tiled=True)  5.87 us
  transfers between devices with their start and end apart: 5, of which 3 were waited for; matrix products, arithmetic and copies ran while one was open for 0% of the time, Pallas kernels for 14%

profile of v4, /device:TPU:2, one launch (start us, length us, event | category | flops | bytes accessed | tf_op | source)
XLA Modules:
  0.0 91.8 jit_solution(1447289765962033219)
XLA Ops:
  0.6 0.1 collective-permute-start
  0.7 1.9 %block_delta.1 = (bf16[768,128]{1,0:T(8,128)(2,1)S(1)}, f32[256,128]{1,0:T(8,128)S(1)}) custom-call(bf16[256,512]{1,0:T(8,128)(2,1)} %k_ref.1, bf16[256,512]{1,0:T(8,128)(2,1)} %v_ref.1, f32[4,256]{1,0:T(4,128)} %ld_far.5), custom_call_target="tpu_custom_call" | custom-call | flops 33554432 | bytes 856064 | tf_op jit(solution)/shard_map/block_delta/pallas_call | solution.py:36
  2.7 0.2 collective-permute-done.other_ref
  2.8 28.3 %all_to_all.39 = bf16[384,2,128]{2,1,0:T(2,128)(2,1)S(1)} all-to-all(bf16[384,2,128]{2,1,0:T(2,128)(2,1)S(1)} %bitcast.14), channel_id=1, replica_groups=mesh['ctx'=128,'head'=2] {'ctx'}, dimensions={0} | all-to-all | bytes 393216 | tf_op jit(solution)/shard_map/all_to_all | solution.py:242
  31.2 1.2 %forward_scan.1 = (bf16[512,128]{1,0:T(8,128)(2,1)}, bf16[256,128]{1,0:T(8,128)(2,1)S(1)}) custom-call(bf16[768,128]{1,0:T(8,128)(2,1)S(1)} %bitcast.11), custom_call_target="tpu_custom_call" | custom-call | flops 33554432 | bytes 393216 | tf_op jit(solution)/shard_map/forward_scan/pallas_call | solution.py:36
  32.3 0.0 collective-permute-start.2
  32.3 6.8 %all-to-all-start.1 = ((bf16[128,4,128]{2,1,0:T(4,128)(2,1)}), bf16[128,4,128]{2,1,0:T(4,128)(2,1)S(1)}, u32[]{:S(2)}, u32[]{:S(2)}) async-start(bf16[128,4,128]{2,1,0:T(4,128)(2,1)} %bitcast.3), calls=%async_computation.1 | async-start | bytes 262144 | tf_op jit(solution)/shard_map/all_to_all | solution.py:250
  39.2 0.0 copy-start.2
  39.2 2.9 %before_norm.1 = (f32[256,512]{1,0:T(8,128)S(1)}, f32[256,512]{1,0:T(8,128)S(1)}) custom-call(s32[1]{0:T(128)} %bitcast.core_ref, f32[256,128]{1,0:T(8,128)S(1)} %get-tuple-element.35.col_ref, bf16[256,1024]{1,0:T(8,128)(2,1)S(1)} %collective-permute-done.other_ref, f32[4,256]{1,0:T(4,128)} %ld_far.5, bf16[256,512]{1,0:T(8,128)(2,1)} %q_far.3, ...), custom_call_target="tpu_custom_call" | custom-call | flops 671088640 | bytes 5115908 | tf_op jit(solution)/shard_map/before_norm/pallas_call | solution.py:36
  42.1 9.5 %all-to-all-done.1 = bf16[128,4,128]{2,1,0:T(4,128)(2,1)S(1)} async-done(((bf16[128,4,128]{2,1,0:T(4,128)(2,1)}), bf16[128,4,128]{2,1,0:T(4,128)(2,1)S(1)}, u32[]{:S(2)}, u32[]{:S(2)}) %all-to-all-start.1) | async-done | bytes 131104 | tf_op jit(solution)/shard_map/all_to_all | solution.py:250
  51.6 0.9 norm_and_grad.1
  52.5 18.0 %all_to_all.40 = bf16[128,4,128]{2,1,0:T(4,128)(2,1)S(1)} all-to-all(bf16[128,4,128]{2,1,0:T(4,128)(2,1)S(1)} %bitcast.15), channel_id=1, replica_groups=mesh['ctx'=128,'head'=2] {'ctx'}, dimensions={0} | all-to-all | bytes 262144 | tf_op jit(solution)/shard_map/all_to_all | solution.py:260
  70.5 0.0 collective-permute-start.1
  70.5 0.9 %backward_scan.1 = bf16[512,128]{1,0:T(8,128)(2,1)} custom-call(bf16[512,128]{1,0:T(8,128)(2,1)S(1)} %bitcast.13, bf16[256,128]{1,0:T(8,128)(2,1)S(1)} %get-tuple-element.49.reach_ref), custom_call_target="tpu_custom_call" | custom-call | flops 33554432 | bytes 327680 | tf_op jit(solution)/shard_map/backward_scan/pallas_call | solution.py:36
  71.4 6.9 %all-to-all-start.3 = ((bf16[128,4,128]{2,1,0:T(4,128)(2,1)}), bf16[128,4,128]{2,1,0:T(4,128)(2,1)S(1)}, u32[]{:S(2)}, u32[]{:S(2)}) async-start(bf16[128,4,128]{2,1,0:T(4,128)(2,1)} %bitcast.7), calls=%async_computation.3 | async-start | bytes 262144 | tf_op jit(solution)/shard_map/all_to_all | solution.py:267
  78.3 3.4 %after_norm.1 = (bf16[256,512]{1,0:T(8,128)(2,1)}, f32[256,512]{1,0:T(8,128)S(1)}, f32[256,512]{1,0:T(8,128)S(1)}) custom-call(bf16[256,512]{1,0:T(8,128)(2,1)S(1)} %get-tuple-element.44.g_ref, bf16[512,128]{1,0:T(8,128)(2,1)S(1)} %bitcast.10, f32[256,128]{1,0:T(8,128)S(1)} %get-tuple-element.35.col_ref, f32[4,256]{1,0:T(4,128)} %ld_far.5, ...), custom_call_target="tpu_custom_call" | custom-call | flops 301989888 | bytes 2625536 | tf_op jit(solution)/shard_map/after_norm/pallas_call | solution.py:36
  81.7 0.0 copy-start
  81.7 0.0 copy-start.1
  81.7 0.0 collective-permute-done.1.other_ref
  81.7 0.0 collective-permute-done.2.w_other_far
  81.7 3.1 %mix.1 = bf16[256,1024]{1,0:T(8,128)(2,1)} custom-call(s32[1]{0:T(128)} %bitcast.core_ref, bf16[256,512]{1,0:T(8,128)(2,1)S(1)} %get-tuple-element.42.normed_ref, bf16[256,512]{1,0:T(8,128)(2,1)S(1)} %collective-permute-done.1.other_ref, bf16[512,2048]{1,0:T(8,128)(2,1)} %w_far.3, bf16[512,2048]{1,0:T(8,128)(2,1)} %collective-permute-done.2.w_other_far), custom_call_target="tpu_custom_call" | custom-call | flops 536870912 | bytes 5242884 | tf_op jit(solution)/shard_map/mix/pallas_call | solution.py:36
  84.8 5.9 %all-to-all-done.3 = bf16[128,4,128]{2,1,0:T(4,128)(2,1)S(1)} async-done(((bf16[128,4,128]{2,1,0:T(4,128)(2,1)}), bf16[128,4,128]{2,1,0:T(4,128)(2,1)S(1)}, u32[]{:S(2)}, u32[]{:S(2)}) %all-to-all-start.3) | async-done | bytes 131104 | tf_op jit(solution)/shard_map/all_to_all | solution.py:267
  90.7 0.0 copy-done.1
  90.7 1.1 %finish.1 = (bf16[256,512]{1,0:T(8,128)(2,1)}, bf16[256,512]{1,0:T(8,128)(2,1)}) custom-call(bf16[256,512]{1,0:T(8,128)(2,1)S(1)} %copy-done, bf16[256,512]{1,0:T(8,128)(2,1)S(1)} %copy-done.1, bf16[512,128]{1,0:T(8,128)(2,1)S(1)} %bitcast.12, f32[256,128]{1,0:T(8,128)S(1)} %get-tuple-element.35.col_ref, f32[256,512]{1,0:T(8,128)S(1)} %get-tuple-element.50.gkp_ref, ...), custom_call_target="tpu_custom_call" | custom-call | flops 67108864 | bytes 2359296 | tf_op jit(solution)/shard_map/finish/pallas_call | solution.py:36
  (2 shorter events, 0.0 us)
Async XLA Ops:
  0.6 2.2 %collective-permute-start = (bf16[256,1024]{1,0:T(8,128)(2,1)}, bf16[256,1024]{1,0:T(8,128)(2,1)S(1)}, u32[]{:S(2)}, u32[]{:S(2)}) collective-permute-start(bf16[256,1024]{1,0:T(8,128)(2,1)} %own_far.1), channel_id=1, source_target_pairs={{0,1},{1,0},{2,3},{3,2},{4,5},{5,4},{6,7},{7,6},{8,9},{9,8},{10,11... | collective-permute-start | bytes 1572872 | tf_op jit(solution)/shard_map/ppermute | solution.py:240
  32.3 49.4 %collective-permute-start.2 = (bf16[512,2048]{1,0:T(8,128)(2,1)}, bf16[512,2048]{1,0:T(8,128)(2,1)}, u32[]{:S(2)}, u32[]{:S(2)}) collective-permute-start(bf16[512,2048]{1,0:T(8,128)(2,1)} %w_far.3), channel_id=1, source_target_pairs={{0,1},{1,0},{2,3},{3,2},{4,5},{5,4},{6,7},{7,6},{8,9},{9,8},{10,11... | collective-permute-start | bytes 6291464 | tf_op jit(solution)/shard_map/ppermute | solution.py:249
  32.3 19.2 %all-to-all-start.1 = ((bf16[128,4,128]{2,1,0:T(4,128)(2,1)}), bf16[128,4,128]{2,1,0:T(4,128)(2,1)S(1)}, u32[]{:S(2)}, u32[]{:S(2)}) async-start(bf16[128,4,128]{2,1,0:T(4,128)(2,1)} %bitcast.3), calls=%async_computation.1 | async-start | bytes 262144 | tf_op jit(solution)/shard_map/all_to_all | solution.py:250
  39.2 12.4 %copy-start.2 = (bf16[256,512]{1,0:T(8,128)(2,1)S(1)}, bf16[256,512]{1,0:T(8,128)(2,1)}, u32[]{:S(2)}) copy-start(bf16[256,512]{1,0:T(8,128)(2,1)} %q_far.3) | copy-start | bytes 786436
  70.5 11.2 %collective-permute-start.1 = (bf16[256,512]{1,0:T(8,128)(2,1)S(1)}, bf16[256,512]{1,0:T(8,128)(2,1)S(1)}, u32[]{:S(2)}, u32[]{:S(2)}) collective-permute-start(bf16[256,512]{1,0:T(8,128)(2,1)S(1)} %get-tuple-element.42.normed_ref), channel_id=1, source_target_pairs={{0,1},{1,0},{2,3},{3,2},{4,5},{5,4},{6,7},{7,6},{8,9},{9,8},{10,11... | collective-permute-start | bytes 786440 | tf_op jit(solution)/shard_map/ppermute | solution.py:262
  71.4 19.3 %all-to-all-start.3 = ((bf16[128,4,128]{2,1,0:T(4,128)(2,1)}), bf16[128,4,128]{2,1,0:T(4,128)(2,1)S(1)}, u32[]{:S(2)}, u32[]{:S(2)}) async-start(bf16[128,4,128]{2,1,0:T(4,128)(2,1)} %bitcast.7), calls=%async_computation.3 | async-start | bytes 262144 | tf_op jit(solution)/shard_map/all_to_all | solution.py:267
  81.7 9.0 %copy-start = (bf16[256,512]{1,0:T(8,128)(2,1)S(1)}, bf16[256,512]{1,0:T(8,128)(2,1)}, u32[]{:S(2)}) copy-start(bf16[256,512]{1,0:T(8,128)(2,1)} %k_ref.1) | copy-start | bytes 786436
  81.7 9.0 %copy-start.1 = (bf16[256,512]{1,0:T(8,128)(2,1)S(1)}, bf16[256,512]{1,0:T(8,128)(2,1)}, u32[]{:S(2)}) copy-start(bf16[256,512]{1,0:T(8,128)(2,1)} %v_ref.1) | copy-start | bytes 786436

commit v5 on v4

--- a/solution.py
+++ b/solution.py
@@ -178,19 +178,14 @@
         pay_ref[head_rows(h)] = dot((q.astype(F32) * growth).astype(BF), g, 0, 0).astype(BF)
 
 
-def mix(core_ref, normed_ref, other_ref, w_far, w_other_far, out_ref, w_ref, w_other_ref, sems):
-    width = out_ref.shape[1]
+def mix(core_ref, normed_ref, w_far, own_ref, other_ref, w_ref, sems):
+    width = own_ref.shape[1]
+    (copy,) = fetch((w_far,), (w_ref,), sems)
     mine = pl.multiple_of(core_ref[0] * width, width)
-    copies = fetch(
-        (w_far.at[:, pl.ds(mine, width)], w_other_far.at[:, pl.ds(mine, width)]),
-        (w_ref.at[:, pl.ds(0, width)], w_other_ref.at[:, pl.ds(0, width)]),
-        sems,
-    )
-    copies[0].wait()
-    copies[1].wait()
-    out_ref[...] = (
-        dot(normed_ref[...], w_ref[:, :width]) + dot(other_ref[...], w_other_ref[:, :width])
-    ).astype(BF)
+    theirs = pl.multiple_of((1 - core_ref[0]) * width, width)
+    copy.wait()
+    other_ref[...] = dot(normed_ref[...], w_ref[:, pl.ds(theirs, width)]).astype(BF)
+    own_ref[...] = dot(normed_ref[...], w_ref[:, pl.ds(mine, width)])
 
 
 def after_norm(g_ref, s_ref, col_ref, ld_far, q_far, k_far, v_far, gq_ref, gk_ref, gv_ref, ld_ref, q_ref, k_ref, v_ref, sems):
@@ -212,7 +207,8 @@
         gv_ref[:, cols] = dot(probs, g, 0, 0)
 
 
-def finish(k_ref, v_ref, e_ref, col_ref, gkp_ref, gvp_ref, gk_ref, gv_ref):
+def finish(k_ref, v_ref, e_ref, col_ref, gkp_ref, gvp_ref, own_ref, other_ref, gk_ref, gv_ref, out_ref):
+    out_ref[...] = (own_ref[...] + other_ref[...].astype(F32)).astype(BF)
     heads = gk_ref.shape[1] // W
     for h in range(heads):
         cols = head_cols(h)
@@ -245,8 +241,6 @@
         forward_scan, [near(lines, W), near(2 * count, count)], got,
         flops=4 * count * lines * W, scratch=[((exchange, W), F32), ((lines, W), F32)],
     )
-    sent, weight_out = lax.optimization_barrier((sent, out_weight))
-    other_weight = lax.ppermute(weight_out, "head", swap)
     state = lax.all_to_all(sent, "ctx", 0, 0, tiled=True)
     within, grad_norm = call(
         before_norm, [near(rows, width, dtype=F32), near(rows, width, dtype=F32)],
@@ -259,7 +253,6 @@
     )
     got = lax.all_to_all(pay, "ctx", 0, 0, tiled=True)
     got, normed, grad_att = lax.optimization_barrier((got, normed, grad_att))
-    other_normed = lax.ppermute(normed, "head", swap)
     (sent,) = call(
         backward_scan, [near(lines, W)], got, reach, flops=4 * count * lines * W,
         scratch=[((lines, W), F32), ((lines, W), F32)],
@@ -268,16 +261,16 @@
     grad_q, gk_part, gv_part = call(
         after_norm,
         [shape(rows, width), near(rows, width, dtype=F32), near(rows, width, dtype=F32)],
-        grad_att, state, col, log_decay, queries, keys, values, flops=rows * width * span * 9, far=(3, 4, 5, 6),
-    )
-    (mixed,) = call(
-        mix, [shape(rows, model // 2)], core, normed, other_normed, out_weight, other_weight,
-        flops=2 * rows * width * model, smem=1, far=(3, 4),
-    )
-    mixed, gk_part = lax.optimization_barrier((mixed, gk_part))
-    grad_k, grad_v = call(
-        finish, [shape(rows, width), shape(rows, width)], keys, values, leaving, col, gk_part, gv_part,
-        flops=rows * width * W * 4,
+        grad_att, state, col, log_decay, queries, keys, values, flops=rows * width * span * 9 * 30, far=(3, 4, 5, 6),
+    )
+    own, other = call(
+        mix, [near(rows, model // 2, dtype=F32), near(rows, model // 2)], core, normed, out_weight,
+        flops=2 * rows * width * model * 1, smem=1, far=(2,),
+    )
+    theirs = lax.ppermute(other, "head", swap)
+    grad_k, grad_v, mixed = call(
+        finish, [shape(rows, width), shape(rows, width), shape(rows, model // 2)],
+        keys, values, leaving, col, gk_part, gv_part, own, theirs, flops=rows * width * W * 4,
     )
     return mixed, grad_q, grad_k, grad_v
 

time: 93.1 us -> 91.5 us (0.983)
  waiting for transfers between devices: 15.5 us -> 13.1 us
  local copies, waits for them, and re-layouts: 0.02 us -> 1.84 us
    unnamed x6 -> x10, local copies, waits for them, and re-layouts: 0.02 us -> 1.84 us
    all_to_all x1, waiting for transfers between devices: 5.87 us -> 4.35 us  [local(): leaving = lax.all_to_all(sent, 'ctx', 0, 0, tiled=True)]
  transfers between devices with their start and end apart: 5 -> 4, of which waited for: 3 -> 3; matrix products, arithmetic and copies ran while one was open for 0% -> 0% of each run, Pallas kernels for 14% -> 12%
where the time goes in v5:
time: 91.5 us; the launch traced here: 91.1 us
  blocking collectives  46.3 us (51%)
  Pallas kernels  15.3 us (17%)
  starting transfers between devices  13.7 us (15%)
  waiting for transfers between devices  13.1 us (14%)
  local copies, waits for them, and re-layouts  1.84 us (2%)
    all_to_all x1, blocking collectives, local(): lax.all_to_all(pay.reshape(-1, 2, W), 'ctx', 0, 0, tiled=True)  28.4 us
    all_to_all x1, blocking collectives, local(): got = lax.all_to_all(pay, 'ctx', 0, 0, tiled=True)  17.9 us
    pallas_call x8, Pallas kernels, call(): pl.pallas_call(body, out_shape=outs, in_specs=[spec(i) for i in range(len...  15.3 us
    all_to_all x1, waiting for transfers between devices, local(): state = lax.all_to_all(sent, 'ctx', 0, 0, tiled=True)  8.66 us
    all_to_all x1, starting transfers between devices, local(): state = lax.all_to_all(sent, 'ctx', 0, 0, tiled=True)  6.83 us
    all_to_all x1, starting transfers between devices, local(): leaving = lax.all_to_all(sent, 'ctx', 0, 0, tiled=True)  6.71 us
    all_to_all x1, waiting for transfers between devices, local(): leaving = lax.all_to_all(sent, 'ctx', 0, 0, tiled=True)  4.35 us
    unnamed x10, local copies, waits for them, and re-layouts  1.84 us
  transfers between devices with their start and end apart: 4, of which 3 were waited for; matrix products, arithmetic and copies ran while one was open for 0% of the time, Pallas kernels for 12%

profile of v5, /device:TPU:2, one launch (start us, length us, event | category | flops | bytes accessed | tf_op | source)
XLA Modules:
  0.0 91.1 jit_solution(1612523043122475230)
XLA Ops:
  0.6 0.1 collective-permute-start
  0.7 2.0 %block_delta.1 = (bf16[768,128]{1,0:T(8,128)(2,1)S(1)}, f32[256,128]{1,0:T(8,128)S(1)}) custom-call(bf16[256,512]{1,0:T(8,128)(2,1)} %k_ref.1, bf16[256,512]{1,0:T(8,128)(2,1)} %v_ref.1, f32[4,256]{1,0:T(4,128)} %ld_far.5), custom_call_target="tpu_custom_call" | custom-call | flops 33554432 | bytes 856064 | tf_op jit(solution)/shard_map/block_delta/pallas_call | solution.py:36
  2.7 0.1 collective-permute-done.other_ref
  2.8 28.4 %all_to_all.39 = bf16[384,2,128]{2,1,0:T(2,128)(2,1)S(1)} all-to-all(bf16[384,2,128]{2,1,0:T(2,128)(2,1)S(1)} %bitcast.14), channel_id=1, replica_groups=mesh['ctx'=128,'head'=2] {'ctx'}, dimensions={0} | all-to-all | bytes 393216 | tf_op jit(solution)/shard_map/all_to_all | solution.py:238
  31.2 1.2 %forward_scan.1 = (bf16[512,128]{1,0:T(8,128)(2,1)}, bf16[256,128]{1,0:T(8,128)(2,1)S(1)}) custom-call(bf16[768,128]{1,0:T(8,128)(2,1)S(1)} %bitcast.9), custom_call_target="tpu_custom_call" | custom-call | flops 33554432 | bytes 393216 | tf_op jit(solution)/shard_map/forward_scan/pallas_call | solution.py:36
  32.4 6.8 %all-to-all-start.1 = ((bf16[128,4,128]{2,1,0:T(4,128)(2,1)}), bf16[128,4,128]{2,1,0:T(4,128)(2,1)S(1)}, u32[]{:S(2)}, u32[]{:S(2)}) async-start(bf16[128,4,128]{2,1,0:T(4,128)(2,1)} %bitcast.2), calls=%async_computation.1 | async-start | bytes 262144 | tf_op jit(solution)/shard_map/all_to_all | solution.py:244
  39.2 0.0 copy-start.2
  39.2 2.9 %before_norm.1 = (f32[256,512]{1,0:T(8,128)S(1)}, f32[256,512]{1,0:T(8,128)S(1)}) custom-call(s32[1]{0:T(128)} %bitcast.4.core_ref, f32[256,128]{1,0:T(8,128)S(1)} %get-tuple-element.33.col_ref, bf16[256,1024]{1,0:T(8,128)(2,1)S(1)} %collective-permute-done.other_ref, f32[4,256]{1,0:T(4,128)} %ld_far.5, bf16[256,512]{1,0:T(8,128)(2,1)} %q_far.3, ...), custom_call_target="tpu_custom_call" | custom-call | flops 671088640 | bytes 5115908 | tf_op jit(solution)/shard_map/before_norm/pallas_call | solution.py:36
  42.1 8.7 %all-to-all-done.1 = bf16[128,4,128]{2,1,0:T(4,128)(2,1)S(1)} async-done(((bf16[128,4,128]{2,1,0:T(4,128)(2,1)}), bf16[128,4,128]{2,1,0:T(4,128)(2,1)S(1)}, u32[]{:S(2)}, u32[]{:S(2)}) %all-to-all-start.1) | async-done | bytes 131104 | tf_op jit(solution)/shard_map/all_to_all | solution.py:244
  50.8 0.9 norm_and_grad.1
  51.7 17.9 %all_to_all.40 = bf16[128,4,128]{2,1,0:T(4,128)(2,1)S(1)} all-to-all(bf16[128,4,128]{2,1,0:T(4,128)(2,1)S(1)} %bitcast.15), channel_id=1, replica_groups=mesh['ctx'=128,'head'=2] {'ctx'}, dimensions={0} | all-to-all | bytes 262144 | tf_op jit(solution)/shard_map/all_to_all | solution.py:254
  69.6 0.9 %backward_scan.1 = bf16[512,128]{1,0:T(8,128)(2,1)} custom-call(bf16[512,128]{1,0:T(8,128)(2,1)S(1)} %bitcast.12, bf16[256,128]{1,0:T(8,128)(2,1)S(1)} %get-tuple-element.41.reach_ref), custom_call_target="tpu_custom_call" | custom-call | flops 33554432 | bytes 327680 | tf_op jit(solution)/shard_map/backward_scan/pallas_call | solution.py:36
  70.5 6.7 %all-to-all-start.3 = ((bf16[128,4,128]{2,1,0:T(4,128)(2,1)}), bf16[128,4,128]{2,1,0:T(4,128)(2,1)S(1)}, u32[]{:S(2)}, u32[]{:S(2)}) async-start(bf16[128,4,128]{2,1,0:T(4,128)(2,1)} %bitcast.7), calls=%async_computation.3 | async-start | bytes 262144 | tf_op jit(solution)/shard_map/all_to_all | solution.py:260
  77.2 2.8 %mix.1 = (f32[256,1024]{1,0:T(8,128)S(1)}, bf16[256,1024]{1,0:T(8,128)(2,1)}) custom-call(s32[1]{0:T(128)} %bitcast.4.core_ref, bf16[256,512]{1,0:T(8,128)(2,1)S(1)} %get-tuple-element.45.normed_ref, bf16[512,2048]{1,0:T(8,128)(2,1)} %w_far.3), custom_call_target="tpu_custom_call" | custom-call | flops 536870912 | bytes 3932164 | tf_op jit(solution)/shard_map/mix/pallas_call | solution.py:36
  80.1 0.0 copy-start
  80.1 0.0 copy-start.1
  80.1 0.1 collective-permute-start.1
  80.2 3.4 %after_norm.1 = (bf16[256,512]{1,0:T(8,128)(2,1)}, f32[256,512]{1,0:T(8,128)S(1)}, f32[256,512]{1,0:T(8,128)S(1)}) custom-call(bf16[256,512]{1,0:T(8,128)(2,1)S(1)} %get-tuple-element.42.g_ref, bf16[512,128]{1,0:T(8,128)(2,1)S(1)} %bitcast.11, f32[256,128]{1,0:T(8,128)S(1)} %get-tuple-element.33.col_ref, f32[4,256]{1,0:T(4,128)} %ld_far.5, ...), custom_call_target="tpu_custom_call" | custom-call | flops 9059696640 | bytes 2625536 | tf_op jit(solution)/shard_map/after_norm/pallas_call | solution.py:36
  83.6 0.0 copy-start.3
  83.6 0.8 copy-done.3
  84.4 4.4 %all-to-all-done.3 = bf16[128,4,128]{2,1,0:T(4,128)(2,1)S(1)} async-done(((bf16[128,4,128]{2,1,0:T(4,128)(2,1)}), bf16[128,4,128]{2,1,0:T(4,128)(2,1)S(1)}, u32[]{:S(2)}, u32[]{:S(2)}) %all-to-all-start.3) | async-done | bytes 131104 | tf_op jit(solution)/shard_map/all_to_all | solution.py:260
  88.8 0.0 collective-permute-done.1.other_ref
  88.8 1.0 %copy-done.4 = f32[256,512]{1,0:T(8,128)S(1)} copy-done((f32[256,512]{1,0:T(8,128)S(1)}, f32[256,512]{1,0:T(8,128)}, u32[]{:S(2)}) %copy-start.4) | copy-done | bytes 524312
  89.8 1.3 %finish.1 = (bf16[256,512]{1,0:T(8,128)(2,1)}, bf16[256,512]{1,0:T(8,128)(2,1)}, bf16[256,1024]{1,0:T(8,128)(2,1)}) custom-call(bf16[256,512]{1,0:T(8,128)(2,1)S(1)} %copy-done, bf16[256,512]{1,0:T(8,128)(2,1)S(1)} %copy-done.1, bf16[512,128]{1,0:T(8,128)(2,1)S(1)} %bitcast.13, f32[256,128]{1,0:T(8,128)S(1)} %get-tuple-element.33.col_ref, ...), custom_call_target="tpu_custom_call" | custom-call | flops 67108864 | bytes 4456448 | tf_op jit(solution)/shard_map/finish/pallas_call | solution.py:36
  (4 shorter events, 0.0 us)
Async XLA Ops:
  0.6 2.2 %collective-permute-start = (bf16[256,1024]{1,0:T(8,128)(2,1)}, bf16[256,1024]{1,0:T(8,128)(2,1)S(1)}, u32[]{:S(2)}, u32[]{:S(2)}) collective-permute-start(bf16[256,1024]{1,0:T(8,128)(2,1)} %own_far.1), channel_id=1, source_target_pairs={{0,1},{1,0},{2,3},{3,2},{4,5},{5,4},{6,7},{7,6},{8,9},{9,8},{10,11... | collective-permute-start | bytes 1572872 | tf_op jit(solution)/shard_map/ppermute | solution.py:236
  32.4 18.4 %all-to-all-start.1 = ((bf16[128,4,128]{2,1,0:T(4,128)(2,1)}), bf16[128,4,128]{2,1,0:T(4,128)(2,1)S(1)}, u32[]{:S(2)}, u32[]{:S(2)}) async-start(bf16[128,4,128]{2,1,0:T(4,128)(2,1)} %bitcast.2), calls=%async_computation.1 | async-start | bytes 262144 | tf_op jit(solution)/shard_map/all_to_all | solution.py:244
  39.2 11.6 %copy-start.2 = (bf16[256,512]{1,0:T(8,128)(2,1)S(1)}, bf16[256,512]{1,0:T(8,128)(2,1)}, u32[]{:S(2)}) copy-start(bf16[256,512]{1,0:T(8,128)(2,1)} %q_far.3) | copy-start | bytes 786436
  70.5 18.3 %all-to-all-start.3 = ((bf16[128,4,128]{2,1,0:T(4,128)(2,1)}), bf16[128,4,128]{2,1,0:T(4,128)(2,1)S(1)}, u32[]{:S(2)}, u32[]{:S(2)}) async-start(bf16[128,4,128]{2,1,0:T(4,128)(2,1)} %bitcast.7), calls=%async_computation.3 | async-start | bytes 262144 | tf_op jit(solution)/shard_map/all_to_all | solution.py:260
  80.1 8.7 %copy-start = (bf16[256,512]{1,0:T(8,128)(2,1)S(1)}, bf16[256,512]{1,0:T(8,128)(2,1)}, u32[]{:S(2)}) copy-start(bf16[256,512]{1,0:T(8,128)(2,1)} %k_ref.1) | copy-start | bytes 786436
  80.1 8.7 %copy-start.1 = (bf16[256,512]{1,0:T(8,128)(2,1)S(1)}, bf16[256,512]{1,0:T(8,128)(2,1)}, u32[]{:S(2)}) copy-start(bf16[256,512]{1,0:T(8,128)(2,1)} %v_ref.1) | copy-start | bytes 786436
  80.1 8.7 %collective-permute-start.1 = (bf16[256,1024]{1,0:T(8,128)(2,1)}, bf16[256,1024]{1,0:T(8,128)(2,1)S(1)}, u32[]{:S(2)}, u32[]{:S(2)}) collective-permute-start(bf16[256,1024]{1,0:T(8,128)(2,1)} %get-tuple-element.47), channel_id=1, source_target_pairs={{0,1},{1,0},{2,3},{3,2},{4,5},{5,4},{6,7},{7,6},{8,9},{9,8},{10,11... | collective-permute-start | bytes 1572872 | tf_op jit(solution)/shard_map/ppermute | solution.py:270
  83.6 0.8 copy-start.3
  88.8 1.0 %copy-start.4 = (f32[256,512]{1,0:T(8,128)S(1)}, f32[256,512]{1,0:T(8,128)}, u32[]{:S(2)}) copy-start(f32[256,512]{1,0:T(8,128)} %copy-done.3) | copy-start | bytes 1572868

commit v6 on v5

--- a/solution.py
+++ b/solution.py
@@ -72,6 +72,12 @@
     return lax.broadcasted_iota(jnp.int32, (n, n), 0), lax.broadcasted_iota(jnp.int32, (n, n), 1)
 
 
+def pieces(x):
+    high = x.astype(BF).astype(F32)
+    mid = (x - high).astype(BF).astype(F32)
+    return high, mid, x - high - mid
+
+
 def block_delta(k_far, v_far, ld_far, pay_ref, col_ref, delta_ref, mixed_ref, k_ref, v_ref, ld_ref, sems):
     heads, span = ld_ref.shape
     slots, six = delta_ref.shape[0] // OWN, OWN + 2
@@ -80,27 +86,26 @@
     a, b = grid_of(span)
     lane = lax.broadcasted_iota(jnp.int32, (per, W), 1)
     copies[2].wait()
-    col = dot((b <= a).astype(F32), ld_ref[...], 1, 1, precision=EXACT)
+    before = (b <= a).astype(BF)
+    col = sum(dot(before, piece.astype(BF), 1, 1) for piece in pieces(ld_ref[...]))
     last = col[span - 1 : span, :]
     weight = jnp.exp(last - col)
-    copies[0].wait()
-    copies[1].wait()
-    for h in range(heads):
-        kw = (k_ref[:, head_cols(h)].astype(F32) * weight[:, h : h + 1]).astype(BF)
-        delta_ref[head_rows(h)] = dot(kw, v_ref[:, head_cols(h)], 0, 0)
-        end = jnp.broadcast_to(last[:, h : h + 1], (per, W))
-        hi = end.astype(BF).astype(F32)
-        mid = (end - hi).astype(BF).astype(F32)
-        low = end - hi - mid
+    col_ref[:, :heads] = jnp.exp(col)
+    col_ref[:, heads : 2 * heads] = weight
+    col_ref[:, 2 * heads : 3 * heads] = col
+    for h in range(heads):
+        hi, mid, low = pieces(jnp.broadcast_to(last[:, h : h + 1], (per, W)))
         tail = jnp.where(lane == 0, hi, jnp.where(lane == 1, mid, jnp.where(lane == 2, low, 0.0)))
         mixed_ref[pl.ds(h * per * six + OWN, per, stride=six)] = tail
         mixed_ref[pl.ds(h * per * six + OWN + 1, per, stride=six)] = tail
+    copies[0].wait()
+    copies[1].wait()
+    for h in range(heads):
+        kw = (k_ref[:, head_cols(h)].astype(F32) * weight[:, h : h + 1]).astype(BF)
+        delta_ref[head_rows(h)] = dot(kw, v_ref[:, head_cols(h)], 0, 0)
     for r in range(OWN):
         mixed_ref[pl.ds(r, slots, stride=six)] = delta_ref[pl.ds(r, slots, stride=OWN)]
     pay_ref[...] = mixed_ref[...].astype(BF)
-    col_ref[:, :heads] = jnp.exp(col)
-    col_ref[:, heads : 2 * heads] = weight
-    col_ref[:, 2 * heads : 3 * heads] = col
 
 
 def masked_probs(h, heads, q, k, col_ref, row, a, b):
@@ -185,7 +190,7 @@
     theirs = pl.multiple_of((1 - core_ref[0]) * width, width)
     copy.wait()
     other_ref[...] = dot(normed_ref[...], w_ref[:, pl.ds(theirs, width)]).astype(BF)
-    own_ref[...] = dot(normed_ref[...], w_ref[:, pl.ds(mine, width)])
+    own_ref[...] = dot(normed_ref[...], w_ref[:, pl.ds(mine, width)]).astype(BF)
 
 
 def after_norm(g_ref, s_ref, col_ref, ld_far, q_far, k_far, v_far, gq_ref, gk_ref, gv_ref, ld_ref, q_ref, k_ref, v_ref, sems):
@@ -208,7 +213,7 @@
 
 
 def finish(k_ref, v_ref, e_ref, col_ref, gkp_ref, gvp_ref, own_ref, other_ref, gk_ref, gv_ref, out_ref):
-    out_ref[...] = (own_ref[...] + other_ref[...].astype(F32)).astype(BF)
+    out_ref[...] = (own_ref[...].astype(F32) + other_ref[...].astype(F32)).astype(BF)
     heads = gk_ref.shape[1] // W
     for h in range(heads):
         cols = head_cols(h)
@@ -264,7 +269,7 @@
         grad_att, state, col, log_decay, queries, keys, values, flops=rows * width * span * 9 * 30, far=(3, 4, 5, 6),
     )
     own, other = call(
-        mix, [near(rows, model // 2, dtype=F32), near(rows, model // 2)], core, normed, out_weight,
+        mix, [near(rows, model // 2), near(rows, model // 2)], core, normed, out_weight,
         flops=2 * rows * width * model * 1, smem=1, far=(2,),
     )
     theirs = lax.ppermute(other, "head", swap)

time: 91.5 us -> 90.4 us (0.988)
  local copies, waits for them, and re-layouts: 1.84 us -> 0.02 us
    unnamed x10 -> x6, local copies, waits for them, and re-layouts: 1.84 us -> 0.02 us
where the time goes in v6:
time: 90.4 us; the launch traced here: 90.1 us
  blocking collectives  46.3 us (51%)
  Pallas kernels  15.4 us (17%)
  starting transfers between devices  13.9 us (15%)
  waiting for transfers between devices  13.7 us (15%)
    all_to_all x1, blocking collectives, local(): lax.all_to_all(pay.reshape(-1, 2, W), 'ctx', 0, 0, tiled=True)  28.4 us
    all_to_all x1, blocking collectives, local(): got = lax.all_to_all(pay, 'ctx', 0, 0, tiled=True)  17.9 us
    pallas_call x8, Pallas kernels, call(): pl.pallas_call(body, out_shape=outs, in_specs=[spec(i) for i in range(len...  15.4 us
    all_to_all x1, waiting for transfers between devices, local(): state = lax.all_to_all(sent, 'ctx', 0, 0, tiled=True)  8.66 us
    all_to_all x1, starting transfers between devices, local(): state = lax.all_to_all(sent, 'ctx', 0, 0, tiled=True)  6.83 us
    all_to_all x1, starting transfers between devices, local(): leaving = lax.all_to_all(sent, 'ctx', 0, 0, tiled=True)  6.7 us
    all_to_all x1, waiting for transfers between devices, local(): leaving = lax.all_to_all(sent, 'ctx', 0, 0, tiled=True)  4.96 us
  transfers between devices with their start and end apart: 4, of which 3 were waited for; matrix products, arithmetic and copies ran while one was open for 0% of the time, Pallas kernels for 12%

profile of v6, /device:TPU:2, one launch (start us, length us, event | category | flops | bytes accessed | tf_op | source)
XLA Modules:
  0.0 90.1 jit_solution(4654358055065151658)
XLA Ops:
  0.6 0.1 collective-permute-start
  0.7 2.0 %block_delta.1 = (bf16[768,128]{1,0:T(8,128)(2,1)S(1)}, f32[256,128]{1,0:T(8,128)S(1)}) custom-call(bf16[256,512]{1,0:T(8,128)(2,1)} %k_ref.1, bf16[256,512]{1,0:T(8,128)(2,1)} %v_ref.1, f32[4,256]{1,0:T(4,128)} %ld_far.5), custom_call_target="tpu_custom_call" | custom-call | flops 33554432 | bytes 856064 | tf_op jit(solution)/shard_map/block_delta/pallas_call | solution.py:36
  2.7 0.1 collective-permute-done.other_ref
  2.8 28.4 %all_to_all.39 = bf16[384,2,128]{2,1,0:T(2,128)(2,1)S(1)} all-to-all(bf16[384,2,128]{2,1,0:T(2,128)(2,1)S(1)} %bitcast.14), channel_id=1, replica_groups=mesh['ctx'=128,'head'=2] {'ctx'}, dimensions={0} | all-to-all | bytes 393216 | tf_op jit(solution)/shard_map/all_to_all | solution.py:243
  31.2 1.2 %forward_scan.1 = (bf16[512,128]{1,0:T(8,128)(2,1)}, bf16[256,128]{1,0:T(8,128)(2,1)S(1)}) custom-call(bf16[768,128]{1,0:T(8,128)(2,1)S(1)} %bitcast.9), custom_call_target="tpu_custom_call" | custom-call | flops 33554432 | bytes 393216 | tf_op jit(solution)/shard_map/forward_scan/pallas_call | solution.py:36
  32.4 6.8 %all-to-all-start.1 = ((bf16[128,4,128]{2,1,0:T(4,128)(2,1)}), bf16[128,4,128]{2,1,0:T(4,128)(2,1)S(1)}, u32[]{:S(2)}, u32[]{:S(2)}) async-start(bf16[128,4,128]{2,1,0:T(4,128)(2,1)} %bitcast.2), calls=%async_computation.1 | async-start | bytes 262144 | tf_op jit(solution)/shard_map/all_to_all | solution.py:249
  39.2 0.0 copy-start.2
  39.2 2.9 %before_norm.1 = (f32[256,512]{1,0:T(8,128)S(1)}, f32[256,512]{1,0:T(8,128)S(1)}) custom-call(s32[1]{0:T(128)} %bitcast.4.core_ref, f32[256,128]{1,0:T(8,128)S(1)} %get-tuple-element.33.col_ref, bf16[256,1024]{1,0:T(8,128)(2,1)S(1)} %collective-permute-done.other_ref, f32[4,256]{1,0:T(4,128)} %ld_far.5, bf16[256,512]{1,0:T(8,128)(2,1)} %q_far.3, ...), custom_call_target="tpu_custom_call" | custom-call | flops 671088640 | bytes 5115908 | tf_op jit(solution)/shard_map/before_norm/pallas_call | solution.py:36
  42.1 8.7 %all-to-all-done.1 = bf16[128,4,128]{2,1,0:T(4,128)(2,1)S(1)} async-done(((bf16[128,4,128]{2,1,0:T(4,128)(2,1)}), bf16[128,4,128]{2,1,0:T(4,128)(2,1)S(1)}, u32[]{:S(2)}, u32[]{:S(2)}) %all-to-all-start.1) | async-done | bytes 131104 | tf_op jit(solution)/shard_map/all_to_all | solution.py:249
  50.8 0.0 copy-done.2
  50.8 0.9 norm_and_grad.1
  51.7 17.9 %all_to_all.40 = bf16[128,4,128]{2,1,0:T(4,128)(2,1)S(1)} all-to-all(bf16[128,4,128]{2,1,0:T(4,128)(2,1)S(1)} %bitcast.15), channel_id=1, replica_groups=mesh['ctx'=128,'head'=2] {'ctx'}, dimensions={0} | all-to-all | bytes 262144 | tf_op jit(solution)/shard_map/all_to_all | solution.py:259
  69.6 0.9 %backward_scan.1 = bf16[512,128]{1,0:T(8,128)(2,1)} custom-call(bf16[512,128]{1,0:T(8,128)(2,1)S(1)} %bitcast.13, bf16[256,128]{1,0:T(8,128)(2,1)S(1)} %get-tuple-element.41.reach_ref), custom_call_target="tpu_custom_call" | custom-call | flops 33554432 | bytes 327680 | tf_op jit(solution)/shard_map/backward_scan/pallas_call | solution.py:36
  70.5 6.7 %all-to-all-start.3 = ((bf16[128,4,128]{2,1,0:T(4,128)(2,1)}), bf16[128,4,128]{2,1,0:T(4,128)(2,1)S(1)}, u32[]{:S(2)}, u32[]{:S(2)}) async-start(bf16[128,4,128]{2,1,0:T(4,128)(2,1)} %bitcast.7), calls=%async_computation.3 | async-start | bytes 262144 | tf_op jit(solution)/shard_map/all_to_all | solution.py:265
  77.2 2.9 %mix.1 = (bf16[256,1024]{1,0:T(8,128)(2,1)S(1)}, bf16[256,1024]{1,0:T(8,128)(2,1)}) custom-call(s32[1]{0:T(128)} %bitcast.4.core_ref, bf16[256,512]{1,0:T(8,128)(2,1)S(1)} %get-tuple-element.45.normed_ref, bf16[512,2048]{1,0:T(8,128)(2,1)} %w_far.3), custom_call_target="tpu_custom_call" | custom-call | flops 536870912 | bytes 3407876 | tf_op jit(solution)/shard_map/mix/pallas_call | solution.py:36
  80.1 0.0 copy-start
  80.1 0.0 copy-start.1
  80.1 0.3 collective-permute-start.1
  80.4 3.4 %after_norm.1 = (bf16[256,512]{1,0:T(8,128)(2,1)}, f32[256,512]{1,0:T(8,128)S(1)}, f32[256,512]{1,0:T(8,128)S(1)}) custom-call(bf16[256,512]{1,0:T(8,128)(2,1)S(1)} %get-tuple-element.42.g_ref, bf16[512,128]{1,0:T(8,128)(2,1)S(1)} %bitcast.11, f32[256,128]{1,0:T(8,128)S(1)} %get-tuple-element.33.col_ref, f32[4,256]{1,0:T(4,128)} %ld_far.5, ...), custom_call_target="tpu_custom_call" | custom-call | flops 9059696640 | bytes 2625536 | tf_op jit(solution)/shard_map/after_norm/pallas_call | solution.py:36
  83.8 5.0 %all-to-all-done.3 = bf16[128,4,128]{2,1,0:T(4,128)(2,1)S(1)} async-done(((bf16[128,4,128]{2,1,0:T(4,128)(2,1)}), bf16[128,4,128]{2,1,0:T(4,128)(2,1)S(1)}, u32[]{:S(2)}, u32[]{:S(2)}) %all-to-all-start.3) | async-done | bytes 131104 | tf_op jit(solution)/shard_map/all_to_all | solution.py:265
  88.8 0.0 collective-permute-done.1.other_ref
  88.8 0.0 copy-done
  88.8 0.0 copy-done.1
  88.8 1.3 %finish.1 = (bf16[256,512]{1,0:T(8,128)(2,1)}, bf16[256,512]{1,0:T(8,128)(2,1)}, bf16[256,1024]{1,0:T(8,128)(2,1)}) custom-call(bf16[256,512]{1,0:T(8,128)(2,1)S(1)} %copy-done, bf16[256,512]{1,0:T(8,128)(2,1)S(1)} %copy-done.1, bf16[512,128]{1,0:T(8,128)(2,1)S(1)} %bitcast.12, f32[256,128]{1,0:T(8,128)S(1)} %get-tuple-element.33.col_ref, ...), custom_call_target="tpu_custom_call" | custom-call | flops 67108864 | bytes 3932160 | tf_op jit(solution)/shard_map/finish/pallas_call | solution.py:36
Async XLA Ops:
  0.6 2.2 %collective-permute-start = (bf16[256,1024]{1,0:T(8,128)(2,1)}, bf16[256,1024]{1,0:T(8,128)(2,1)S(1)}, u32[]{:S(2)}, u32[]{:S(2)}) collective-permute-start(bf16[256,1024]{1,0:T(8,128)(2,1)} %own_far.1), channel_id=1, source_target_pairs={{0,1},{1,0},{2,3},{3,2},{4,5},{5,4},{6,7},{7,6},{8,9},{9,8},{10,11... | collective-permute-start | bytes 1572872 | tf_op jit(solution)/shard_map/ppermute | solution.py:241
  32.4 18.4 %all-to-all-start.1 = ((bf16[128,4,128]{2,1,0:T(4,128)(2,1)}), bf16[128,4,128]{2,1,0:T(4,128)(2,1)S(1)}, u32[]{:S(2)}, u32[]{:S(2)}) async-start(bf16[128,4,128]{2,1,0:T(4,128)(2,1)} %bitcast.2), calls=%async_computation.1 | async-start | bytes 262144 | tf_op jit(solution)/shard_map/all_to_all | solution.py:249
  39.2 11.6 %copy-start.2 = (bf16[256,512]{1,0:T(8,128)(2,1)S(1)}, bf16[256,512]{1,0:T(8,128)(2,1)}, u32[]{:S(2)}) copy-start(bf16[256,512]{1,0:T(8,128)(2,1)} %q_far.3) | copy-start | bytes 786436
  70.5 18.3 %all-to-all-start.3 = ((bf16[128,4,128]{2,1,0:T(4,128)(2,1)}), bf16[128,4,128]{2,1,0:T(4,128)(2,1)S(1)}, u32[]{:S(2)}, u32[]{:S(2)}) async-start(bf16[128,4,128]{2,1,0:T(4,128)(2,1)} %bitcast.7), calls=%async_computation.3 | async-start | bytes 262144 | tf_op jit(solution)/shard_map/all_to_all | solution.py:265
  80.1 8.7 %copy-start = (bf16[256,512]{1,0:T(8,128)(2,1)S(1)}, bf16[256,512]{1,0:T(8,128)(2,1)}, u32[]{:S(2)}) copy-start(bf16[256,512]{1,0:T(8,128)(2,1)} %k_ref.1) | copy-start | bytes 786436
  80.1 8.7 %copy-start.1 = (bf16[256,512]{1,0:T(8,128)(2,1)S(1)}, bf16[256,512]{1,0:T(8,128)(2,1)}, u32[]{:S(2)}) copy-start(bf16[256,512]{1,0:T(8,128)(2,1)} %v_ref.1) | copy-start | bytes 786436
  80.1 8.6 %collective-permute-start.1 = (bf16[256,1024]{1,0:T(8,128)(2,1)}, bf16[256,1024]{1,0:T(8,128)(2,1)S(1)}, u32[]{:S(2)}, u32[]{:S(2)}) collective-permute-start(bf16[256,1024]{1,0:T(8,128)(2,1)} %get-tuple-element.47), channel_id=1, source_target_pairs={{0,1},{1,0},{2,3},{3,2},{4,5},{5,4},{6,7},{7,6},{8,9},{9,8},{10,11... | collective-permute-start | bytes 1572872 | tf_op jit(solution)/shard_map/ppermute | solution.py:275

commit v7 on v6

--- a/solution.py
+++ b/solution.py
@@ -82,12 +82,13 @@
     heads, span = ld_ref.shape
     slots, six = delta_ref.shape[0] // OWN, OWN + 2
     per = slots // heads
-    copies = fetch((k_far, v_far, ld_far), (k_ref, v_ref, ld_ref), sems)
+    copies = fetch((ld_far, k_far, v_far), (ld_ref, k_ref, v_ref), sems)
     a, b = grid_of(span)
     lane = lax.broadcasted_iota(jnp.int32, (per, W), 1)
-    copies[2].wait()
+    copies[0].wait()
     before = (b <= a).astype(BF)
-    col = sum(dot(before, piece.astype(BF), 1, 1) for piece in pieces(ld_ref[...]))
+    split = jnp.concatenate([piece.astype(BF) for piece in pieces(ld_ref[...])], axis=1)
+    col = dot(jnp.concatenate([before] * 3, axis=1), split, 1, 1)
     last = col[span - 1 : span, :]
     weight = jnp.exp(last - col)
     col_ref[:, :heads] = jnp.exp(col)
@@ -98,8 +99,8 @@
         tail = jnp.where(lane == 0, hi, jnp.where(lane == 1, mid, jnp.where(lane == 2, low, 0.0)))
         mixed_ref[pl.ds(h * per * six + OWN, per, stride=six)] = tail
         mixed_ref[pl.ds(h * per * six + OWN + 1, per, stride=six)] = tail
-    copies[0].wait()
     copies[1].wait()
+    copies[2].wait()
     for h in range(heads):
         kw = (k_ref[:, head_cols(h)].astype(F32) * weight[:, h : h + 1]).astype(BF)
         delta_ref[head_rows(h)] = dot(kw, v_ref[:, head_cols(h)], 0, 0)
@@ -136,35 +137,37 @@
     )
 
 
+def planes(x32_ref, count, stride):
+    x = jnp.concatenate([x32_ref[pl.ds(r, count, stride=stride)] for r in range(OWN)], axis=1).astype(BF)
+    return jnp.concatenate([x, x], axis=0)
+
+
+def unplane(y, y32_ref, y_ref):
+    for r in range(OWN):
+        y32_ref[pl.ds(r, y.shape[0], stride=OWN)] = y[:, r * W : (r + 1) * W]
+    y_ref[...] = y32_ref[...].astype(BF)
+
+
 def forward_scan(x_ref, y_ref, reach_ref, x32_ref, y32_ref):
     count = reach_ref.shape[1]
     six = x_ref.shape[0] // count
     x32_ref[...] = x_ref[...].astype(F32)
     i, j = grid_of(count)
     before = (j < i).astype(BF)
-    gap = jnp.zeros((count, count), F32)
     ends = x32_ref[pl.ds(OWN, count, stride=six)]
-    for piece in range(3):
-        gap = gap + dot(before, jnp.where(j < i, ends[:, piece : piece + 1], 0.0).astype(BF))
+    split = [jnp.where(j < i, ends[:, piece : piece + 1], 0.0).astype(BF) for piece in range(3)]
+    gap = dot(jnp.concatenate([before] * 3, axis=1), jnp.concatenate(split, axis=0))
     reach = jnp.where(j < i, jnp.exp(jnp.minimum(gap, 0.0)), 0.0)
     high = reach.astype(BF)
     low = (reach - high.astype(F32)).astype(BF)
     reach_ref[:count] = high
     reach_ref[count:] = low
-    for r in range(OWN):
-        x = x32_ref[pl.ds(r, count, stride=six)].astype(BF)
-        y32_ref[pl.ds(r, count, stride=OWN)] = dot(high, x) + dot(low, x)
-    y_ref[...] = y32_ref[...].astype(BF)
+    unplane(dot(jnp.concatenate([high, low], axis=1), planes(x32_ref, count, six)), y32_ref, y_ref)
 
 
 def backward_scan(x_ref, reach_ref, y_ref, x32_ref, y32_ref):
-    count = reach_ref.shape[1]
     x32_ref[...] = x_ref[...].astype(F32)
-    high, low = reach_ref[:count], reach_ref[count:]
-    for r in range(OWN):
-        x = x32_ref[pl.ds(r, count, stride=OWN)].astype(BF)
-        y32_ref[pl.ds(r, count, stride=OWN)] = dot(high, x, 0, 0) + dot(low, x, 0, 0)
-    y_ref[...] = y32_ref[...].astype(BF)
+    unplane(dot(reach_ref[...], planes(x32_ref, reach_ref.shape[1], OWN), 0, 0), y32_ref, y_ref)
 
 
 def norm_and_grad(q_ref, s_ref, col_ref, in_ref, gn_ref, normed_ref, g_ref, pay_ref):

time: 90.4 us -> 90 us (level)
  no operation moved by 1% of the time
where the time goes in v7:
time: 90 us; the launch traced here: 89.7 us
  blocking collectives  45.9 us (51%)
  Pallas kernels  15.1 us (17%)
  waiting for transfers between devices  14.2 us (16%)
  starting transfers between devices  13.8 us (15%)
    all_to_all x1, blocking collectives, local(): lax.all_to_all(pay.reshape(-1, 2, W), 'ctx', 0, 0, tiled=True)  28 us
    all_to_all x1, blocking collectives, local(): got = lax.all_to_all(pay, 'ctx', 0, 0, tiled=True)  17.8 us
    pallas_call x8, Pallas kernels, call(): pl.pallas_call(body, out_shape=outs, in_specs=[spec(i) for i in range(len...  15.1 us
    all_to_all x1, waiting for transfers between devices, local(): state = lax.all_to_all(sent, 'ctx', 0, 0, tiled=True)  8.71 us
    all_to_all x1, starting transfers between devices, local(): state = lax.all_to_all(sent, 'ctx', 0, 0, tiled=True)  6.92 us
    all_to_all x1, starting transfers between devices, local(): leaving = lax.all_to_all(sent, 'ctx', 0, 0, tiled=True)  6.66 us
    all_to_all x1, waiting for transfers between devices, local(): leaving = lax.all_to_all(sent, 'ctx', 0, 0, tiled=True)  5.11 us
  transfers between devices with their start and end apart: 4, of which 3 were waited for; matrix products, arithmetic and copies ran while one was open for 0% of the time, Pallas kernels for 12%

profile of v7, /device:TPU:2, one launch (start us, length us, event | category | flops | bytes accessed | tf_op | source)
XLA Modules:
  0.0 89.7 jit_solution(18288461645125708582)
XLA Ops:
  0.6 0.1 collective-permute-start
  0.7 1.7 %block_delta.1 = (bf16[768,128]{1,0:T(8,128)(2,1)S(1)}, f32[256,128]{1,0:T(8,128)S(1)}) custom-call(bf16[256,512]{1,0:T(8,128)(2,1)} %k_ref.1, bf16[256,512]{1,0:T(8,128)(2,1)} %v_ref.1, f32[4,256]{1,0:T(4,128)} %ld_far.5), custom_call_target="tpu_custom_call" | custom-call | flops 33554432 | bytes 856064 | tf_op jit(solution)/shard_map/block_delta/pallas_call | solution.py:36
  2.5 0.4 collective-permute-done.other_ref
  2.8 28.0 %all_to_all.39 = bf16[384,2,128]{2,1,0:T(2,128)(2,1)S(1)} all-to-all(bf16[384,2,128]{2,1,0:T(2,128)(2,1)S(1)} %bitcast.14), channel_id=1, replica_groups=mesh['ctx'=128,'head'=2] {'ctx'}, dimensions={0} | all-to-all | bytes 393216 | tf_op jit(solution)/shard_map/all_to_all | solution.py:246
  30.9 1.1 %forward_scan.1 = (bf16[512,128]{1,0:T(8,128)(2,1)}, bf16[256,128]{1,0:T(8,128)(2,1)S(1)}) custom-call(bf16[768,128]{1,0:T(8,128)(2,1)S(1)} %bitcast.9), custom_call_target="tpu_custom_call" | custom-call | flops 33554432 | bytes 393216 | tf_op jit(solution)/shard_map/forward_scan/pallas_call | solution.py:36
  32.0 6.9 %all-to-all-start.1 = ((bf16[128,4,128]{2,1,0:T(4,128)(2,1)}), bf16[128,4,128]{2,1,0:T(4,128)(2,1)S(1)}, u32[]{:S(2)}, u32[]{:S(2)}) async-start(bf16[128,4,128]{2,1,0:T(4,128)(2,1)} %bitcast.2), calls=%async_computation.1 | async-start | bytes 262144 | tf_op jit(solution)/shard_map/all_to_all | solution.py:252
  38.9 0.0 copy-start.2
  38.9 2.9 %before_norm.1 = (f32[256,512]{1,0:T(8,128)S(1)}, f32[256,512]{1,0:T(8,128)S(1)}) custom-call(s32[1]{0:T(128)} %bitcast.4.core_ref, f32[256,128]{1,0:T(8,128)S(1)} %get-tuple-element.33.col_ref, bf16[256,1024]{1,0:T(8,128)(2,1)S(1)} %collective-permute-done.other_ref, f32[4,256]{1,0:T(4,128)} %ld_far.5, bf16[256,512]{1,0:T(8,128)(2,1)} %q_far.3, ...), custom_call_target="tpu_custom_call" | custom-call | flops 671088640 | bytes 5115908 | tf_op jit(solution)/shard_map/before_norm/pallas_call | solution.py:36
  41.8 8.7 %all-to-all-done.1 = bf16[128,4,128]{2,1,0:T(4,128)(2,1)S(1)} async-done(((bf16[128,4,128]{2,1,0:T(4,128)(2,1)}), bf16[128,4,128]{2,1,0:T(4,128)(2,1)S(1)}, u32[]{:S(2)}, u32[]{:S(2)}) %all-to-all-start.1) | async-done | bytes 131104 | tf_op jit(solution)/shard_map/all_to_all | solution.py:252
  50.5 0.0 copy-done.2
  50.5 0.9 norm_and_grad.1
  51.4 17.8 %all_to_all.40 = bf16[128,4,128]{2,1,0:T(4,128)(2,1)S(1)} all-to-all(bf16[128,4,128]{2,1,0:T(4,128)(2,1)S(1)} %bitcast.15), channel_id=1, replica_groups=mesh['ctx'=128,'head'=2] {'ctx'}, dimensions={0} | all-to-all | bytes 262144 | tf_op jit(solution)/shard_map/all_to_all | solution.py:262
  69.3 0.9 backward_scan.1
  70.1 6.7 %all-to-all-start.3 = ((bf16[128,4,128]{2,1,0:T(4,128)(2,1)}), bf16[128,4,128]{2,1,0:T(4,128)(2,1)S(1)}, u32[]{:S(2)}, u32[]{:S(2)}) async-start(bf16[128,4,128]{2,1,0:T(4,128)(2,1)} %bitcast.7), calls=%async_computation.3 | async-start | bytes 262144 | tf_op jit(solution)/shard_map/all_to_all | solution.py:268
  76.8 2.9 %mix.1 = (bf16[256,1024]{1,0:T(8,128)(2,1)S(1)}, bf16[256,1024]{1,0:T(8,128)(2,1)}) custom-call(s32[1]{0:T(128)} %bitcast.4.core_ref, bf16[256,512]{1,0:T(8,128)(2,1)S(1)} %get-tuple-element.45.normed_ref, bf16[512,2048]{1,0:T(8,128)(2,1)} %w_far.3), custom_call_target="tpu_custom_call" | custom-call | flops 536870912 | bytes 3407876 | tf_op jit(solution)/shard_map/mix/pallas_call | solution.py:36
  79.7 0.0 copy-start
  79.7 0.0 copy-start.1
  79.7 0.1 collective-permute-start.1
  79.8 3.4 %after_norm.1 = (bf16[256,512]{1,0:T(8,128)(2,1)}, f32[256,512]{1,0:T(8,128)S(1)}, f32[256,512]{1,0:T(8,128)S(1)}) custom-call(bf16[256,512]{1,0:T(8,128)(2,1)S(1)} %get-tuple-element.42.g_ref, bf16[512,128]{1,0:T(8,128)(2,1)S(1)} %bitcast.11, f32[256,128]{1,0:T(8,128)S(1)} %get-tuple-element.33.col_ref, f32[4,256]{1,0:T(4,128)} %ld_far.5, ...), custom_call_target="tpu_custom_call" | custom-call | flops 9059696640 | bytes 2625536 | tf_op jit(solution)/shard_map/after_norm/pallas_call | solution.py:36
  83.2 5.1 %all-to-all-done.3 = bf16[128,4,128]{2,1,0:T(4,128)(2,1)S(1)} async-done(((bf16[128,4,128]{2,1,0:T(4,128)(2,1)}), bf16[128,4,128]{2,1,0:T(4,128)(2,1)S(1)}, u32[]{:S(2)}, u32[]{:S(2)}) %all-to-all-start.3) | async-done | bytes 131104 | tf_op jit(solution)/shard_map/all_to_all | solution.py:268
  88.4 0.0 collective-permute-done.1.other_ref
  88.4 0.0 copy-done
  88.4 0.0 copy-done.1
  88.4 1.3 %finish.1 = (bf16[256,512]{1,0:T(8,128)(2,1)}, bf16[256,512]{1,0:T(8,128)(2,1)}, bf16[256,1024]{1,0:T(8,128)(2,1)}) custom-call(bf16[256,512]{1,0:T(8,128)(2,1)S(1)} %copy-done, bf16[256,512]{1,0:T(8,128)(2,1)S(1)} %copy-done.1, bf16[512,128]{1,0:T(8,128)(2,1)S(1)} %bitcast.12, f32[256,128]{1,0:T(8,128)S(1)} %get-tuple-element.33.col_ref, ...), custom_call_target="tpu_custom_call" | custom-call | flops 67108864 | bytes 3932160 | tf_op jit(solution)/shard_map/finish/pallas_call | solution.py:36
Async XLA Ops:
  0.6 2.2 %collective-permute-start = (bf16[256,1024]{1,0:T(8,128)(2,1)}, bf16[256,1024]{1,0:T(8,128)(2,1)S(1)}, u32[]{:S(2)}, u32[]{:S(2)}) collective-permute-start(bf16[256,1024]{1,0:T(8,128)(2,1)} %own_far.1), channel_id=1, source_target_pairs={{0,1},{1,0},{2,3},{3,2},{4,5},{5,4},{6,7},{7,6},{8,9},{9,8},{10,11... | collective-permute-start | bytes 1572872 | tf_op jit(solution)/shard_map/ppermute | solution.py:244
  32.0 18.5 %all-to-all-start.1 = ((bf16[128,4,128]{2,1,0:T(4,128)(2,1)}), bf16[128,4,128]{2,1,0:T(4,128)(2,1)S(1)}, u32[]{:S(2)}, u32[]{:S(2)}) async-start(bf16[128,4,128]{2,1,0:T(4,128)(2,1)} %bitcast.2), calls=%async_computation.1 | async-start | bytes 262144 | tf_op jit(solution)/shard_map/all_to_all | solution.py:252
  38.9 11.6 %copy-start.2 = (bf16[256,512]{1,0:T(8,128)(2,1)S(1)}, bf16[256,512]{1,0:T(8,128)(2,1)}, u32[]{:S(2)}) copy-start(bf16[256,512]{1,0:T(8,128)(2,1)} %q_far.3) | copy-start | bytes 786436
  70.1 18.2 %all-to-all-start.3 = ((bf16[128,4,128]{2,1,0:T(4,128)(2,1)}), bf16[128,4,128]{2,1,0:T(4,128)(2,1)S(1)}, u32[]{:S(2)}, u32[]{:S(2)}) async-start(bf16[128,4,128]{2,1,0:T(4,128)(2,1)} %bitcast.7), calls=%async_computation.3 | async-start | bytes 262144 | tf_op jit(solution)/shard_map/all_to_all | solution.py:268
  79.7 8.7 %copy-start = (bf16[256,512]{1,0:T(8,128)(2,1)S(1)}, bf16[256,512]{1,0:T(8,128)(2,1)}, u32[]{:S(2)}) copy-start(bf16[256,512]{1,0:T(8,128)(2,1)} %k_ref.1) | copy-start | bytes 786436
  79.7 8.7 %copy-start.1 = (bf16[256,512]{1,0:T(8,128)(2,1)S(1)}, bf16[256,512]{1,0:T(8,128)(2,1)}, u32[]{:S(2)}) copy-start(bf16[256,512]{1,0:T(8,128)(2,1)} %v_ref.1) | copy-start | bytes 786436
  79.7 8.6 %collective-permute-start.1 = (bf16[256,1024]{1,0:T(8,128)(2,1)}, bf16[256,1024]{1,0:T(8,128)(2,1)S(1)}, u32[]{:S(2)}, u32[]{:S(2)}) collective-permute-start(bf16[256,1024]{1,0:T(8,128)(2,1)} %get-tuple-element.47), channel_id=1, source_target_pairs={{0,1},{1,0},{2,3},{3,2},{4,5},{5,4},{6,7},{7,6},{8,9},{9,8},{10,11... | collective-permute-start | bytes 1572872 | tf_op jit(solution)/shard_map/ppermute | solution.py:278

commit v8 on v7

--- a/solution.py
+++ b/solution.py
@@ -21,7 +21,7 @@
     )
 
 
-def call(body, outs, *args, flops=0, far=(), smem=0, scratch=()):
+def call(body, outs, *args, flops=0, far=(), smem=0, scratch=(), sent=0):
     def spec(i):
         if i < smem:
             return pl.BlockSpec(memory_space=pltpu.SMEM)
@@ -32,12 +32,14 @@
     if far:
         buffers += [pltpu.SemaphoreType.DMA((len(far),))]
     args = [pltpu.with_memory_space_constraint(a, pltpu.HBM) if i in far else a for i, a in enumerate(args)]
+    if sent:
+        buffers += [pltpu.VMEM(a.shape, a.dtype) for a in outs] + [pltpu.SemaphoreType.DMA((sent,))]
     moved = sum(math.prod(a.shape) * a.dtype.itemsize for a in (*args, *outs))
     return pl.pallas_call(
         body,
         out_shape=outs,
         in_specs=[spec(i) for i in range(len(args))],
-        out_specs=[pl.BlockSpec(memory_space=pltpu.VMEM)] * len(outs),
+        out_specs=[pl.BlockSpec(memory_space=pltpu.HBM if sent else pltpu.VMEM)] * len(outs),
         scratch_shapes=buffers,
         compiler_params=pltpu.CompilerParams(vmem_limit_bytes=12 << 20),
         cost_estimate=pl.CostEstimate(flops=flops, bytes_accessed=moved, transcendentals=0),
@@ -215,15 +217,22 @@
         gv_ref[:, cols] = dot(probs, g, 0, 0)
 
 
-def finish(k_ref, v_ref, e_ref, col_ref, gkp_ref, gvp_ref, own_ref, other_ref, gk_ref, gv_ref, out_ref):
+def finish(k_ref, v_ref, e_ref, col_ref, gkp_ref, gvp_ref, own_ref, other_ref, gk_far, gv_far, out_far, gk_ref, gv_ref, out_ref, sems):
+    heads = gk_ref.shape[1] // W
     out_ref[...] = (own_ref[...].astype(F32) + other_ref[...].astype(F32)).astype(BF)
-    heads = gk_ref.shape[1] // W
+    copies = [pltpu.make_async_copy(out_ref, out_far, sems.at[0])]
+    copies[0].start()
     for h in range(heads):
         cols = head_cols(h)
         weight = col_ref[:, heads + h : heads + h + 1]
         e = e_ref[head_rows(h)]
         gk_ref[:, cols] = (gkp_ref[:, cols] + weight * dot(v_ref[:, cols], e, 1, 1)).astype(BF)
         gv_ref[:, cols] = (gvp_ref[:, cols] + weight * dot(k_ref[:, cols], e)).astype(BF)
+        for n, (near_ref, far_ref) in enumerate(((gk_ref, gk_far), (gv_ref, gv_far))):
+            copies.append(pltpu.make_async_copy(near_ref.at[:, cols], far_ref.at[:, cols], sems.at[1 + 2 * h + n]))
+            copies[-1].start()
+    for copy in copies:
+        copy.wait()
 
 
 def local(queries, keys, values, log_decay, out_weight, out_grad):
@@ -278,7 +287,7 @@
     theirs = lax.ppermute(other, "head", swap)
     grad_k, grad_v, mixed = call(
         finish, [shape(rows, width), shape(rows, width), shape(rows, model // 2)],
-        keys, values, leaving, col, gk_part, gv_part, own, theirs, flops=rows * width * W * 4,
+        keys, values, leaving, col, gk_part, gv_part, own, theirs, flops=rows * width * W * 4, sent=1 + 2 * heads,
     )
     return mixed, grad_q, grad_k, grad_v
 

time: 90 us -> 90.2 us (level)
  no operation moved by 1% of the time
where the time goes in v8:
time: 90.2 us; the launch traced here: 89.8 us
  blocking collectives  45.9 us (51%)
  Pallas kernels  15.2 us (17%)
  waiting for transfers between devices  14.2 us (16%)
  starting transfers between devices  13.8 us (15%)
    all_to_all x1, blocking collectives, local(): lax.all_to_all(pay.reshape(-1, 2, W), 'ctx', 0, 0, tiled=True)  28 us
    all_to_all x1, blocking collectives, local(): got = lax.all_to_all(pay, 'ctx', 0, 0, tiled=True)  17.8 us
    pallas_call x8, Pallas kernels, call(): pl.pallas_call(body, out_shape=outs, in_specs=[spec(i) for i in range(len...  15.2 us
    all_to_all x1, waiting for transfers between devices, local(): state = lax.all_to_all(sent, 'ctx', 0, 0, tiled=True)  8.71 us
    all_to_all x1, starting transfers between devices, local(): state = lax.all_to_all(sent, 'ctx', 0, 0, tiled=True)  6.92 us
    all_to_all x1, starting transfers between devices, local(): leaving = lax.all_to_all(sent, 'ctx', 0, 0, tiled=True)  6.66 us
    all_to_all x1, waiting for transfers between devices, local(): leaving = lax.all_to_all(sent, 'ctx', 0, 0, tiled=True)  5.11 us
  transfers between devices with their start and end apart: 4, of which 3 were waited for; matrix products, arithmetic and copies ran while one was open for 0% of the time, Pallas kernels for 12%

profile of v8, /device:TPU:2, one launch (start us, length us, event | category | flops | bytes accessed | tf_op | source)
XLA Modules:
  0.0 89.8 jit_solution(15549630657903049559)
XLA Ops:
  0.6 0.1 collective-permute-start
  0.7 1.7 %block_delta.1 = (bf16[768,128]{1,0:T(8,128)(2,1)S(1)}, f32[256,128]{1,0:T(8,128)S(1)}) custom-call(bf16[256,512]{1,0:T(8,128)(2,1)} %k_ref.1, bf16[256,512]{1,0:T(8,128)(2,1)} %v_ref.1, f32[4,256]{1,0:T(4,128)} %ld_far.5), custom_call_target="tpu_custom_call" | custom-call | flops 33554432 | bytes 856064 | tf_op jit(solution)/shard_map/block_delta/pallas_call | solution.py:38
  2.5 0.4 collective-permute-done.other_ref
  2.8 28.0 %all_to_all.39 = bf16[384,2,128]{2,1,0:T(2,128)(2,1)S(1)} all-to-all(bf16[384,2,128]{2,1,0:T(2,128)(2,1)S(1)} %bitcast.14), channel_id=1, replica_groups=mesh['ctx'=128,'head'=2] {'ctx'}, dimensions={0} | all-to-all | bytes 393216 | tf_op jit(solution)/shard_map/all_to_all | solution.py:255
  30.9 1.1 %forward_scan.1 = (bf16[512,128]{1,0:T(8,128)(2,1)}, bf16[256,128]{1,0:T(8,128)(2,1)S(1)}) custom-call(bf16[768,128]{1,0:T(8,128)(2,1)S(1)} %bitcast.9), custom_call_target="tpu_custom_call" | custom-call | flops 33554432 | bytes 393216 | tf_op jit(solution)/shard_map/forward_scan/pallas_call | solution.py:38
  32.0 6.9 %all-to-all-start.1 = ((bf16[128,4,128]{2,1,0:T(4,128)(2,1)}), bf16[128,4,128]{2,1,0:T(4,128)(2,1)S(1)}, u32[]{:S(2)}, u32[]{:S(2)}) async-start(bf16[128,4,128]{2,1,0:T(4,128)(2,1)} %bitcast.2), calls=%async_computation.1 | async-start | bytes 262144 | tf_op jit(solution)/shard_map/all_to_all | solution.py:261
  38.9 0.0 copy-start.2
  38.9 2.9 %before_norm.1 = (f32[256,512]{1,0:T(8,128)S(1)}, f32[256,512]{1,0:T(8,128)S(1)}) custom-call(s32[1]{0:T(128)} %bitcast.4.core_ref, f32[256,128]{1,0:T(8,128)S(1)} %get-tuple-element.33.col_ref, bf16[256,1024]{1,0:T(8,128)(2,1)S(1)} %collective-permute-done.other_ref, f32[4,256]{1,0:T(4,128)} %ld_far.5, bf16[256,512]{1,0:T(8,128)(2,1)} %q_far.3, ...), custom_call_target="tpu_custom_call" | custom-call | flops 671088640 | bytes 5115908 | tf_op jit(solution)/shard_map/before_norm/pallas_call | solution.py:38
  41.8 8.7 %all-to-all-done.1 = bf16[128,4,128]{2,1,0:T(4,128)(2,1)S(1)} async-done(((bf16[128,4,128]{2,1,0:T(4,128)(2,1)}), bf16[128,4,128]{2,1,0:T(4,128)(2,1)S(1)}, u32[]{:S(2)}, u32[]{:S(2)}) %all-to-all-start.1) | async-done | bytes 131104 | tf_op jit(solution)/shard_map/all_to_all | solution.py:261
  50.5 0.0 copy-done.2
  50.5 0.9 norm_and_grad.1
  51.4 17.8 %all_to_all.40 = bf16[128,4,128]{2,1,0:T(4,128)(2,1)S(1)} all-to-all(bf16[128,4,128]{2,1,0:T(4,128)(2,1)S(1)} %bitcast.15), channel_id=1, replica_groups=mesh['ctx'=128,'head'=2] {'ctx'}, dimensions={0} | all-to-all | bytes 262144 | tf_op jit(solution)/shard_map/all_to_all | solution.py:271
  69.3 0.9 backward_scan.1
  70.1 6.7 %all-to-all-start.3 = ((bf16[128,4,128]{2,1,0:T(4,128)(2,1)}), bf16[128,4,128]{2,1,0:T(4,128)(2,1)S(1)}, u32[]{:S(2)}, u32[]{:S(2)}) async-start(bf16[128,4,128]{2,1,0:T(4,128)(2,1)} %bitcast.7), calls=%async_computation.3 | async-start | bytes 262144 | tf_op jit(solution)/shard_map/all_to_all | solution.py:277
  76.8 2.9 %mix.1 = (bf16[256,1024]{1,0:T(8,128)(2,1)S(1)}, bf16[256,1024]{1,0:T(8,128)(2,1)}) custom-call(s32[1]{0:T(128)} %bitcast.4.core_ref, bf16[256,512]{1,0:T(8,128)(2,1)S(1)} %get-tuple-element.45.normed_ref, bf16[512,2048]{1,0:T(8,128)(2,1)} %w_far.3), custom_call_target="tpu_custom_call" | custom-call | flops 536870912 | bytes 3407876 | tf_op jit(solution)/shard_map/mix/pallas_call | solution.py:38
  79.7 0.0 copy-start
  79.7 0.0 copy-start.1
  79.7 0.1 collective-permute-start.1
  79.8 3.4 %after_norm.1 = (bf16[256,512]{1,0:T(8,128)(2,1)}, f32[256,512]{1,0:T(8,128)S(1)}, f32[256,512]{1,0:T(8,128)S(1)}) custom-call(bf16[256,512]{1,0:T(8,128)(2,1)S(1)} %get-tuple-element.42.g_ref, bf16[512,128]{1,0:T(8,128)(2,1)S(1)} %bitcast.11, f32[256,128]{1,0:T(8,128)S(1)} %get-tuple-element.33.col_ref, f32[4,256]{1,0:T(4,128)} %ld_far.5, ...), custom_call_target="tpu_custom_call" | custom-call | flops 9059696640 | bytes 2625536 | tf_op jit(solution)/shard_map/after_norm/pallas_call | solution.py:38
  83.2 5.1 %all-to-all-done.3 = bf16[128,4,128]{2,1,0:T(4,128)(2,1)S(1)} async-done(((bf16[128,4,128]{2,1,0:T(4,128)(2,1)}), bf16[128,4,128]{2,1,0:T(4,128)(2,1)S(1)}, u32[]{:S(2)}, u32[]{:S(2)}) %all-to-all-start.3) | async-done | bytes 131104 | tf_op jit(solution)/shard_map/all_to_all | solution.py:277
  88.4 0.0 collective-permute-done.1.other_ref
  88.4 0.0 copy-done
  88.4 0.0 copy-done.1
  88.4 1.4 %finish.1 = (bf16[256,512]{1,0:T(8,128)(2,1)}, bf16[256,512]{1,0:T(8,128)(2,1)}, bf16[256,1024]{1,0:T(8,128)(2,1)}) custom-call(bf16[256,512]{1,0:T(8,128)(2,1)S(1)} %copy-done, bf16[256,512]{1,0:T(8,128)(2,1)S(1)} %copy-done.1, bf16[512,128]{1,0:T(8,128)(2,1)S(1)} %bitcast.12, f32[256,128]{1,0:T(8,128)S(1)} %get-tuple-element.33.col_ref, ...), custom_call_target="tpu_custom_call" | custom-call | flops 67108864 | bytes 3932160 | tf_op jit(solution)/shard_map/finish/pallas_call | solution.py:38
Async XLA Ops:
  0.6 2.2 %collective-permute-start = (bf16[256,1024]{1,0:T(8,128)(2,1)}, bf16[256,1024]{1,0:T(8,128)(2,1)S(1)}, u32[]{:S(2)}, u32[]{:S(2)}) collective-permute-start(bf16[256,1024]{1,0:T(8,128)(2,1)} %own_far.1), channel_id=1, source_target_pairs={{0,1},{1,0},{2,3},{3,2},{4,5},{5,4},{6,7},{7,6},{8,9},{9,8},{10,11... | collective-permute-start | bytes 1572872 | tf_op jit(solution)/shard_map/ppermute | solution.py:253
  32.0 18.5 %all-to-all-start.1 = ((bf16[128,4,128]{2,1,0:T(4,128)(2,1)}), bf16[128,4,128]{2,1,0:T(4,128)(2,1)S(1)}, u32[]{:S(2)}, u32[]{:S(2)}) async-start(bf16[128,4,128]{2,1,0:T(4,128)(2,1)} %bitcast.2), calls=%async_computation.1 | async-start | bytes 262144 | tf_op jit(solution)/shard_map/all_to_all | solution.py:261
  38.9 11.6 %copy-start.2 = (bf16[256,512]{1,0:T(8,128)(2,1)S(1)}, bf16[256,512]{1,0:T(8,128)(2,1)}, u32[]{:S(2)}) copy-start(bf16[256,512]{1,0:T(8,128)(2,1)} %q_far.3) | copy-start | bytes 786436
  70.1 18.2 %all-to-all-start.3 = ((bf16[128,4,128]{2,1,0:T(4,128)(2,1)}), bf16[128,4,128]{2,1,0:T(4,128)(2,1)S(1)}, u32[]{:S(2)}, u32[]{:S(2)}) async-start(bf16[128,4,128]{2,1,0:T(4,128)(2,1)} %bitcast.7), calls=%async_computation.3 | async-start | bytes 262144 | tf_op jit(solution)/shard_map/all_to_all | solution.py:277
  79.7 8.7 %copy-start = (bf16[256,512]{1,0:T(8,128)(2,1)S(1)}, bf16[256,512]{1,0:T(8,128)(2,1)}, u32[]{:S(2)}) copy-start(bf16[256,512]{1,0:T(8,128)(2,1)} %k_ref.1) | copy-start | bytes 786436
  79.7 8.7 %copy-start.1 = (bf16[256,512]{1,0:T(8,128)(2,1)S(1)}, bf16[256,512]{1,0:T(8,128)(2,1)}, u32[]{:S(2)}) copy-start(bf16[256,512]{1,0:T(8,128)(2,1)} %v_ref.1) | copy-start | bytes 786436
  79.7 8.6 %collective-permute-start.1 = (bf16[256,1024]{1,0:T(8,128)(2,1)}, bf16[256,1024]{1,0:T(8,128)(2,1)S(1)}, u32[]{:S(2)}, u32[]{:S(2)}) collective-permute-start(bf16[256,1024]{1,0:T(8,128)(2,1)} %get-tuple-element.47), channel_id=1, source_target_pairs={{0,1},{1,0},{2,3},{3,2},{4,5},{5,4},{6,7},{7,6},{8,9},{9,8},{10,11... | collective-permute-start | bytes 1572872 | tf_op jit(solution)/shard_map/ppermute | solution.py:287

commit v9 on v7

--- a/solution.py
+++ b/solution.py
@@ -171,19 +171,21 @@
 
 
 def norm_and_grad(q_ref, s_ref, col_ref, in_ref, gn_ref, normed_ref, g_ref, pay_ref):
-    heads = in_ref.shape[1] // W
-    for h in range(heads):
-        cols = head_cols(h)
-        growth = col_ref[:, h : h + 1]
-        q = q_ref[:, cols]
-        att = in_ref[:, cols] + growth * dot(q, s_ref[head_rows(h)])
-        inv = lax.rsqrt(jnp.mean(att * att, axis=1, keepdims=True) + EPS)
-        normed_ref[:, cols] = (att * inv).astype(BF)
-        gn = gn_ref[:, cols]
-        g = inv * gn - att * (inv * inv * inv * jnp.mean(gn * att, axis=1, keepdims=True))
-        g = g.astype(BF)
-        g_ref[:, cols] = g
-        pay_ref[head_rows(h)] = dot((q.astype(F32) * growth).astype(BF), g, 0, 0).astype(BF)
+    every = range(in_ref.shape[1] // W)
+    growth = [col_ref[:, h : h + 1] for h in every]
+    read = [dot(q_ref[:, head_cols(h)], s_ref[head_rows(h)]) for h in every]
+    att = [in_ref[:, head_cols(h)] + growth[h] * read[h] for h in every]
+    inv = [lax.rsqrt(jnp.mean(x * x, axis=1, keepdims=True) + EPS) for x in att]
+    grads = []
+    for h in every:
+        gn = gn_ref[:, head_cols(h)]
+        along = inv[h] * inv[h] * inv[h] * jnp.mean(gn * att[h], axis=1, keepdims=True)
+        grads.append((inv[h] * gn - att[h] * along).astype(BF))
+    for h in every:
+        weighted = (q_ref[:, head_cols(h)].astype(F32) * growth[h]).astype(BF)
+        pay_ref[head_rows(h)] = dot(weighted, grads[h], 0, 0).astype(BF)
+        g_ref[:, head_cols(h)] = grads[h]
+        normed_ref[:, head_cols(h)] = (att[h] * inv[h]).astype(BF)
 
 
 def mix(core_ref, normed_ref, w_far, own_ref, other_ref, w_ref, sems):

time: 90 us -> 89.9 us (level)
  no operation moved by 1% of the time
where the time goes in v9:
time: 89.9 us; the launch traced here: 89.6 us
  blocking collectives  45.9 us (51%)
  Pallas kernels  15 us (17%)
  waiting for transfers between devices  14.2 us (16%)
  starting transfers between devices  13.8 us (15%)
    all_to_all x1, blocking collectives, local(): lax.all_to_all(pay.reshape(-1, 2, W), 'ctx', 0, 0, tiled=True)  28 us
    all_to_all x1, blocking collectives, local(): got = lax.all_to_all(pay, 'ctx', 0, 0, tiled=True)  17.8 us
    pallas_call x8, Pallas kernels, call(): pl.pallas_call(body, out_shape=outs, in_specs=[spec(i) for i in range(len...  15 us
    all_to_all x1, waiting for transfers between devices, local(): state = lax.all_to_all(sent, 'ctx', 0, 0, tiled=True)  8.71 us
    all_to_all x1, starting transfers between devices, local(): state = lax.all_to_all(sent, 'ctx', 0, 0, tiled=True)  6.92 us
    all_to_all x1, starting transfers between devices, local(): leaving = lax.all_to_all(sent, 'ctx', 0, 0, tiled=True)  6.66 us
    all_to_all x1, waiting for transfers between devices, local(): leaving = lax.all_to_all(sent, 'ctx', 0, 0, tiled=True)  5.11 us
  transfers between devices with their start and end apart: 4, of which 3 were waited for; matrix products, arithmetic and copies ran while one was open for 0% of the time, Pallas kernels for 12%

profile of v9, /device:TPU:2, one launch (start us, length us, event | category | flops | bytes accessed | tf_op | source)
XLA Modules:
  0.0 89.6 jit_solution(6855455829189431101)
XLA Ops:
  0.6 0.1 collective-permute-start
  0.7 1.7 %block_delta.1 = (bf16[768,128]{1,0:T(8,128)(2,1)S(1)}, f32[256,128]{1,0:T(8,128)S(1)}) custom-call(bf16[256,512]{1,0:T(8,128)(2,1)} %k_ref.1, bf16[256,512]{1,0:T(8,128)(2,1)} %v_ref.1, f32[4,256]{1,0:T(4,128)} %ld_far.5), custom_call_target="tpu_custom_call" | custom-call | flops 33554432 | bytes 856064 | tf_op jit(solution)/shard_map/block_delta/pallas_call | solution.py:36
  2.5 0.4 collective-permute-done.other_ref
  2.8 28.0 %all_to_all.39 = bf16[384,2,128]{2,1,0:T(2,128)(2,1)S(1)} all-to-all(bf16[384,2,128]{2,1,0:T(2,128)(2,1)S(1)} %bitcast.14), channel_id=1, replica_groups=mesh['ctx'=128,'head'=2] {'ctx'}, dimensions={0} | all-to-all | bytes 393216 | tf_op jit(solution)/shard_map/all_to_all | solution.py:248
  30.9 1.1 %forward_scan.1 = (bf16[512,128]{1,0:T(8,128)(2,1)}, bf16[256,128]{1,0:T(8,128)(2,1)S(1)}) custom-call(bf16[768,128]{1,0:T(8,128)(2,1)S(1)} %bitcast.9), custom_call_target="tpu_custom_call" | custom-call | flops 33554432 | bytes 393216 | tf_op jit(solution)/shard_map/forward_scan/pallas_call | solution.py:36
  32.0 6.9 %all-to-all-start.1 = ((bf16[128,4,128]{2,1,0:T(4,128)(2,1)}), bf16[128,4,128]{2,1,0:T(4,128)(2,1)S(1)}, u32[]{:S(2)}, u32[]{:S(2)}) async-start(bf16[128,4,128]{2,1,0:T(4,128)(2,1)} %bitcast.2), calls=%async_computation.1 | async-start | bytes 262144 | tf_op jit(solution)/shard_map/all_to_all | solution.py:254
  38.9 0.0 copy-start.2
  38.9 2.9 %before_norm.1 = (f32[256,512]{1,0:T(8,128)S(1)}, f32[256,512]{1,0:T(8,128)S(1)}) custom-call(s32[1]{0:T(128)} %bitcast.4.core_ref, f32[256,128]{1,0:T(8,128)S(1)} %get-tuple-element.33.col_ref, bf16[256,1024]{1,0:T(8,128)(2,1)S(1)} %collective-permute-done.other_ref, f32[4,256]{1,0:T(4,128)} %ld_far.5, bf16[256,512]{1,0:T(8,128)(2,1)} %q_far.3, ...), custom_call_target="tpu_custom_call" | custom-call | flops 671088640 | bytes 5115908 | tf_op jit(solution)/shard_map/before_norm/pallas_call | solution.py:36
  41.8 8.7 %all-to-all-done.1 = bf16[128,4,128]{2,1,0:T(4,128)(2,1)S(1)} async-done(((bf16[128,4,128]{2,1,0:T(4,128)(2,1)}), bf16[128,4,128]{2,1,0:T(4,128)(2,1)S(1)}, u32[]{:S(2)}, u32[]{:S(2)}) %all-to-all-start.1) | async-done | bytes 131104 | tf_op jit(solution)/shard_map/all_to_all | solution.py:254
  50.5 0.0 copy-done.2
  50.5 0.8 norm_and_grad.1
  51.3 17.8 %all_to_all.40 = bf16[128,4,128]{2,1,0:T(4,128)(2,1)S(1)} all-to-all(bf16[128,4,128]{2,1,0:T(4,128)(2,1)S(1)} %bitcast.15), channel_id=1, replica_groups=mesh['ctx'=128,'head'=2] {'ctx'}, dimensions={0} | all-to-all | bytes 262144 | tf_op jit(solution)/shard_map/all_to_all | solution.py:264
  69.1 0.9 backward_scan.1
  70.0 6.7 %all-to-all-start.3 = ((bf16[128,4,128]{2,1,0:T(4,128)(2,1)}), bf16[128,4,128]{2,1,0:T(4,128)(2,1)S(1)}, u32[]{:S(2)}, u32[]{:S(2)}) async-start(bf16[128,4,128]{2,1,0:T(4,128)(2,1)} %bitcast.7), calls=%async_computation.3 | async-start | bytes 262144 | tf_op jit(solution)/shard_map/all_to_all | solution.py:270
  76.7 2.9 %mix.1 = (bf16[256,1024]{1,0:T(8,128)(2,1)S(1)}, bf16[256,1024]{1,0:T(8,128)(2,1)}) custom-call(s32[1]{0:T(128)} %bitcast.4.core_ref, bf16[256,512]{1,0:T(8,128)(2,1)S(1)} %get-tuple-element.45.normed_ref, bf16[512,2048]{1,0:T(8,128)(2,1)} %w_far.3), custom_call_target="tpu_custom_call" | custom-call | flops 536870912 | bytes 3407876 | tf_op jit(solution)/shard_map/mix/pallas_call | solution.py:36
  79.6 0.0 copy-start
  79.6 0.0 copy-start.1
  79.6 0.1 collective-permute-start.1
  79.7 3.4 %after_norm.1 = (bf16[256,512]{1,0:T(8,128)(2,1)}, f32[256,512]{1,0:T(8,128)S(1)}, f32[256,512]{1,0:T(8,128)S(1)}) custom-call(bf16[256,512]{1,0:T(8,128)(2,1)S(1)} %get-tuple-element.42.g_ref, bf16[512,128]{1,0:T(8,128)(2,1)S(1)} %bitcast.11, f32[256,128]{1,0:T(8,128)S(1)} %get-tuple-element.33.col_ref, f32[4,256]{1,0:T(4,128)} %ld_far.5, ...), custom_call_target="tpu_custom_call" | custom-call | flops 9059696640 | bytes 2625536 | tf_op jit(solution)/shard_map/after_norm/pallas_call | solution.py:36
  83.1 5.1 %all-to-all-done.3 = bf16[128,4,128]{2,1,0:T(4,128)(2,1)S(1)} async-done(((bf16[128,4,128]{2,1,0:T(4,128)(2,1)}), bf16[128,4,128]{2,1,0:T(4,128)(2,1)S(1)}, u32[]{:S(2)}, u32[]{:S(2)}) %all-to-all-start.3) | async-done | bytes 131104 | tf_op jit(solution)/shard_map/all_to_all | solution.py:270
  88.2 0.0 collective-permute-done.1.other_ref
  88.2 0.0 copy-done
  88.2 0.0 copy-done.1
  88.2 1.3 %finish.1 = (bf16[256,512]{1,0:T(8,128)(2,1)}, bf16[256,512]{1,0:T(8,128)(2,1)}, bf16[256,1024]{1,0:T(8,128)(2,1)}) custom-call(bf16[256,512]{1,0:T(8,128)(2,1)S(1)} %copy-done, bf16[256,512]{1,0:T(8,128)(2,1)S(1)} %copy-done.1, bf16[512,128]{1,0:T(8,128)(2,1)S(1)} %bitcast.12, f32[256,128]{1,0:T(8,128)S(1)} %get-tuple-element.33.col_ref, ...), custom_call_target="tpu_custom_call" | custom-call | flops 67108864 | bytes 3932160 | tf_op jit(solution)/shard_map/finish/pallas_call | solution.py:36
Async XLA Ops:
  0.6 2.2 %collective-permute-start = (bf16[256,1024]{1,0:T(8,128)(2,1)}, bf16[256,1024]{1,0:T(8,128)(2,1)S(1)}, u32[]{:S(2)}, u32[]{:S(2)}) collective-permute-start(bf16[256,1024]{1,0:T(8,128)(2,1)} %own_far.1), channel_id=1, source_target_pairs={{0,1},{1,0},{2,3},{3,2},{4,5},{5,4},{6,7},{7,6},{8,9},{9,8},{10,11... | collective-permute-start | bytes 1572872 | tf_op jit(solution)/shard_map/ppermute | solution.py:246
  32.0 18.5 %all-to-all-start.1 = ((bf16[128,4,128]{2,1,0:T(4,128)(2,1)}), bf16[128,4,128]{2,1,0:T(4,128)(2,1)S(1)}, u32[]{:S(2)}, u32[]{:S(2)}) async-start(bf16[128,4,128]{2,1,0:T(4,128)(2,1)} %bitcast.2), calls=%async_computation.1 | async-start | bytes 262144 | tf_op jit(solution)/shard_map/all_to_all | solution.py:254
  38.9 11.6 %copy-start.2 = (bf16[256,512]{1,0:T(8,128)(2,1)S(1)}, bf16[256,512]{1,0:T(8,128)(2,1)}, u32[]{:S(2)}) copy-start(bf16[256,512]{1,0:T(8,128)(2,1)} %q_far.3) | copy-start | bytes 786436
  70.0 18.2 %all-to-all-start.3 = ((bf16[128,4,128]{2,1,0:T(4,128)(2,1)}), bf16[128,4,128]{2,1,0:T(4,128)(2,1)S(1)}, u32[]{:S(2)}, u32[]{:S(2)}) async-start(bf16[128,4,128]{2,1,0:T(4,128)(2,1)} %bitcast.7), calls=%async_computation.3 | async-start | bytes 262144 | tf_op jit(solution)/shard_map/all_to_all | solution.py:270
  79.6 8.7 %copy-start = (bf16[256,512]{1,0:T(8,128)(2,1)S(1)}, bf16[256,512]{1,0:T(8,128)(2,1)}, u32[]{:S(2)}) copy-start(bf16[256,512]{1,0:T(8,128)(2,1)} %k_ref.1) | copy-start | bytes 786436
  79.6 8.7 %copy-start.1 = (bf16[256,512]{1,0:T(8,128)(2,1)S(1)}, bf16[256,512]{1,0:T(8,128)(2,1)}, u32[]{:S(2)}) copy-start(bf16[256,512]{1,0:T(8,128)(2,1)} %v_ref.1) | copy-start | bytes 786436
  79.6 8.6 %collective-permute-start.1 = (bf16[256,1024]{1,0:T(8,128)(2,1)}, bf16[256,1024]{1,0:T(8,128)(2,1)S(1)}, u32[]{:S(2)}, u32[]{:S(2)}) collective-permute-start(bf16[256,1024]{1,0:T(8,128)(2,1)} %get-tuple-element.47), channel_id=1, source_target_pairs={{0,1},{1,0},{2,3},{3,2},{4,5},{5,4},{6,7},{7,6},{8,9},{9,8},{10,11... | collective-permute-start | bytes 1572872 | tf_op jit(solution)/shard_map/ppermute | solution.py:280
